TPU v7x, 32 devices: a whole 2x2x4 slice. The times are simulated.
32 devices in a mesh: pages: 2 (over y), tile: 4 (over z), mp: 2 (over x), batch: 2 (over core).
Axes of the slice: x: 2, y: 2, z: 4, core: 2. Of those that a mesh axis runs over, the one named last changes fastest.
Arguments:
- page_cells: bfloat16 [4, 48, 24, 1024], P(('pages', 'batch'), 'tile'), parts along dimension 0, may hold values from -40 to 40
- text_states: bfloat16 [4, 1024, 1024], P(('pages', 'batch'), 'tile'), parts along dimension 0, may hold values from -40 to 40
- enc_query: bfloat16 [1024, 1024], P('batch', 'mp'), may hold values from -2.5 to 2.5
- enc_keyval: bfloat16 [1024, 2, 1024], P('batch', None, 'mp'), may hold values from -0.1875 to 0.1875
- enc_proj: bfloat16 [1024, 1024], P('mp', 'batch'), may hold values from -0.1875 to 0.1875
- dec_query: bfloat16 [1024, 1024], P('batch', 'mp'), may hold values from -2.5 to 2.5
- dec_keyval: bfloat16 [1024, 2, 1024], P('batch', None, 'mp'), may hold values from -0.1875 to 0.1875
- dec_out: bfloat16 [1024, 1024], P('mp', 'batch'), may hold values from -0.1875 to 0.1875
Outputs:
- encoded: bfloat16 [4, 48, 24, 1024], P(('pages', 'batch'), 'tile'), parts along dimension 0
- decoded: bfloat16 [4, 1024, 1024], P(('pages', 'batch'), ('tile', 'mp')), parts along dimension 0
There are 2 independent parts, one for each index of `pages`. A program takes and returns all parts, laid end to end along the dimension named above; an argument that names none is the same for every part. Nothing has to cross between parts.
All inputs are finite; a program needn't handle non-finite values.
Results may differ from a plain program's by a relative error of at most 0.012.
Values may be sent and summed in bfloat16 or wider, within the bound.
No kernel may reach another device: no remote copies, remote signals or barrier semaphores. Data moves between devices by JAX's collectives and lax.ppermute only.
A program may use at most 64 MiB of HBM per device.

v0:
```python
import math

import jax
import jax.numpy as jnp
from jax import lax
from jax.sharding import PartitionSpec as P

HEAD_ENC = 32
HEAD_DEC = 64


def from_behind(value, axis, by):
    devices = lax.axis_size(axis)
    return lax.ppermute(value, axis, [(i, (i + by) % devices) for i in range(devices)])


def layer_norm(values):
    center = values - jnp.mean(values, axis=-1, keepdims=True)
    variance = jnp.mean(center * center, axis=-1, keepdims=True)
    return center / jnp.sqrt(variance + 1e-05)


def regions(length, window, offset):
    index_row = jnp.arange(length, dtype=jnp.int32)
    return jnp.where(
        index_row < length - window, 0, jnp.where(index_row < length - offset, 1, 2)
    ).astype(jnp.int32)


def body(page_cells, text_states, enc_query, enc_keyval, enc_proj, dec_query, dec_keyval, dec_out):
    wq_enc, wkv_enc, wproj_enc, wq_dec, wkv_dec, wout_dec = (
        lax.all_gather(enc_query, "batch", axis=0, tiled=True),
        lax.all_gather(enc_keyval, "batch", axis=0, tiled=True),
        lax.all_gather(enc_proj, "batch", axis=1, tiled=True),
        lax.all_gather(dec_query, "batch", axis=0, tiled=True),
        lax.all_gather(dec_keyval, "batch", axis=0, tiled=True),
        lax.all_gather(dec_out, "batch", axis=1, tiled=True),
    )
    pages_here, window, columns, width = page_cells.shape
    offset = window // 2
    own_rows = window * columns
    hq_enc = wq_enc.shape[1]
    heads_enc = hq_enc // HEAD_ENC
    joined = jnp.concatenate([wq_enc, wkv_enc.reshape(width, 2 * hq_enc)], axis=1)
    rows_below = from_behind(page_cells[:, :offset], "tile", -1)
    normed = layer_norm(
        jnp.concatenate([page_cells[:, offset:], rows_below], axis=1).astype(jnp.float32)
    ).astype(jnp.bfloat16)
    projected = jnp.einsum(
        "prcd,de->prce", normed, joined, preferred_element_type=jnp.float32
    ).astype(jnp.bfloat16)
    projected = jnp.roll(projected, -offset, axis=2)
    per_row = columns // window
    shaped = projected.reshape(pages_here, window, per_row, window, 3, heads_enc, HEAD_ENC)
    shaped = jnp.swapaxes(shaped, 1, 2).reshape(
        pages_here, per_row, window * window, 3, heads_enc, HEAD_ENC
    )
    win_q = shaped[:, :, :, 0]
    win_k = shaped[:, :, :, 1]
    win_v = shaped[:, :, :, 2]
    is_last = lax.axis_index("tile") == lax.axis_size("tile") - 1
    local_rows = jnp.arange(window, dtype=jnp.int32)
    row_region = jnp.where(is_last, jnp.where(local_rows < window - offset, 1, 2), 0).astype(
        jnp.int32
    )
    labels = row_region[:, None] * 3 + regions(columns, window, offset)[None, :]
    labels = jnp.swapaxes(labels.reshape(window, per_row, window), 0, 1).reshape(
        per_row, window * window
    )
    allowed = labels[:, :, None] == labels[:, None, :]
    win_scores = jnp.einsum(
        "pnqhd,pnkhd->pnhqk", win_q, win_k, preferred_element_type=jnp.float32
    ) / math.sqrt(HEAD_ENC)
    win_scores = jnp.where(allowed[None, :, None], win_scores, -jnp.inf)
    top = jnp.max(win_scores, axis=-1, keepdims=True)
    expd = jnp.exp(win_scores - top)
    win_weights = (expd / jnp.sum(expd, axis=-1, keepdims=True)).astype(jnp.bfloat16)
    win_out = jnp.einsum(
        "pnhqk,pnkhd->pnqhd", win_weights, win_v, preferred_element_type=jnp.float32
    ).astype(jnp.bfloat16)
    win_out = win_out.reshape(pages_here, per_row, window, window, hq_enc)
    win_out = jnp.swapaxes(win_out, 1, 2).reshape(pages_here, window, columns, hq_enc)
    win_out = jnp.roll(win_out, offset, axis=2)
    rows_above = from_behind(win_out[:, window - offset :], "tile", 1)
    unrolled = jnp.concatenate([rows_above, win_out[:, : window - offset]], axis=1)
    partial_proj = jnp.einsum(
        "prce,ed->prcd", unrolled, wproj_enc, preferred_element_type=jnp.float32
    )
    summed = lax.psum(partial_proj.astype(jnp.bfloat16), "mp").astype(jnp.float32)
    encoded = (page_cells.astype(jnp.float32) + summed).astype(jnp.bfloat16)
    hq_dec = wq_dec.shape[1]
    heads_dec = hq_dec // HEAD_DEC
    page_normed = (
        layer_norm(encoded.astype(jnp.float32))
        .astype(jnp.bfloat16)
        .reshape(pages_here, own_rows, width)
    )
    page_kv = jnp.einsum(
        "pnd,de->pne",
        page_normed,
        wkv_dec.reshape(width, 2 * hq_dec),
        preferred_element_type=jnp.float32,
    ).astype(jnp.bfloat16)
    text_normed = layer_norm(text_states.astype(jnp.float32)).astype(jnp.bfloat16)
    queries = jnp.einsum(
        "ptd,de->pte", text_normed, wq_dec, preferred_element_type=jnp.float32
    ).astype(jnp.bfloat16)
    text_len = text_states.shape[1]
    query_heads = queries.reshape(pages_here, text_len, heads_dec, HEAD_DEC)
    start_state = (
        jnp.full((pages_here, heads_dec, text_len), -jnp.inf, jnp.float32),
        jnp.zeros((pages_here, heads_dec, text_len), jnp.float32),
        jnp.zeros((pages_here, heads_dec, text_len, HEAD_DEC), jnp.float32),
    )
    carried = start_state
    shard_rows = lax.all_gather(page_kv, "tile", axis=1, tiled=True)
    count = shard_rows.shape[1] // own_rows
    grouped = max(
        (
            factor
            for factor in range(1, count + 1)
            if count % factor == 0 and factor * own_rows <= 2048
        )
    )
    blocks = jnp.moveaxis(
        shard_rows.reshape(pages_here, count // grouped, grouped * own_rows, 2 * hq_dec), 1, 0
    )

    def advance(running, block_kv):
        maxima, totals, accum = running
        span = block_kv.shape[1]
        block_keys = block_kv[..., :hq_dec].reshape(pages_here, span, heads_dec, HEAD_DEC)
        block_vals = block_kv[..., hq_dec:].reshape(pages_here, span, heads_dec, HEAD_DEC)
        cross_scores = jnp.einsum(
            "pqhd,pkhd->phqk", query_heads, block_keys, preferred_element_type=jnp.float32
        ) / math.sqrt(HEAD_DEC)
        newest = jnp.maximum(maxima, jnp.max(cross_scores, axis=-1))
        rescale = jnp.exp(maxima - newest)
        expo = jnp.exp(cross_scores - newest[..., None])
        totals = totals * rescale + jnp.sum(expo, axis=-1)
        accum = accum * rescale[..., None] + jnp.einsum(
            "phqk,pkhd->phqd",
            expo.astype(jnp.bfloat16),
            block_vals,
            preferred_element_type=jnp.float32,
        )
        return ((newest, totals, accum), None)

    carried, unused = lax.scan(advance, carried, blocks)
    maxima, totals, accum = carried
    context = (
        jnp.transpose(accum / totals[..., None], (0, 2, 1, 3))
        .reshape(pages_here, text_len, hq_dec)
        .astype(jnp.bfloat16)
    )
    share = text_len // lax.axis_size("mp")
    mixed = lax.psum_scatter(
        jnp.einsum("pte,ed->tpd", context, wout_dec, preferred_element_type=jnp.float32).astype(
            jnp.bfloat16
        ),
        "mp",
        scatter_dimension=0,
        tiled=True,
    ).astype(jnp.float32)
    own_text = lax.dynamic_slice_in_dim(text_states, lax.axis_index("mp") * share, share, 1)
    decoded = (own_text.astype(jnp.float32) + jnp.moveaxis(mixed, 0, 1)).astype(jnp.bfloat16)
    return (encoded, decoded)


def solution(mesh):
    placed = (
        P(("pages", "batch"), "tile", None, None),
        P(("pages", "batch"), "tile", None),
        P("batch", "mp"),
        P("batch", None, "mp"),
        P("mp", "batch"),
        P("batch", "mp"),
        P("batch", None, "mp"),
        P("mp", "batch"),
    )
    return jax.shard_map(
        body,
        mesh=mesh,
        in_specs=placed,
        out_specs=(
            P(("pages", "batch"), "tile", None, None),
            P(("pages", "batch"), ("tile", "mp"), None),
        ),
        check_vma=False,
    )
```

profile of v0, /device:TPU:0, one launch (start us, length us, event | category | flops | bytes accessed | tf_op | source)
XLA Modules:
  0.0 199.5 jit_solution(16749749369688853707)
XLA Ops:
  9.6 5.1 %collective-permute-start = (bf16[1,6,24,1024]{3,2,1,0:T(8,128)(2,1)S(1)}, bf16[1,6,24,1024]{3,2,1,0:T(8,128)(2,1)S(1)}, u32[]{:S(2)}, u32[]{:S(2)}) collective-permute-start(bf16[1,6,24,1024]{3,2,1,0:T(8,128)(2,1)S(1)} %get-tuple-element.29), channel_id=1, source_target_pairs={{0,12},{4,0},{8,4},{12,8},{1,13},{5,1},{9,5},{13,9},{2,14},{6,2},{... | collective-permute-start | bytes 884744 | tf_op jit(solution)/shard_map/ppermute | solution.py:14
  15.8 5.1 %collective-permute-done = bf16[1,6,24,1024]{3,2,1,0:T(8,128)(2,1)S(1)} collective-permute-done((bf16[1,6,24,1024]{3,2,1,0:T(8,128)(2,1)S(1)}, bf16[1,6,24,1024]{3,2,1,0:T(8,128)(2,1)S(1)}, u32[]{:S(2)}, u32[]{:S(2)}) %collective-permute-start) | collective-permute-done | bytes 294944 | tf_op jit(solution)/shard_map/ppermute | solution.py:14
  22.9 2.1 %copy.40 = bf16[128,8,2,512]{3,1,2,0:T(8,128)(2,1)S(1)} copy(bf16[128,8,2,512]{3,2,1,0:T(2,128)(2,1)} %bitcast.102) | data formatting | bytes 4194304
  25.1 9.6 %all-gather.9.cloned.1.call-done = bf16[1024,512]{1,0:T(8,128)(2,1)} async-done(((bf16[512,512]{1,0:T(8,128)(2,1)}), bf16[1024,512]{1,0:T(8,128)(2,1)}) %all-gather.9.cloned.1.call-update) | async-done | bytes 1048592 | tf_op jit(solution)/shard_map/all_gather | solution.py:32
  34.7 2.4 %fusion.12 = bf16[1,12,24,1536]{3,2,1,0:T(8,128)(2,1)S(1)} fusion(bf16[1024,1024]{1,0:T(8,128)(2,1)S(1)} %bitcast.104, bf16[1024,512]{1,0:T(8,128)(2,1)} %all-gather.9.cloned.1.call-done, bf16[6,24,1024]{2,1,0:T(8,128)(2,1)S(1)} %bitcast.106, bf16[6,24,1024]{2,1,0:T(8,128)(2,1)S(1)} %get-tuple-element.28, f32[12,24]{1,0:T(8,128)S(1)} %add_sqrt_fusion.1, ...), kind=kOutput, calls=%fused_computation.17 | convolution fusion | flops 914178048 | bytes 4622592 | tf_op jit(solution)/shard_map/prcd,de->prce/dot_general | solution.py:49
  38.5 3.7 %reshape.311 = bf16[1,12,2,12,3,16,32]{6,5,4,3,2,1,0:T(8,128)(2,1)S(1)} reshape(bf16[1,12,24,1536]{3,2,1,0:T(8,128)(2,1)} %pad_maximum_fusion) | data formatting | bytes 1769472 | tf_op jit(solution)/shard_map/reshape | solution.py:54
  43.4 1.7 copy.39
  47.2 4.0 %fusion.81 = (f32[2,16,144]{2,1,0:T(8,128)S(1)}, f32[2,16,144,144]{2,3,1,0:T(8,128)}) fusion(pred[2,144,144]{1,2,0:T(8,128)(4,1)S(1)} %copy-done.8, bf16[1,2,144,1,16,32]{2,5,4,1,3,0:T(8,128)(2,1)S(1)} %copy-done.7, bf16[1,2,144,1,16,32]{2,5,4,1,3,0:T(8,128)(2,1)S(1)} %copy.38), kind=kOutput, calls=%fused_computation.103 | convolution fusion | flops 45121680 | bytes 3303936 | tf_op jit(solution)/shard_map/sub | solution.py:76
  51.2 2.8 %fusion.23 = bf16[1,2,144,16,32]{2,4,3,1,0:T(8,128)(2,1)S(1)} fusion(f32[2,16,144,144]{2,3,1,0:T(8,128)} %get-tuple-element.33, f32[2,16,144]{2,1,0:T(8,128)S(1)} %get-tuple-element.32, bf16[1,2,144,1,16,32]{2,5,4,1,3,0:T(8,128)(2,1)S(1)} %copy.37), kind=kOutput, calls=%fused_computation.37 | convolution fusion | flops 43941888 | bytes 3262464 | tf_op jit(solution)/shard_map/pnhqk,pnkhd->pnqhd/dot_general | solution.py:78
  56.2 1.8 collective-permute-start.1
  58.0 6.2 %collective-permute-done.1 = bf16[1,6,24,512]{3,2,1,0:T(8,128)(2,1)S(1)} collective-permute-done((bf16[1,6,24,512]{3,2,1,0:T(8,128)(2,1)S(1)}, bf16[1,6,24,512]{3,2,1,0:T(8,128)(2,1)S(1)}, u32[]{:S(2)}, u32[]{:S(2)}) %collective-permute-start.1) | collective-permute-done | bytes 147488 | tf_op jit(solution)/shard_map/ppermute | solution.py:14
  64.1 2.5 %fusion.20 = bf16[1,12,24,1024]{3,2,1,0:T(8,128)(2,1)} fusion(bf16[512,1024]{1,0:T(8,128)(2,1)} %all-gather.13.cloned.1.call-done, bf16[1,12,18,512]{3,2,1,0:T(8,128)(2,1)S(1)} %bitcast.99, bf16[1,12,6,512]{3,2,1,0:T(8,128)(2,1)S(1)} %slice.63, bf16[1,6,24,512]{3,2,1,0:T(8,128)(2,1)S(1)} %collective-permute-done.1), kind=kOutput, calls=%fused_computation.34 | convolution fusion | flops 303169536 | bytes 2080768 | tf_op jit(solution)/shard_map/prce,ed->prcd/dot_general | solution.py:86
  67.5 3.6 %copy.41 = bf16[128,8,2,512]{3,1,2,0:T(8,128)(2,1)} copy(bf16[128,8,2,512]{3,2,1,0:T(2,128)(2,1)} %bitcast.101) | data formatting | bytes 4194304
  71.1 25.1 %all-reduce.2.cloned.1.call-done = bf16[1,12,24,1024]{3,2,1,0:T(8,128)(2,1)} async-done(((bf16[1,12,24,1024]{3,2,1,0:T(8,128)(2,1)}), bf16[1,12,24,1024]{3,2,1,0:T(8,128)(2,1)}) %all-reduce.2.cloned.1.call-update) | async-done | bytes 589840 | tf_op jit(solution)/shard_map/psum | solution.py:89
  101.1 5.6 %all-gather.15.cloned.1.call-done = bf16[1024,512]{1,0:T(8,128)(2,1)} async-done(((bf16[512,512]{1,0:T(8,128)(2,1)}), bf16[1024,512]{1,0:T(8,128)(2,1)}) %all-gather.15.cloned.1.call-update) | async-done | bytes 1048592 | tf_op jit(solution)/shard_map/all_gather | solution.py:35
  109.3 50.8 %all-gather.21.cloned.1.call-done = bf16[1152,1024]{1,0:T(8,128)(2,1)} async-done(((bf16[288,1024]{1,0:T(8,128)(2,1)}), bf16[1152,1024]{1,0:T(8,128)(2,1)}) %all-gather.21.cloned.1.call-update) | async-done | bytes 2359312 | tf_op jit(solution)/shard_map/all_gather | solution.py:116
  160.1 1.8 fusion.79
  162.6 2.5 %multiply_reduce_fusion = (f32[8,256]{1,0:T(8,128)S(1)}, f32[8,256,1152]{2,1,0:T(8,128)S(1)}) fusion(bf16[256,8,64]{0,2,1:T(8,128)(2,1)} %bitcast.108, bf16[1152,8,64]{0,2,1:T(8,128)(2,1)S(1)} %bitcast.97), kind=kOutput, calls=%fused_computation.2 | convolution fusion | flops 306706432 | bytes 10887168 | tf_op jit(solution)/shard_map/while/body/eval_jaxpr/pqhd,pkhd->phqk/dot_general | solution.py:134
  165.1 1.9 fusion.1
  167.0 1.7 copy-done
  169.4 5.5 %fusion.40 = bf16[8,256,64]{1,2,0:T(8,128)(2,1)S(1)} fusion(bf16[1152,8,64]{0,2,1:T(8,128)(2,1)S(1)} %bitcast.105, f32[8,256,1152]{2,1,0:T(8,128)} %copy-done, f32[8,256]{1,0:T(8,128)S(1)} %get-tuple-element.34, f32[8,256]{1,0:T(8,128)S(1)} %get-tuple-element.31, f32[8,256]{1,0:T(8,128)S(1)} %get-tuple-element.30), kind=kOutput, calls=%fused_computation.52 | convolution fusion | flops 309460992 | bytes 10903552 | tf_op jit(solution)/shard_map/while/body/eval_jaxpr/phqk,pkhd->phqd/dot_general | solution.py:141
  175.0 2.5 %fusion.24 = bf16[256,1,1024]{2,0,1:T(8,128)(2,1)} fusion(bf16[256,512]{0,1:T(8,128)(2,1)S(1)} %bitcast.110, bf16[512,1024]{1,0:T(8,128)(2,1)} %all-gather.19.cloned.1.call-done), kind=kOutput, calls=%fused_computation.38 | convolution fusion | flops 268697600 | bytes 1835008 | tf_op jit(solution)/shard_map/pte,ed->tpd/dot_general | solution.py:158
  177.6 13.6 %reduce-scatter.2.cloned.1.call-done = bf16[128,1,1024]{2,0,1:T(8,128)(2,1)} async-done(((bf16[256,1,1024]{2,0,1:T(8,128)(2,1)}), bf16[128,1,1024]{2,0,1:T(8,128)(2,1)}) %reduce-scatter.2.cloned.1.call-update) | async-done | bytes 262160 | tf_op jit(solution)/shard_map/reduce_scatter | solution.py:157
  191.2 1.7 fusion.50
  (80 shorter events, 21.8 us)
Async XLA Ops:
  7.2 2.3 %copy-start.4 = (bf16[1,12,24,1024]{3,2,1,0:T(8,128)(2,1)S(1)}, bf16[1,12,24,1024]{3,2,1,0:T(8,128)(2,1)}, u32[]{:S(2)}) copy-start(bf16[1,12,24,1024]{3,2,1,0:T(8,128)(2,1)} %param.8) | copy-start | bytes 1769476
  7.2 15.8 %all-gather.11.cloned.1.call-start = ((), (), s32[]{:S(2)}) async-start(), calls=%async_computation.2 | async-start | bytes 3145728 | tf_op jit(solution)/shard_map/all_gather | solution.py:33
  7.9 26.8 %all-gather.9.cloned.1.call-start = ((), (), s32[]{:S(2)}) async-start(), calls=%async_computation.1 | async-start | bytes 1572864 | tf_op jit(solution)/shard_map/all_gather | solution.py:32
  8.7 49.3 %all-gather.13.cloned.1.call-start = ((), (), s32[]{:S(2)}) async-start(), calls=%async_computation.3 | async-start | bytes 1572864 | tf_op jit(solution)/shard_map/all_gather | solution.py:34
  9.4 58.1 %all-gather.17.cloned.1.call-start = ((), (), s32[]{:S(2)}) async-start(), calls=%async_computation.6 | async-start | bytes 3145728 | tf_op jit(solution)/shard_map/all_gather | solution.py:36
  9.6 11.4 %collective-permute-start = (bf16[1,6,24,1024]{3,2,1,0:T(8,128)(2,1)S(1)}, bf16[1,6,24,1024]{3,2,1,0:T(8,128)(2,1)S(1)}, u32[]{:S(2)}, u32[]{:S(2)}) collective-permute-start(bf16[1,6,24,1024]{3,2,1,0:T(8,128)(2,1)S(1)} %get-tuple-element.29), channel_id=1, source_target_pairs={{0,12},{4,0},{8,4},{12,8},{1,13},{5,1},{9,5},{13,9},{2,14},{6,2},{... | collective-permute-start | bytes 884744 | tf_op jit(solution)/shard_map/ppermute | solution.py:14
  14.7 81.5 %all-reduce.2.cloned.1.call-start = ((), (), s32[]{:S(2)}) async-start(), calls=%async_computation.4 | async-start | bytes 1179648 | tf_op jit(solution)/shard_map/psum | solution.py:89
  45.1 2.1 %copy-start.7 = (bf16[1,2,144,1,16,32]{2,5,4,1,3,0:T(8,128)(2,1)S(1)}, bf16[1,2,144,1,16,32]{2,5,4,1,3,0:T(8,128)(2,1)}, u32[]{:S(2)}) copy-start(bf16[1,2,144,1,16,32]{2,5,4,1,3,0:T(8,128)(2,1)} %copy.39) | copy-start | bytes 884740
  45.1 2.1 %copy-start.8 = (pred[2,144,144]{1,2,0:T(8,128)(4,1)S(1)}, pred[2,144,144]{1,2,0:T(8,128)(4,1)}, u32[]{:S(2)}) copy-start(pred[2,144,144]{1,2,0:T(8,128)(4,1)} %broadcast_compare_fusion) | copy-start | bytes 124420
  56.2 8.0 %collective-permute-start.1 = (bf16[1,6,24,512]{3,2,1,0:T(8,128)(2,1)S(1)}, bf16[1,6,24,512]{3,2,1,0:T(8,128)(2,1)S(1)}, u32[]{:S(2)}, u32[]{:S(2)}) collective-permute-start(bf16[1,6,24,512]{3,2,1,0:T(8,128)(2,1)S(1)} %fusion.70), channel_id=1, source_target_pairs={{0,4},{4,8},{8,12},{12,0},{1,5},{5,9},{9,13},{13,1},{2,6},{6,10},{... | collective-permute-start | bytes 442376 | tf_op jit(solution)/shard_map/ppermute | solution.py:14
  66.7 40.1 %all-gather.15.cloned.1.call-start = ((), (), s32[]{:S(2)}) async-start(), calls=%async_computation.5 | async-start | bytes 1572864 | tf_op jit(solution)/shard_map/all_gather | solution.py:35
  67.3 92.8 %all-gather.21.cloned.1.call-start = ((), (), s32[]{:S(2)}) async-start(), calls=%async_computation.9 | async-start | bytes 2949120 | tf_op jit(solution)/shard_map/all_gather | solution.py:116
  67.5 28.7 %copy-start.5 = (bf16[1,12,24,1024]{3,2,1,0:T(8,128)(2,1)S(1)}, bf16[1,12,24,1024]{3,2,1,0:T(8,128)(2,1)}, u32[]{:S(2)}) copy-start(bf16[1,12,24,1024]{3,2,1,0:T(8,128)(2,1)} %param.8) | copy-start | bytes 1769476
  96.2 2.0 %copy-start.6 = (bf16[128,8,2,512]{3,1,2,0:T(8,128)(2,1)S(1)}, bf16[128,8,2,512]{3,1,2,0:T(8,128)(2,1)}, u32[]{:S(2)}) copy-start(bf16[128,8,2,512]{3,1,2,0:T(8,128)(2,1)} %copy.41) | copy-start | bytes 6291460
  97.7 2.2 %copy-start.1 = (bf16[1,12,24,1024]{3,2,1,0:T(8,128)(2,1)}, bf16[1,12,24,1024]{3,2,1,0:T(8,128)(2,1)S(1)}, u32[]{:S(2)}) copy-start(bf16[1,12,24,1024]{3,2,1,0:T(8,128)(2,1)S(1)} %get-tuple-element.15) | copy-start | bytes 1769476
  98.2 2.4 %copy-start.2 = (bf16[1,256,1024]{2,1,0:T(8,128)(2,1)S(1)}, bf16[1,256,1024]{2,1,0:T(8,128)(2,1)}, u32[]{:S(2)}) copy-start(bf16[1,256,1024]{2,1,0:T(8,128)(2,1)} %param.9) | copy-start | bytes 1572868
  99.9 75.1 %all-gather.19.cloned.1.call-start = ((), (), s32[]{:S(2)}) async-start(), calls=%async_computation.7 | async-start | bytes 1572864 | tf_op jit(solution)/shard_map/all_gather | solution.py:37
  100.6 90.6 %reduce-scatter.2.cloned.1.call-start = ((), (), s32[]{:S(2)}) async-start(), calls=%async_computation.8 | async-start | bytes 786432 | tf_op jit(solution)/shard_map/reduce_scatter | solution.py:157
  165.1 3.7 %copy-start = (f32[8,256,1152]{2,1,0:T(8,128)}, f32[8,256,1152]{2,1,0:T(8,128)S(1)}, u32[]{:S(2)}) copy-start(f32[8,256,1152]{2,1,0:T(8,128)S(1)} %get-tuple-element.35) | copy-start | bytes 28311556
  175.0 16.3 %copy-start.3 = (bf16[1,256,1024]{2,1,0:T(8,128)(2,1)S(1)}, bf16[1,256,1024]{2,1,0:T(8,128)(2,1)}, u32[]{:S(2)}) copy-start(bf16[1,256,1024]{2,1,0:T(8,128)(2,1)} %param.9) | copy-start | bytes 1572868
Sparse Core Ops, SparseCore 0:
  9.6 13.3 all-gather.10
  24.5 10.1 all-gather.8
  36.3 10.1 all-gather.12
  47.9 11.7 all-gather.16
  66.8 29.3 all-reduce.1
  97.7 9.0 all-gather.14
  108.4 51.6 all-gather.20
  161.7 7.8 all-gather.18
  177.7 13.4 reduce-scatter.1
where the time goes:
time: 200 us; the launch traced here: 199 us
  waiting for transfers between devices  121 us (60%)
  matrix products  25.6 us (13%)
  local copies, waits for them, and re-layouts  22.9 us (11%)
  between operations  14.2 us (7%)
  other arithmetic  8.42 us (4%)
  starting transfers between devices  7.43 us (4%)
    all_gather x1, waiting for transfers between devices, body(): shard_rows = lax.all_gather(page_kv, 'tile', axis=1, tiled=True)  50.8 us
    psum x1, waiting for transfers between devices, body(): lax.psum(partial_proj.astype(jnp.bfloat16), 'mp').astype(jnp.float32)  25.1 us
    reduce_scatter x1, waiting for transfers between devices, body(): lax.psum_scatter(jnp.einsum('pte,ed->tpd', context, wout_dec, preferred_e...  13.6 us
    ppermute x2, waiting for transfers between devices, from_behind(): lax.ppermute(value, axis, [(i, (i + by) % devices) for i in range(devices)])  11.3 us
    unnamed x23, local copies, waits for them, and re-layouts  11.3 us
    all_gather x1, waiting for transfers between devices, body(): lax.all_gather(enc_query, 'batch', axis=0, tiled=True)  9.63 us
    ppermute x2, starting transfers between devices, from_behind(): lax.ppermute(value, axis, [(i, (i + by) % devices) for i in range(devices)])  6.9 us
    all_gather x1, waiting for transfers between devices, body(): lax.all_gather(dec_query, 'batch', axis=0, tiled=True)  5.6 us
  transfers between devices with their start and end apart: 11, of which 8 were waited for; matrix products, arithmetic and copies ran while one was open for 25% of the time, Pallas kernels for 0%

commit v1 on v0

v1 whole, which is shorter than its diff:
```python
import functools
import math

import jax
import jax.numpy as jnp
from jax import lax
from jax.experimental import pallas as pl
from jax.experimental.pallas import tpu as pltpu
from jax.sharding import PartitionSpec as P

HEAD_ENC = 32
HEAD_DEC = 64
LANES = 128
VMEM_LIMIT = 48 << 20
F32 = jnp.float32
BF16 = jnp.bfloat16


def from_behind(value, axis, by):
    devices = lax.axis_size(axis)
    return lax.ppermute(value, axis, [(i, (i + by) % devices) for i in range(devices)])


def layer_norm(values):
    center = values - jnp.mean(values, axis=-1, keepdims=True)
    variance = jnp.mean(center * center, axis=-1, keepdims=True)
    return center / jnp.sqrt(variance + 1e-05)


def regions(length, window, offset):
    index_row = jnp.arange(length, dtype=jnp.int32)
    return jnp.where(
        index_row < length - window, 0, jnp.where(index_row < length - offset, 1, 2)
    ).astype(jnp.int32)


def general_body(
    page_cells, text_states, enc_query, enc_keyval, enc_proj, dec_query, dec_keyval, dec_out
):
    wq_enc, wkv_enc, wproj_enc, wq_dec, wkv_dec, wout_dec = (
        lax.all_gather(enc_query, "batch", axis=0, tiled=True),
        lax.all_gather(enc_keyval, "batch", axis=0, tiled=True),
        lax.all_gather(enc_proj, "batch", axis=1, tiled=True),
        lax.all_gather(dec_query, "batch", axis=0, tiled=True),
        lax.all_gather(dec_keyval, "batch", axis=0, tiled=True),
        lax.all_gather(dec_out, "batch", axis=1, tiled=True),
    )
    pages_here, window, columns, width = page_cells.shape
    offset = window // 2
    own_rows = window * columns
    hq_enc = wq_enc.shape[1]
    heads_enc = hq_enc // HEAD_ENC
    joined = jnp.concatenate([wq_enc, wkv_enc.reshape(width, 2 * hq_enc)], axis=1)
    rows_below = from_behind(page_cells[:, :offset], "tile", -1)
    normed = layer_norm(
        jnp.concatenate([page_cells[:, offset:], rows_below], axis=1).astype(F32)
    ).astype(BF16)
    projected = jnp.einsum("prcd,de->prce", normed, joined, preferred_element_type=F32).astype(BF16)
    projected = jnp.roll(projected, -offset, axis=2)
    per_row = columns // window
    shaped = projected.reshape(pages_here, window, per_row, window, 3, heads_enc, HEAD_ENC)
    shaped = jnp.swapaxes(shaped, 1, 2).reshape(
        pages_here, per_row, window * window, 3, heads_enc, HEAD_ENC
    )
    win_q = shaped[:, :, :, 0]
    win_k = shaped[:, :, :, 1]
    win_v = shaped[:, :, :, 2]
    is_last = lax.axis_index("tile") == lax.axis_size("tile") - 1
    local_rows = jnp.arange(window, dtype=jnp.int32)
    row_region = jnp.where(is_last, jnp.where(local_rows < window - offset, 1, 2), 0).astype(
        jnp.int32
    )
    labels = row_region[:, None] * 3 + regions(columns, window, offset)[None, :]
    labels = jnp.swapaxes(labels.reshape(window, per_row, window), 0, 1).reshape(
        per_row, window * window
    )
    allowed = labels[:, :, None] == labels[:, None, :]
    win_scores = jnp.einsum(
        "pnqhd,pnkhd->pnhqk", win_q, win_k, preferred_element_type=F32
    ) / math.sqrt(HEAD_ENC)
    win_scores = jnp.where(allowed[None, :, None], win_scores, -jnp.inf)
    top = jnp.max(win_scores, axis=-1, keepdims=True)
    expd = jnp.exp(win_scores - top)
    win_weights = (expd / jnp.sum(expd, axis=-1, keepdims=True)).astype(BF16)
    win_out = jnp.einsum(
        "pnhqk,pnkhd->pnqhd", win_weights, win_v, preferred_element_type=F32
    ).astype(BF16)
    win_out = win_out.reshape(pages_here, per_row, window, window, hq_enc)
    win_out = jnp.swapaxes(win_out, 1, 2).reshape(pages_here, window, columns, hq_enc)
    win_out = jnp.roll(win_out, offset, axis=2)
    rows_above = from_behind(win_out[:, window - offset :], "tile", 1)
    unrolled = jnp.concatenate([rows_above, win_out[:, : window - offset]], axis=1)
    partial_proj = jnp.einsum("prce,ed->prcd", unrolled, wproj_enc, preferred_element_type=F32)
    summed = lax.psum(partial_proj.astype(BF16), "mp").astype(F32)
    encoded = (page_cells.astype(F32) + summed).astype(BF16)
    hq_dec = wq_dec.shape[1]
    heads_dec = hq_dec // HEAD_DEC
    page_normed = (
        layer_norm(encoded.astype(F32)).astype(BF16).reshape(pages_here, own_rows, width)
    )
    page_kv = jnp.einsum(
        "pnd,de->pne", page_normed, wkv_dec.reshape(width, 2 * hq_dec), preferred_element_type=F32
    ).astype(BF16)
    text_normed = layer_norm(text_states.astype(F32)).astype(BF16)
    queries = jnp.einsum("ptd,de->pte", text_normed, wq_dec, preferred_element_type=F32).astype(
        BF16
    )
    text_len = text_states.shape[1]
    query_heads = queries.reshape(pages_here, text_len, heads_dec, HEAD_DEC)
    carried = (
        jnp.full((pages_here, heads_dec, text_len), -jnp.inf, F32),
        jnp.zeros((pages_here, heads_dec, text_len), F32),
        jnp.zeros((pages_here, heads_dec, text_len, HEAD_DEC), F32),
    )
    shard_rows = lax.all_gather(page_kv, "tile", axis=1, tiled=True)
    count = shard_rows.shape[1] // own_rows
    grouped = max(
        (
            factor
            for factor in range(1, count + 1)
            if count % factor == 0 and factor * own_rows <= 2048
        )
    )
    blocks = jnp.moveaxis(
        shard_rows.reshape(pages_here, count // grouped, grouped * own_rows, 2 * hq_dec), 1, 0
    )

    def advance(running, block_kv):
        maxima, totals, accum = running
        span = block_kv.shape[1]
        block_keys = block_kv[..., :hq_dec].reshape(pages_here, span, heads_dec, HEAD_DEC)
        block_vals = block_kv[..., hq_dec:].reshape(pages_here, span, heads_dec, HEAD_DEC)
        cross_scores = jnp.einsum(
            "pqhd,pkhd->phqk", query_heads, block_keys, preferred_element_type=F32
        ) / math.sqrt(HEAD_DEC)
        newest = jnp.maximum(maxima, jnp.max(cross_scores, axis=-1))
        rescale = jnp.exp(maxima - newest)
        expo = jnp.exp(cross_scores - newest[..., None])
        totals = totals * rescale + jnp.sum(expo, axis=-1)
        accum = accum * rescale[..., None] + jnp.einsum(
            "phqk,pkhd->phqd", expo.astype(BF16), block_vals, preferred_element_type=F32
        )
        return ((newest, totals, accum), None)

    carried, unused = lax.scan(advance, carried, blocks)
    maxima, totals, accum = carried
    context = (
        jnp.transpose(accum / totals[..., None], (0, 2, 1, 3))
        .reshape(pages_here, text_len, hq_dec)
        .astype(BF16)
    )
    share = text_len // lax.axis_size("mp")
    mixed = lax.psum_scatter(
        jnp.einsum("pte,ed->tpd", context, wout_dec, preferred_element_type=F32).astype(BF16),
        "mp",
        scatter_dimension=0,
        tiled=True,
    ).astype(F32)
    own_text = lax.dynamic_slice_in_dim(text_states, lax.axis_index("mp") * share, share, 1)
    decoded = (own_text.astype(F32) + jnp.moveaxis(mixed, 0, 1)).astype(BF16)
    return (encoded, decoded)


def swapped(value, axis):
    return lax.ppermute(value, axis, [(0, 1), (1, 0)])


def norm_rows(ref):
    v = ref[...].astype(F32)
    center = v - jnp.mean(v, axis=-1, keepdims=True)
    variance = jnp.mean(center * center, axis=-1, keepdims=True)
    return (center / jnp.sqrt(variance + 1e-05)).astype(BF16)


def halves(width):
    b = lax.axis_index("batch")
    half = width // 2
    own = pl.multiple_of(b * half, half)
    other = pl.multiple_of((1 - b) * half, half)
    return pl.ds(own, half), pl.ds(other, half)


def dot(a, b):
    return jnp.dot(a, b, preferred_element_type=F32)


def dot_t(a, b):
    return lax.dot_general(a, b, (((1,), (1,)), ((), ())), preferred_element_type=F32)


def lane_head(shape, size):
    return lax.broadcasted_iota(jnp.int32, shape, 1) // size


def enc_kernel(
    columns, page, above, below, wq_o, wq_x, wkv_o, wkv_x, wp_o, wp_x, part, xn, qs, kvs, wo, bias
):
    rows, width = page.shape
    part_rows = rows // 2
    offset = part_rows // columns
    window = 2 * offset
    hq = wq_o.shape[1]
    own, other = halves(width)
    xn[:part_rows] = norm_rows(above)
    xn[part_rows : part_rows + rows] = norm_rows(page)
    xn[part_rows + rows :] = norm_rows(below)
    kvs[...] = (dot(xn[:, own], wkv_o[...]) + dot(xn[:, other], wkv_x[...])).astype(BF16)
    mine = slice(part_rows, part_rows + rows)
    qs[...] = (dot(xn[mine, own], wq_o[...]) + dot(xn[mine, other], wq_x[...])).astype(BF16)

    tile = lax.axis_index("tile")
    edge = (tile == 0, tile == lax.axis_size("tile") - 1)
    shape = (part_rows, rows)
    q_col = lax.broadcasted_iota(jnp.int32, shape, 0) % columns
    key = lax.broadcasted_iota(jnp.int32, shape, 1)
    k_col = key % columns

    def group(col):
        return jnp.where(col < offset, 0, 1 + (col - offset + window) // window)

    same = group(q_col) == group(k_col)
    outside = (key < part_rows, key >= part_rows)
    for half in range(2):
        cut = jnp.logical_and(outside[half], edge[half])
        allowed = jnp.logical_and(same, jnp.logical_not(cut))
        bias[half] = jnp.where(allowed, 0.0, -jnp.inf).astype(F32)

    scale = 1.0 / math.sqrt(HEAD_ENC)
    q_head = lane_head((part_rows, LANES), HEAD_ENC)
    k_head = lane_head((rows, LANES), HEAD_ENC)
    for half in range(2):
        q_rows = slice(half * part_rows, (half + 1) * part_rows)
        k_rows = slice(half * rows, (half + 1) * rows)
        for lanes in range(hq // LANES):
            cols = slice(lanes * LANES, (lanes + 1) * LANES)
            v_cols = slice(hq + lanes * LANES, hq + (lanes + 1) * LANES)
            q = qs[q_rows, cols]
            k = kvs[k_rows, cols]
            v = kvs[k_rows, v_cols]
            acc = jnp.zeros((part_rows, LANES), F32)
            for head in range(LANES // HEAD_ENC):
                s = dot_t(jnp.where(q_head == head, q, jnp.zeros_like(q)), k) * scale
                s = s + bias[half]
                e = jnp.exp(s - jnp.max(s, axis=-1, keepdims=True))
                w = (e / jnp.sum(e, axis=-1, keepdims=True)).astype(BF16)
                acc = acc + dot(w, jnp.where(k_head == head, v, jnp.zeros_like(v)))
            wo[q_rows, cols] = acc.astype(BF16)
    part[:, own] = dot(wo[...], wp_o[...]).astype(BF16)
    part[:, other] = dot(wo[...], wp_x[...]).astype(BF16)


def pieces(scratch, first_col, outs, out_col):
    tiles = len(outs)
    tile = lax.axis_index("tile")
    for s in range(tiles):
        dest = lax.rem(tile + s, tiles)
        start = pl.multiple_of(dest * LANES + first_col, LANES)
        outs[s][:, out_col : out_col + LANES] = scratch[:, pl.ds(start, LANES)]


def kv_kernel(page, mine, theirs, wkv_o, wkv_x, encoded, *rest):
    outs, (xn, kvs) = rest[:-2], rest[-2:]
    width = page.shape[1]
    own, other = halves(width)
    total = mine[...].astype(F32) + theirs[...].astype(F32)
    encoded[...] = (page[...].astype(F32) + total).astype(BF16)
    xn[...] = norm_rows(encoded)
    kvs[...] = (dot(xn[:, own], wkv_o[...]) + dot(xn[:, other], wkv_x[...])).astype(BF16)
    pieces(kvs, 0, outs, 0)
    pieces(kvs, kvs.shape[1] // 2, outs, LANES)


def query_kernel(text, wq_o, wq_x, *rest):
    outs, (xn, qs) = rest[:-2], rest[-2:]
    own, other = halves(text.shape[1])
    xn[...] = norm_rows(text)
    qs[...] = (dot(xn[:, own], wq_o[...]) + dot(xn[:, other], wq_x[...])).astype(BF16)
    pieces(qs, 0, outs, 0)


def cross_kernel(tiles, *refs):
    q_in = refs[:tiles]
    kv_in = refs[tiles : 2 * tiles]
    outs = refs[2 * tiles : 3 * tiles]
    kv, sem = refs[3 * tiles :]
    rows = kv_in[0].shape[0]
    copies = [
        pltpu.make_async_copy(kv_in[s], kv.at[pl.ds(s * rows, rows)], sem.at[s])
        for s in range(tiles)
    ]
    for copy in copies:
        copy.start()
    for copy in copies:
        copy.wait()
    scale = 1.0 / math.sqrt(HEAD_DEC)
    q_head = lane_head(q_in[0].shape, HEAD_DEC)
    for s in range(tiles):
        q = q_in[s][...]
        acc = None
        for head in range(LANES // HEAD_DEC):
            sc = dot_t(jnp.where(q_head == head, q, jnp.zeros_like(q)), kv[:, :LANES]) * scale
            e = jnp.exp(sc - jnp.max(sc, axis=-1, keepdims=True))
            total = jnp.sum(e, axis=-1, keepdims=True)
            out = dot(e.astype(BF16), kv[:, LANES:]) / total
            acc = out if acc is None else jnp.where(q_head == head, out, acc)
        outs[s][...] = acc.astype(BF16)


def out_kernel(tiles, *refs):
    ctx_in = refs[:tiles]
    wo_o, wo_x, text, keep, send, ctx, acc = refs[tiles:]
    tokens = ctx.shape[0]
    own, other = halves(acc.shape[1])
    tile = lax.axis_index("tile")
    for s in range(tiles):
        start = pl.multiple_of(lax.rem(tile + s, tiles) * LANES, LANES)
        ctx[:, pl.ds(start, LANES)] = ctx_in[s][...]
    acc[:, own] = dot(ctx[...], wo_o[...])
    acc[:, other] = dot(ctx[...], wo_x[...])
    half = tokens // 2
    m = lax.axis_index("mp")
    own_rows = pl.ds(pl.multiple_of(m * half, half), half)
    send_rows = pl.ds(pl.multiple_of((1 - m) * half, half), half)
    keep[...] = text[own_rows, :].astype(F32) + acc[own_rows, :]
    send[...] = acc[send_rows, :].astype(BF16)


VM = pl.BlockSpec(memory_space=pltpu.VMEM)
ANY = pl.BlockSpec(memory_space=pl.ANY)


def call(kernel, outs, scratch, *args, specs=None):
    return pl.pallas_call(
        kernel,
        out_shape=[jax.ShapeDtypeStruct(shape, dtype) for shape, dtype in outs],
        in_specs=specs or [VM] * len(args),
        out_specs=[VM] * len(outs),
        scratch_shapes=scratch,
        compiler_params=pltpu.CompilerParams(vmem_limit_bytes=VMEM_LIMIT),
    )(*args)


def body(page_cells, text_states, enc_query, enc_keyval, enc_proj, dec_query, dec_keyval, dec_out):
    tiles = lax.axis_size("tile")
    pages_here, window, columns, width = page_cells.shape
    hq_enc = enc_query.shape[1]
    hq_dec = dec_query.shape[1]
    if (
        pages_here != 1
        or lax.axis_size("batch") != 2
        or lax.axis_size("mp") != 2
        or hq_dec != tiles * LANES
        or hq_enc % LANES
    ):
        return general_body(
            page_cells, text_states, enc_query, enc_keyval, enc_proj, dec_query, dec_keyval, dec_out
        )
    rows = window * columns
    half_rows = rows // 2
    page = page_cells.reshape(rows, width)
    text = text_states.reshape(-1, width)
    tokens = text.shape[0]
    wkv_enc = enc_keyval.reshape(width // 2, 2 * hq_enc)
    wkv_dec = dec_keyval.reshape(width // 2, 2 * hq_dec)
    up = [(i, i + 1) for i in range(tiles - 1)]
    down = [(i + 1, i) for i in range(tiles - 1)]
    wq_x = swapped(enc_query, "batch")
    wkv_x = swapped(wkv_enc, "batch")
    above = lax.ppermute(page[half_rows:], "tile", up)
    below = lax.ppermute(page[:half_rows], "tile", down)
    wp_x = swapped(enc_proj, "batch")
    dq_x = swapped(dec_query, "batch")
    dkv_x = swapped(wkv_dec, "batch")
    do_x = swapped(dec_out, "batch")

    (part,) = call(
        functools.partial(enc_kernel, columns),
        [((rows, width), BF16)],
        [
            pltpu.VMEM((2 * rows, width), BF16),
            pltpu.VMEM((rows, hq_enc), BF16),
            pltpu.VMEM((2 * rows, 2 * hq_enc), BF16),
            pltpu.VMEM((rows, hq_enc), BF16),
            pltpu.VMEM((2, half_rows, rows), F32),
        ],
        page,
        above,
        below,
        enc_query,
        wq_x,
        wkv_enc,
        wkv_x,
        enc_proj,
        wp_x,
    )
    theirs = swapped(part, "mp")

    q_out = call(
        query_kernel,
        [((tokens, LANES), BF16)] * tiles,
        [pltpu.VMEM((tokens, width), BF16), pltpu.VMEM((tokens, hq_dec), BF16)],
        text,
        dec_query,
        dq_x,
    )
    q_in = [q_out[0]] + [from_behind(q_out[s], "tile", s) for s in range(1, tiles)]

    encoded, *kv_out = call(
        kv_kernel,
        [((rows, width), BF16)] + [((rows, 2 * LANES), BF16)] * tiles,
        [pltpu.VMEM((rows, width), BF16), pltpu.VMEM((rows, 2 * hq_dec), BF16)],
        page,
        part,
        theirs,
        wkv_dec,
        dkv_x,
    )
    kv_in = [kv_out[0]] + [from_behind(kv_out[s], "tile", s) for s in range(1, tiles)]

    ctx_out = call(
        functools.partial(cross_kernel, tiles),
        [((tokens, LANES), BF16)] * tiles,
        [pltpu.VMEM((tiles * rows, 2 * LANES), BF16), pltpu.SemaphoreType.DMA((tiles,))],
        *q_in,
        *kv_in,
        specs=[VM] * tiles + [ANY] * tiles,
    )
    ctx_in = [ctx_out[0]] + [from_behind(ctx_out[s], "tile", -s) for s in range(1, tiles)]

    keep, send = call(
        functools.partial(out_kernel, tiles),
        [((tokens // 2, width), F32), ((tokens // 2, width), BF16)],
        [pltpu.VMEM((tokens, hq_dec), BF16), pltpu.VMEM((tokens, width), F32)],
        *ctx_in,
        dec_out,
        do_x,
        text,
    )
    received = swapped(send, "mp")
    decoded = (keep + received.astype(F32)).astype(BF16)
    return (
        encoded.reshape(page_cells.shape),
        decoded.reshape(1, tokens // 2, width),
    )


def solution(mesh):
    placed = (
        P(("pages", "batch"), "tile", None, None),
        P(("pages", "batch"), "tile", None),
        P("batch", "mp"),
        P("batch", None, "mp"),
        P("mp", "batch"),
        P("batch", "mp"),
        P("batch", None, "mp"),
        P("mp", "batch"),
    )
    return jax.shard_map(
        body,
        mesh=mesh,
        in_specs=placed,
        out_specs=(
            P(("pages", "batch"), "tile", None, None),
            P(("pages", "batch"), ("tile", "mp"), None),
        ),
        check_vma=False,
    )
```

time: 200 us -> 96.2 us (0.48)
  waiting for transfers between devices: 121 us -> 45.2 us
  matrix products: 25.6 us -> 0 us
  Pallas kernels: 0 us -> 21.1 us
  local copies, waits for them, and re-layouts: 22.9 us -> 1.9 us
  starting transfers between devices: 7.43 us -> 26.3 us
  between operations: 14.2 us -> 0.79 us
  other arithmetic: 8.42 us -> 0.76 us
    all_gather x7 -> x0, waiting for transfers between devices: 67.6 us -> none  [the longest x1 50.8 us: body(): shard_rows = lax.all_gather(page_kv, 'tile', axis=1, tiled=True)]
    ppermute x0 -> x10, waiting for transfers between devices: none -> 30.1 us  [the longest x8 14.5 us: swapped(): return lax.ppermute(value, axis, [(0, 1), (1, 0)])]
    psum x1 -> x0, waiting for transfers between devices: 25.1 us -> none  [body(): lax.psum(partial_proj.astype(jnp.bfloat16), 'mp').astype(jnp.float32)]
    dot_general x8 -> x0, matrix products: 21.6 us -> none  [the longest x1 5.51 us: advance(): jnp.einsum('phqk,pkhd->phqd', expo.astype(jnp.bfloat16), block_vals, pref...]
    pallas_call x0 -> x5, Pallas kernels: none -> 21.1 us  [call(): pl.pallas_call(kernel, out_shape=[jax.ShapeDtypeStruct(shape, dtype) for...]
    reduce_scatter x1 -> x0, waiting for transfers between devices: 13.6 us -> none  [body(): lax.psum_scatter(jnp.einsum('pte,ed->tpd', context, wout_dec, preferred_e...]
    ppermute x0 -> x10, starting transfers between devices: none -> 10.8 us  [the longest x8 4.86 us: swapped(): return lax.ppermute(value, axis, [(0, 1), (1, 0)])]
    unnamed x23 -> x16, local copies, waits for them, and re-layouts: 11.3 us -> 1.86 us
  transfers between devices with their start and end apart: 11 -> 19, of which waited for: 8 -> 9; matrix products, arithmetic and copies ran while one was open for 25% -> 0% of each run, Pallas kernels for 0% -> 21%
where the time goes in v1:
time: 96.2 us; the launch traced here: 96 us
  waiting for transfers between devices  45.2 us (47%)
  starting transfers between devices  26.3 us (27%)
  Pallas kernels  21.1 us (22%)
  local copies, waits for them, and re-layouts  1.9 us (2%)
    pallas_call x5, Pallas kernels, call(): pl.pallas_call(kernel, out_shape=[jax.ShapeDtypeStruct(shape, dtype) for...  21.1 us
    ppermute x9, starting transfers between devices, from_behind(): lax.ppermute(value, axis, [(i, (i + by) % devices) for i in range(devices)])  15.5 us
    ppermute x9, waiting for transfers between devices, from_behind(): lax.ppermute(value, axis, [(i, (i + by) % devices) for i in range(devices)])  15.2 us
    ppermute x8, waiting for transfers between devices, swapped(): return lax.ppermute(value, axis, [(0, 1), (1, 0)])  14.5 us
    ppermute x1, waiting for transfers between devices, body(): below = lax.ppermute(page[:half_rows], 'tile', down)  9.81 us
    ppermute x1, waiting for transfers between devices, body(): above = lax.ppermute(page[half_rows:], 'tile', up)  5.76 us
    ppermute x8, starting transfers between devices, swapped(): return lax.ppermute(value, axis, [(0, 1), (1, 0)])  4.86 us
    ppermute x1, starting transfers between devices, body(): above = lax.ppermute(page[half_rows:], 'tile', up)  4.65 us
  transfers between devices with their start and end apart: 19, of which 9 were waited for; matrix products, arithmetic and copies ran while one was open for 0% of the time, Pallas kernels for 21%

profile of v1, /device:TPU:0, one launch (start us, length us, event | category | flops | bytes accessed | tf_op | source)
XLA Modules:
  0.0 96.0 jit_solution(15672764474681666506)
XLA Ops:
  0.6 1.6 %copy.10 = bf16[64,8,2,512]{3,1,2,0:T(8,128)(2,1)S(1)} copy(bf16[64,8,2,512]{3,2,1,0:T(2,128)(2,1)} %bitcast.19) | data formatting | bytes 2097152
  2.8 4.7 %collective-permute-start = (bf16[144,1024]{1,0:T(8,128)(2,1)S(1)}, bf16[144,1024]{1,0:T(8,128)(2,1)S(1)}, u32[]{:S(2)}, u32[]{:S(2)}) collective-permute-start(bf16[144,1024]{1,0:T(8,128)(2,1)S(1)} %bitcast.22), channel_id=1, source_target_pairs={{0,4},{4,8},{8,12},{1,5},{5,9},{9,13},{2,6},{6,10},{10,14},{3,7},{... | collective-permute-start | bytes 884744 | tf_op jit(solution)/shard_map/ppermute | solution.py:369
  8.5 5.8 %collective-permute-done.above = bf16[144,1024]{1,0:T(8,128)(2,1)S(1)} collective-permute-done((bf16[144,1024]{1,0:T(8,128)(2,1)S(1)}, bf16[144,1024]{1,0:T(8,128)(2,1)S(1)}, u32[]{:S(2)}, u32[]{:S(2)}) %collective-permute-start) | collective-permute-done | bytes 294944 | tf_op jit(solution)/shard_map/ppermute | solution.py:369
  14.2 1.3 %collective-permute-start.1 = (bf16[144,1024]{1,0:T(8,128)(2,1)S(1)}, bf16[144,1024]{1,0:T(8,128)(2,1)S(1)}, u32[]{:S(2)}, u32[]{:S(2)}) collective-permute-start(bf16[144,1024]{1,0:T(8,128)(2,1)S(1)} %bitcast.21), channel_id=1, source_target_pairs={{4,0},{8,4},{12,8},{5,1},{9,5},{13,9},{6,2},{10,6},{14,10},{7,3},{... | collective-permute-start | bytes 884744 | tf_op jit(solution)/shard_map/ppermute | solution.py:370
  15.5 9.8 %collective-permute-done.1.below = bf16[144,1024]{1,0:T(8,128)(2,1)S(1)} collective-permute-done((bf16[144,1024]{1,0:T(8,128)(2,1)S(1)}, bf16[144,1024]{1,0:T(8,128)(2,1)S(1)}, u32[]{:S(2)}, u32[]{:S(2)}) %collective-permute-start.1) | collective-permute-done | bytes 294944 | tf_op jit(solution)/shard_map/ppermute | solution.py:370
  25.4 12.2 %shard_map.95.mine = bf16[288,1024]{1,0:T(8,128)(2,1)S(1)} custom-call(bf16[288,1024]{1,0:T(8,128)(2,1)S(1)} %bitcast.11, bf16[144,1024]{1,0:T(8,128)(2,1)S(1)} %collective-permute-done.above, bf16[144,1024]{1,0:T(8,128)(2,1)S(1)} %collective-permute-done.1.below, bf16[512,512]{1,0:T(8,128)(2,1)S(1)} %copy-done.2, ...), custom_call_target="tpu_custom_call" | custom-call | tf_op jit(solution)/shard_map/pallas_call | solution.py:333
  37.6 1.6 %collective-permute-start.5 = (bf16[288,1024]{1,0:T(8,128)(2,1)S(1)}, bf16[288,1024]{1,0:T(8,128)(2,1)S(1)}, u32[]{:S(2)}, u32[]{:S(2)}) collective-permute-start(bf16[288,1024]{1,0:T(8,128)(2,1)S(1)} %shard_map.95.mine), channel_id=1, source_target_pairs={{0,2},{2,0},{1,3},{3,1},{4,6},{6,4},{5,7},{7,5},{8,10},{10,8},{9,1... | collective-permute-start | bytes 1769480 | tf_op jit(solution)/shard_map/ppermute | solution.py:165
  39.7 1.4 %collective-permute-done.7.wq_x = bf16[512,512]{1,0:T(8,128)(2,1)S(1)} collective-permute-done((bf16[512,512]{1,0:T(8,128)(2,1)S(1)}, bf16[512,512]{1,0:T(8,128)(2,1)S(1)}, u32[]{:S(2)}, u32[]{:S(2)}) %collective-permute-start.7) | collective-permute-done | bytes 524320 | tf_op jit(solution)/shard_map/ppermute | solution.py:165
  41.9 1.8 %collective-permute-start.10 = (bf16[256,128]{1,0:T(8,128)(2,1)S(1)}, bf16[256,128]{1,0:T(8,128)(2,1)S(1)}, u32[]{:S(2)}, u32[]{:S(2)}) collective-permute-start(bf16[256,128]{1,0:T(8,128)(2,1)S(1)} %get-tuple-element.21), channel_id=1, source_target_pairs={{0,12},{4,0},{8,4},{12,8},{1,13},{5,1},{9,5},{13,9},{2,14},{6,2},{... | collective-permute-start | bytes 196616 | tf_op jit(solution)/shard_map/ppermute | solution.py:21
  43.7 8.2 %collective-permute-done.5.theirs = bf16[288,1024]{1,0:T(8,128)(2,1)S(1)} collective-permute-done((bf16[288,1024]{1,0:T(8,128)(2,1)S(1)}, bf16[288,1024]{1,0:T(8,128)(2,1)S(1)}, u32[]{:S(2)}, u32[]{:S(2)}) %collective-permute-start.5) | collective-permute-done | bytes 589856 | tf_op jit(solution)/shard_map/ppermute | solution.py:165
  51.9 1.9 %shard_map.96 = (bf16[288,1024]{1,0:T(8,128)(2,1)}, bf16[288,256]{1,0:T(8,128)(2,1)S(1)}, bf16[288,256]{1,0:T(8,128)(2,1)S(1)}, bf16[288,256]{1,0:T(8,128)(2,1)S(1)}, bf16[288,256]{1,0:T(8,128)(2,1)S(1)}) custom-call(bf16[288,1024]{1,0:T(8,128)(2,1)S(1)} %bitcast.12, bf16[288,1024]{1,0:T(8,128)(2,1)S(1)} %shard_map.95.mine, ...), custom_call_target="tpu_custom_call" | custom-call | tf_op jit(solution)/shard_map/pallas_call | solution.py:333
  53.8 1.4 %collective-permute-start.11 = (bf16[288,256]{1,0:T(8,128)(2,1)S(1)}, bf16[288,256]{1,0:T(8,128)(2,1)S(1)}, u32[]{:S(2)}, u32[]{:S(2)}) collective-permute-start(bf16[288,256]{1,0:T(8,128)(2,1)S(1)} %get-tuple-element.23), channel_id=1, source_target_pairs={{0,4},{4,8},{8,12},{12,0},{1,5},{5,9},{9,13},{13,1},{2,6},{6,10},{... | collective-permute-start | bytes 442376 | tf_op jit(solution)/shard_map/ppermute | solution.py:21
  55.2 1.0 %collective-permute-start.12 = (bf16[288,256]{1,0:T(8,128)(2,1)S(1)}, bf16[288,256]{1,0:T(8,128)(2,1)S(1)}, u32[]{:S(2)}, u32[]{:S(2)}) collective-permute-start(bf16[288,256]{1,0:T(8,128)(2,1)S(1)} %get-tuple-element.24), channel_id=1, source_target_pairs={{0,8},{4,12},{8,0},{12,4},{1,9},{5,13},{9,1},{13,5},{2,10},{6,14},... | collective-permute-start | bytes 442376 | tf_op jit(solution)/shard_map/ppermute | solution.py:21
  56.2 2.9 %collective-permute-start.13 = (bf16[288,256]{1,0:T(8,128)(2,1)S(1)}, bf16[288,256]{1,0:T(8,128)(2,1)S(1)}, u32[]{:S(2)}, u32[]{:S(2)}) collective-permute-start(bf16[288,256]{1,0:T(8,128)(2,1)S(1)} %get-tuple-element.25), channel_id=1, source_target_pairs={{0,12},{4,0},{8,4},{12,8},{1,13},{5,1},{9,5},{13,9},{2,14},{6,2},{... | collective-permute-start | bytes 442376 | tf_op jit(solution)/shard_map/ppermute | solution.py:21
  59.1 8.1 %collective-permute-done.8.refs_1_ = bf16[256,128]{1,0:T(8,128)(2,1)S(1)} collective-permute-done((bf16[256,128]{1,0:T(8,128)(2,1)S(1)}, bf16[256,128]{1,0:T(8,128)(2,1)S(1)}, u32[]{:S(2)}, u32[]{:S(2)}) %collective-permute-start.8) | collective-permute-done | bytes 65568 | tf_op jit(solution)/shard_map/ppermute | solution.py:21
  67.2 4.0 %collective-permute-start.9 = (bf16[256,128]{1,0:T(8,128)(2,1)S(1)}, bf16[256,128]{1,0:T(8,128)(2,1)S(1)}, u32[]{:S(2)}, u32[]{:S(2)}) collective-permute-start(bf16[256,128]{1,0:T(8,128)(2,1)S(1)} %get-tuple-element.20), channel_id=1, source_target_pairs={{0,8},{4,12},{8,0},{12,4},{1,9},{5,13},{9,1},{13,5},{2,10},{6,14},... | collective-permute-start | bytes 196616 | tf_op jit(solution)/shard_map/ppermute | solution.py:21
  71.3 2.9 %collective-permute-done.9.refs_2_ = bf16[256,128]{1,0:T(8,128)(2,1)S(1)} collective-permute-done((bf16[256,128]{1,0:T(8,128)(2,1)S(1)}, bf16[256,128]{1,0:T(8,128)(2,1)S(1)}, u32[]{:S(2)}, u32[]{:S(2)}) %collective-permute-start.9) | collective-permute-done | bytes 65568 | tf_op jit(solution)/shard_map/ppermute | solution.py:21
  74.2 5.6 %shard_map.98 = (bf16[256,128]{1,0:T(8,128)(2,1)S(1)}, bf16[256,128]{1,0:T(8,128)(2,1)S(1)}, bf16[256,128]{1,0:T(8,128)(2,1)S(1)}, bf16[256,128]{1,0:T(8,128)(2,1)S(1)}) custom-call(bf16[256,128]{1,0:T(8,128)(2,1)S(1)} %get-tuple-element.18.refs_0_, bf16[256,128]{1,0:T(8,128)(2,1)S(1)} %collective-permute-done.8.refs_1_, ...), custom_call_target="tpu_custom_call" | custom-call | tf_op jit(solution)/shard_map/pallas_call | solution.py:333
  80.2 2.1 %collective-permute-start.15 = (bf16[256,128]{1,0:T(8,128)(2,1)S(1)}, bf16[256,128]{1,0:T(8,128)(2,1)S(1)}, u32[]{:S(2)}, u32[]{:S(2)}) collective-permute-start(bf16[256,128]{1,0:T(8,128)(2,1)S(1)} %get-tuple-element.28), channel_id=1, source_target_pairs={{0,8},{4,12},{8,0},{12,4},{1,9},{5,13},{9,1},{13,5},{2,10},{6,14},... | collective-permute-start | bytes 196616 | tf_op jit(solution)/shard_map/ppermute | solution.py:21
  82.2 1.9 %collective-permute-start.16 = (bf16[256,128]{1,0:T(8,128)(2,1)S(1)}, bf16[256,128]{1,0:T(8,128)(2,1)S(1)}, u32[]{:S(2)}, u32[]{:S(2)}) collective-permute-start(bf16[256,128]{1,0:T(8,128)(2,1)S(1)} %get-tuple-element.29), channel_id=1, source_target_pairs={{0,4},{4,8},{8,12},{12,0},{1,5},{5,9},{9,13},{13,1},{2,6},{6,10},{... | collective-permute-start | bytes 196616 | tf_op jit(solution)/shard_map/ppermute | solution.py:21
  84.2 1.1 %collective-permute-done.15.refs_2_ = bf16[256,128]{1,0:T(8,128)(2,1)S(1)} collective-permute-done((bf16[256,128]{1,0:T(8,128)(2,1)S(1)}, bf16[256,128]{1,0:T(8,128)(2,1)S(1)}, u32[]{:S(2)}, u32[]{:S(2)}) %collective-permute-start.15) | collective-permute-done | bytes 65568 | tf_op jit(solution)/shard_map/ppermute | solution.py:21
  85.3 3.0 %collective-permute-done.16.refs_3_ = bf16[256,128]{1,0:T(8,128)(2,1)S(1)} collective-permute-done((bf16[256,128]{1,0:T(8,128)(2,1)S(1)}, bf16[256,128]{1,0:T(8,128)(2,1)S(1)}, u32[]{:S(2)}, u32[]{:S(2)}) %collective-permute-start.16) | collective-permute-done | bytes 65568 | tf_op jit(solution)/shard_map/ppermute | solution.py:21
  88.8 1.5 %collective-permute-start.18 = (bf16[128,1024]{1,0:T(8,128)(2,1)S(1)}, bf16[128,1024]{1,0:T(8,128)(2,1)S(1)}, u32[]{:S(2)}, u32[]{:S(2)}) collective-permute-start(bf16[128,1024]{1,0:T(8,128)(2,1)S(1)} %get-tuple-element.31), channel_id=1, source_target_pairs={{0,2},{2,0},{1,3},{3,1},{4,6},{6,4},{5,7},{7,5},{8,10},{10,8},{9,1... | collective-permute-start | bytes 786440 | tf_op jit(solution)/shard_map/ppermute | solution.py:165
  90.4 4.9 %collective-permute-done.18 = bf16[128,1024]{1,0:T(8,128)(2,1)S(1)} collective-permute-done((bf16[128,1024]{1,0:T(8,128)(2,1)S(1)}, bf16[128,1024]{1,0:T(8,128)(2,1)S(1)}, u32[]{:S(2)}, u32[]{:S(2)}) %collective-permute-start.18) | collective-permute-done | bytes 262176 | tf_op jit(solution)/shard_map/ppermute | solution.py:165
  (37 shorter events, 4.5 us)
Async XLA Ops:
  0.6 7.4 %copy-start.6 = (bf16[512,2,512]{2,1,0:T(2,128)(2,1)S(1)}, bf16[512,2,512]{2,1,0:T(2,128)(2,1)}, u32[]{:S(2)}) copy-start(bf16[512,2,512]{2,1,0:T(2,128)(2,1)} %param.14) | copy-start | bytes 3145732
  2.3 5.4 %copy-start.3 = (bf16[512,512]{1,0:T(8,128)(2,1)S(1)}, bf16[512,512]{1,0:T(8,128)(2,1)}, u32[]{:S(2)}) copy-start(bf16[512,512]{1,0:T(8,128)(2,1)} %wp_o.1) | copy-start | bytes 1572868
  2.3 23.1 %collective-permute-start.3 = (bf16[512,1024]{1,0:T(8,128)(2,1)S(1)}, bf16[512,1024]{1,0:T(8,128)(2,1)S(1)}, u32[]{:S(2)}, u32[]{:S(2)}) collective-permute-start(bf16[512,1024]{1,0:T(8,128)(2,1)S(1)} %bitcast.15), channel_id=1, source_target_pairs={{0,1},{1,0},{2,3},{3,2},{4,5},{5,4},{6,7},{7,6},{8,9},{9,8},{10,11... | collective-permute-start | bytes 3145736 | tf_op jit(solution)/shard_map/ppermute | solution.py:165
  2.8 11.4 %collective-permute-start = (bf16[144,1024]{1,0:T(8,128)(2,1)S(1)}, bf16[144,1024]{1,0:T(8,128)(2,1)S(1)}, u32[]{:S(2)}, u32[]{:S(2)}) collective-permute-start(bf16[144,1024]{1,0:T(8,128)(2,1)S(1)} %bitcast.22), channel_id=1, source_target_pairs={{0,4},{4,8},{8,12},{1,5},{5,9},{9,13},{2,6},{6,10},{10,14},{3,7},{... | collective-permute-start | bytes 884744 | tf_op jit(solution)/shard_map/ppermute | solution.py:369
  7.5 17.8 %collective-permute-start.2 = (bf16[512,512]{1,0:T(8,128)(2,1)S(1)}, bf16[512,512]{1,0:T(8,128)(2,1)S(1)}, u32[]{:S(2)}, u32[]{:S(2)}) collective-permute-start(bf16[512,512]{1,0:T(8,128)(2,1)S(1)} %copy-done.2), channel_id=1, source_target_pairs={{0,1},{1,0},{2,3},{3,2},{4,5},{5,4},{6,7},{7,6},{8,9},{9,8},{10,11... | collective-permute-start | bytes 1572872 | tf_op jit(solution)/shard_map/ppermute | solution.py:165
  7.6 17.7 %collective-permute-start.4 = (bf16[512,512]{1,0:T(8,128)(2,1)S(1)}, bf16[512,512]{1,0:T(8,128)(2,1)S(1)}, u32[]{:S(2)}, u32[]{:S(2)}) collective-permute-start(bf16[512,512]{1,0:T(8,128)(2,1)S(1)} %copy-done.3), channel_id=1, source_target_pairs={{0,1},{1,0},{2,3},{3,2},{4,5},{5,4},{6,7},{7,6},{8,9},{9,8},{10,11... | collective-permute-start | bytes 1572872 | tf_op jit(solution)/shard_map/ppermute | solution.py:165
  8.3 35.3 %collective-permute-start.6 = (bf16[512,1024]{1,0:T(8,128)(2,1)S(1)}, bf16[512,1024]{1,0:T(8,128)(2,1)S(1)}, u32[]{:S(2)}, u32[]{:S(2)}) collective-permute-start(bf16[512,1024]{1,0:T(8,128)(2,1)S(1)} %bitcast.13), channel_id=1, source_target_pairs={{0,1},{1,0},{2,3},{3,2},{4,5},{5,4},{6,7},{7,6},{8,9},{9,8},{10,11... | collective-permute-start | bytes 3145736 | tf_op jit(solution)/shard_map/ppermute | solution.py:165
  14.2 11.1 %collective-permute-start.1 = (bf16[144,1024]{1,0:T(8,128)(2,1)S(1)}, bf16[144,1024]{1,0:T(8,128)(2,1)S(1)}, u32[]{:S(2)}, u32[]{:S(2)}) collective-permute-start(bf16[144,1024]{1,0:T(8,128)(2,1)S(1)} %bitcast.21), channel_id=1, source_target_pairs={{4,0},{8,4},{12,8},{5,1},{9,5},{13,9},{6,2},{10,6},{14,10},{7,3},{... | collective-permute-start | bytes 884744 | tf_op jit(solution)/shard_map/ppermute | solution.py:370
  25.3 13.8 %copy-start.4 = (bf16[512,512]{1,0:T(8,128)(2,1)S(1)}, bf16[512,512]{1,0:T(8,128)(2,1)}, u32[]{:S(2)}) copy-start(bf16[512,512]{1,0:T(8,128)(2,1)} %wq_o.3) | copy-start | bytes 1572868
  25.4 13.8 %copy-start.5 = (bf16[512,512]{1,0:T(8,128)(2,1)S(1)}, bf16[512,512]{1,0:T(8,128)(2,1)}, u32[]{:S(2)}) copy-start(bf16[512,512]{1,0:T(8,128)(2,1)} %refs_4_.1) | copy-start | bytes 1572868
  25.4 15.7 %copy-start.1 = (bf16[1,256,1024]{2,1,0:T(8,128)(2,1)S(1)}, bf16[1,256,1024]{2,1,0:T(8,128)(2,1)}, u32[]{:S(2)}) copy-start(bf16[1,256,1024]{2,1,0:T(8,128)(2,1)} %param.9) | copy-start | bytes 1572868
  37.6 14.3 %collective-permute-start.5 = (bf16[288,1024]{1,0:T(8,128)(2,1)S(1)}, bf16[288,1024]{1,0:T(8,128)(2,1)S(1)}, u32[]{:S(2)}, u32[]{:S(2)}) collective-permute-start(bf16[288,1024]{1,0:T(8,128)(2,1)S(1)} %shard_map.95.mine), channel_id=1, source_target_pairs={{0,2},{2,0},{1,3},{3,1},{4,6},{6,4},{5,7},{7,5},{8,10},{10,8},{9,1... | collective-permute-start | bytes 1769480 | tf_op jit(solution)/shard_map/ppermute | solution.py:165
  39.2 1.9 %collective-permute-start.7 = (bf16[512,512]{1,0:T(8,128)(2,1)S(1)}, bf16[512,512]{1,0:T(8,128)(2,1)S(1)}, u32[]{:S(2)}, u32[]{:S(2)}) collective-permute-start(bf16[512,512]{1,0:T(8,128)(2,1)S(1)} %copy-done.4), channel_id=1, source_target_pairs={{0,1},{1,0},{2,3},{3,2},{4,5},{5,4},{6,7},{7,6},{8,9},{9,8},{10,11... | collective-permute-start | bytes 1572872 | tf_op jit(solution)/shard_map/ppermute | solution.py:165
  39.2 45.0 %collective-permute-start.17 = (bf16[512,512]{1,0:T(8,128)(2,1)S(1)}, bf16[512,512]{1,0:T(8,128)(2,1)S(1)}, u32[]{:S(2)}, u32[]{:S(2)}) collective-permute-start(bf16[512,512]{1,0:T(8,128)(2,1)S(1)} %copy-done.5), channel_id=1, source_target_pairs={{0,1},{1,0},{2,3},{3,2},{4,5},{5,4},{6,7},{7,6},{8,9},{9,8},{10,11... | collective-permute-start | bytes 1572872 | tf_op jit(solution)/shard_map/ppermute | solution.py:165
  41.9 17.2 %collective-permute-start.10 = (bf16[256,128]{1,0:T(8,128)(2,1)S(1)}, bf16[256,128]{1,0:T(8,128)(2,1)S(1)}, u32[]{:S(2)}, u32[]{:S(2)}) collective-permute-start(bf16[256,128]{1,0:T(8,128)(2,1)S(1)} %get-tuple-element.21), channel_id=1, source_target_pairs={{0,12},{4,0},{8,4},{12,8},{1,13},{5,1},{9,5},{13,9},{2,14},{6,2},{... | collective-permute-start | bytes 196616 | tf_op jit(solution)/shard_map/ppermute | solution.py:21
  53.8 20.5 %collective-permute-start.11 = (bf16[288,256]{1,0:T(8,128)(2,1)S(1)}, bf16[288,256]{1,0:T(8,128)(2,1)S(1)}, u32[]{:S(2)}, u32[]{:S(2)}) collective-permute-start(bf16[288,256]{1,0:T(8,128)(2,1)S(1)} %get-tuple-element.23), channel_id=1, source_target_pairs={{0,4},{4,8},{8,12},{12,0},{1,5},{5,9},{9,13},{13,1},{2,6},{6,10},{... | collective-permute-start | bytes 442376 | tf_op jit(solution)/shard_map/ppermute | solution.py:21
  55.2 19.0 %collective-permute-start.12 = (bf16[288,256]{1,0:T(8,128)(2,1)S(1)}, bf16[288,256]{1,0:T(8,128)(2,1)S(1)}, u32[]{:S(2)}, u32[]{:S(2)}) collective-permute-start(bf16[288,256]{1,0:T(8,128)(2,1)S(1)} %get-tuple-element.24), channel_id=1, source_target_pairs={{0,8},{4,12},{8,0},{12,4},{1,9},{5,13},{9,1},{13,5},{2,10},{6,14},... | collective-permute-start | bytes 442376 | tf_op jit(solution)/shard_map/ppermute | solution.py:21
  56.2 18.0 %collective-permute-start.13 = (bf16[288,256]{1,0:T(8,128)(2,1)S(1)}, bf16[288,256]{1,0:T(8,128)(2,1)S(1)}, u32[]{:S(2)}, u32[]{:S(2)}) collective-permute-start(bf16[288,256]{1,0:T(8,128)(2,1)S(1)} %get-tuple-element.25), channel_id=1, source_target_pairs={{0,12},{4,0},{8,4},{12,8},{1,13},{5,1},{9,5},{13,9},{2,14},{6,2},{... | collective-permute-start | bytes 442376 | tf_op jit(solution)/shard_map/ppermute | solution.py:21
  59.1 8.1 %collective-permute-start.8 = (bf16[256,128]{1,0:T(8,128)(2,1)S(1)}, bf16[256,128]{1,0:T(8,128)(2,1)S(1)}, u32[]{:S(2)}, u32[]{:S(2)}) collective-permute-start(bf16[256,128]{1,0:T(8,128)(2,1)S(1)} %get-tuple-element.19), channel_id=1, source_target_pairs={{0,4},{4,8},{8,12},{12,0},{1,5},{5,9},{9,13},{13,1},{2,6},{6,10},{... | collective-permute-start | bytes 196616 | tf_op jit(solution)/shard_map/ppermute | solution.py:21
  67.2 7.0 %collective-permute-start.9 = (bf16[256,128]{1,0:T(8,128)(2,1)S(1)}, bf16[256,128]{1,0:T(8,128)(2,1)S(1)}, u32[]{:S(2)}, u32[]{:S(2)}) collective-permute-start(bf16[256,128]{1,0:T(8,128)(2,1)S(1)} %get-tuple-element.20), channel_id=1, source_target_pairs={{0,8},{4,12},{8,0},{12,4},{1,9},{5,13},{9,1},{13,5},{2,10},{6,14},... | collective-permute-start | bytes 196616 | tf_op jit(solution)/shard_map/ppermute | solution.py:21
  79.9 4.3 %collective-permute-start.14 = (bf16[256,128]{1,0:T(8,128)(2,1)S(1)}, bf16[256,128]{1,0:T(8,128)(2,1)S(1)}, u32[]{:S(2)}, u32[]{:S(2)}) collective-permute-start(bf16[256,128]{1,0:T(8,128)(2,1)S(1)} %get-tuple-element.27), channel_id=1, source_target_pairs={{0,12},{4,0},{8,4},{12,8},{1,13},{5,1},{9,5},{13,9},{2,14},{6,2},{... | collective-permute-start | bytes 196616 | tf_op jit(solution)/shard_map/ppermute | solution.py:21
  80.2 5.2 %collective-permute-start.15 = (bf16[256,128]{1,0:T(8,128)(2,1)S(1)}, bf16[256,128]{1,0:T(8,128)(2,1)S(1)}, u32[]{:S(2)}, u32[]{:S(2)}) collective-permute-start(bf16[256,128]{1,0:T(8,128)(2,1)S(1)} %get-tuple-element.28), channel_id=1, source_target_pairs={{0,8},{4,12},{8,0},{12,4},{1,9},{5,13},{9,1},{13,5},{2,10},{6,14},... | collective-permute-start | bytes 196616 | tf_op jit(solution)/shard_map/ppermute | solution.py:21
  82.2 6.1 %collective-permute-start.16 = (bf16[256,128]{1,0:T(8,128)(2,1)S(1)}, bf16[256,128]{1,0:T(8,128)(2,1)S(1)}, u32[]{:S(2)}, u32[]{:S(2)}) collective-permute-start(bf16[256,128]{1,0:T(8,128)(2,1)S(1)} %get-tuple-element.29), channel_id=1, source_target_pairs={{0,4},{4,8},{8,12},{12,0},{1,5},{5,9},{9,13},{13,1},{2,6},{6,10},{... | collective-permute-start | bytes 196616 | tf_op jit(solution)/shard_map/ppermute | solution.py:21
  88.8 6.4 %collective-permute-start.18 = (bf16[128,1024]{1,0:T(8,128)(2,1)S(1)}, bf16[128,1024]{1,0:T(8,128)(2,1)S(1)}, u32[]{:S(2)}, u32[]{:S(2)}) collective-permute-start(bf16[128,1024]{1,0:T(8,128)(2,1)S(1)} %get-tuple-element.31), channel_id=1, source_target_pairs={{0,2},{2,0},{1,3},{3,1},{4,6},{6,4},{5,7},{7,5},{8,10},{10,8},{9,1... | collective-permute-start | bytes 786440 | tf_op jit(solution)/shard_map/ppermute | solution.py:165
  (2 other events, 7.4 us)

commit v2 on v1

--- a/solution.py
+++ b/solution.py
@@ -192,59 +192,76 @@
     return lax.broadcasted_iota(jnp.int32, shape, 1) // size
 
 
-def enc_kernel(
-    columns, page, above, below, wq_o, wq_x, wkv_o, wkv_x, wp_o, wp_x, part, xn, qs, kvs, wo, bias
+LOG2E = math.log2(math.e)
+EXCLUDED = -1e30
+
+
+def own_kernel(page, wq_o, wq_x, wkv_o, wkv_x, q_out, kv_out, xn):
+    own, other = halves(page.shape[1])
+    xn[...] = norm_rows(page)
+    q_out[...] = (dot(xn[:, own], wq_o[...]) + dot(xn[:, other], wq_x[...])).astype(BF16)
+    kv_out[...] = (dot(xn[:, own], wkv_o[...]) + dot(xn[:, other], wkv_x[...])).astype(BF16)
+
+
+def col_group(col, offset):
+    window = 2 * offset
+    return jnp.where(col < offset, 0, 1 + jnp.maximum(col - offset, 0) // window)
+
+
+def win_kernel(
+    columns, half, q_own, kv_own, halo, wkv_o, wkv_x, wp_o, wp_x, part, xn, kx, vx, ql, wo
 ):
-    rows, width = page.shape
-    part_rows = rows // 2
-    offset = part_rows // columns
-    window = 2 * offset
-    hq = wq_o.shape[1]
+    rows, width = halo.shape
+    hq = q_own.shape[1]
+    offset = rows // columns
+    groups = columns // (2 * offset) + 1
     own, other = halves(width)
-    xn[:part_rows] = norm_rows(above)
-    xn[part_rows : part_rows + rows] = norm_rows(page)
-    xn[part_rows + rows :] = norm_rows(below)
-    kvs[...] = (dot(xn[:, own], wkv_o[...]) + dot(xn[:, other], wkv_x[...])).astype(BF16)
-    mine = slice(part_rows, part_rows + rows)
-    qs[...] = (dot(xn[mine, own], wq_o[...]) + dot(xn[mine, other], wq_x[...])).astype(BF16)
+    xn[...] = norm_rows(halo)
+    kv_halo = (dot(xn[:, own], wkv_o[...]) + dot(xn[:, other], wkv_x[...])).astype(BF16)
+    kv_here = kv_own[half * rows : (half + 1) * rows, :]
 
     tile = lax.axis_index("tile")
-    edge = (tile == 0, tile == lax.axis_size("tile") - 1)
-    shape = (part_rows, rows)
-    q_col = lax.broadcasted_iota(jnp.int32, shape, 0) % columns
-    key = lax.broadcasted_iota(jnp.int32, shape, 1)
-    k_col = key % columns
-
-    def group(col):
-        return jnp.where(col < offset, 0, 1 + (col - offset + window) // window)
-
-    same = group(q_col) == group(k_col)
-    outside = (key < part_rows, key >= part_rows)
-    for half in range(2):
-        cut = jnp.logical_and(outside[half], edge[half])
-        allowed = jnp.logical_and(same, jnp.logical_not(cut))
-        bias[half] = jnp.where(allowed, 0.0, -jnp.inf).astype(F32)
-
-    scale = 1.0 / math.sqrt(HEAD_ENC)
-    q_head = lane_head((part_rows, LANES), HEAD_ENC)
-    k_head = lane_head((rows, LANES), HEAD_ENC)
-    for half in range(2):
-        q_rows = slice(half * part_rows, (half + 1) * part_rows)
-        k_rows = slice(half * rows, (half + 1) * rows)
-        for lanes in range(hq // LANES):
-            cols = slice(lanes * LANES, (lanes + 1) * LANES)
-            v_cols = slice(hq + lanes * LANES, hq + (lanes + 1) * LANES)
-            q = qs[q_rows, cols]
-            k = kvs[k_rows, cols]
-            v = kvs[k_rows, v_cols]
-            acc = jnp.zeros((part_rows, LANES), F32)
-            for head in range(LANES // HEAD_ENC):
-                s = dot_t(jnp.where(q_head == head, q, jnp.zeros_like(q)), k) * scale
-                s = s + bias[half]
-                e = jnp.exp(s - jnp.max(s, axis=-1, keepdims=True))
-                w = (e / jnp.sum(e, axis=-1, keepdims=True)).astype(BF16)
-                acc = acc + dot(w, jnp.where(k_head == head, v, jnp.zeros_like(v)))
-            wo[q_rows, cols] = acc.astype(BF16)
+    edge = tile == (0 if half == 0 else lax.axis_size("tile") - 1)
+    lane = lax.broadcasted_iota(jnp.int32, (rows, LANES), 1)
+    group = col_group(lax.broadcasted_iota(jnp.int32, (rows, LANES), 0) % columns, offset)
+    unlike = jnp.logical_and(lane < groups, lane != group)
+    cut = jnp.logical_and(lane == groups, edge)
+    off = jnp.full((rows, LANES), EXCLUDED, F32)
+    here_marks = jnp.where(unlike, off, 0.0).astype(BF16)
+    halo_marks = jnp.where(jnp.logical_or(unlike, cut), off, 0.0).astype(BF16)
+    q_marks = jnp.where(jnp.logical_or(lane == group, lane == groups), 1.0, 0.0).astype(BF16)
+    ones = jnp.ones((2 * rows, LANES), BF16)
+    heads = LANES // HEAD_ENC
+    for h in range(heads):
+        ql[h * rows : (h + 1) * rows, LANES:] = q_marks
+    for g in range(hq // LANES):
+        k_cols = slice(g * LANES, (g + 1) * LANES)
+        v_cols = slice(hq + g * LANES, hq + (g + 1) * LANES)
+        wide = slice(2 * g * LANES, (2 * g + 1) * LANES)
+        extra = slice((2 * g + 1) * LANES, (2 * g + 2) * LANES)
+        kx[:rows, wide] = kv_here[:, k_cols]
+        kx[rows:, wide] = kv_halo[:, k_cols]
+        kx[:rows, extra] = here_marks
+        kx[rows:, extra] = halo_marks
+        vx[:rows, wide] = kv_here[:, v_cols]
+        vx[rows:, wide] = kv_halo[:, v_cols]
+        vx[:, extra] = ones
+    scale = LOG2E / math.sqrt(HEAD_ENC)
+    q_head = lane // HEAD_ENC
+    for g in range(hq // LANES):
+        q = q_own[half * rows : (half + 1) * rows, g * LANES : (g + 1) * LANES]
+        both = slice(2 * g * LANES, (2 * g + 2) * LANES)
+        for h in range(heads):
+            ql[h * rows : (h + 1) * rows, :LANES] = jnp.where(q_head == h, q, jnp.zeros_like(q))
+        s = dot_t(ql[...], kx[:, both])
+        e = jnp.exp2((s - jnp.max(s, axis=-1, keepdims=True)) * scale).astype(BF16)
+        o = dot(e, vx[:, both])
+        acc = None
+        for h in range(heads):
+            block = slice(h * rows, (h + 1) * rows)
+            one = o[block, :LANES] / o[block, LANES:]
+            acc = one if acc is None else jnp.where(q_head == h, one, acc)
+        wo[:, g * LANES : (g + 1) * LANES] = acc.astype(BF16)
     part[:, own] = dot(wo[...], wp_o[...]).astype(BF16)
     part[:, other] = dot(wo[...], wp_x[...]).astype(BF16)
 
@@ -258,12 +275,13 @@
         outs[s][:, out_col : out_col + LANES] = scratch[:, pl.ds(start, LANES)]
 
 
-def kv_kernel(page, mine, theirs, wkv_o, wkv_x, encoded, *rest):
+def kv_kernel(half, page, mine, theirs, wkv_o, wkv_x, encoded, *rest):
     outs, (xn, kvs) = rest[:-2], rest[-2:]
-    width = page.shape[1]
+    rows, width = mine.shape
     own, other = halves(width)
     total = mine[...].astype(F32) + theirs[...].astype(F32)
-    encoded[...] = (page[...].astype(F32) + total).astype(BF16)
+    here = page[half * rows : (half + 1) * rows, :]
+    encoded[...] = (here.astype(F32) + total).astype(BF16)
     xn[...] = norm_rows(encoded)
     kvs[...] = (dot(xn[:, own], wkv_o[...]) + dot(xn[:, other], wkv_x[...])).astype(BF16)
     pieces(kvs, 0, outs, 0)
@@ -280,30 +298,33 @@
 
 def cross_kernel(tiles, *refs):
     q_in = refs[:tiles]
-    kv_in = refs[tiles : 2 * tiles]
-    outs = refs[2 * tiles : 3 * tiles]
-    kv, sem = refs[3 * tiles :]
+    kv_in = refs[tiles : 3 * tiles]
+    outs = refs[3 * tiles : 4 * tiles]
+    kv, ql, sem = refs[4 * tiles :]
     rows = kv_in[0].shape[0]
     copies = [
-        pltpu.make_async_copy(kv_in[s], kv.at[pl.ds(s * rows, rows)], sem.at[s])
-        for s in range(tiles)
+        pltpu.make_async_copy(
+            kv_in[s], kv.at[pl.ds(s * rows, rows), pl.ds(0, 2 * LANES)], sem.at[s]
+        )
+        for s in range(2 * tiles)
     ]
     for copy in copies:
         copy.start()
+    kv[:, 2 * LANES :] = jnp.ones((kv.shape[0], LANES), BF16)
+    tokens = q_in[0].shape[0]
+    q_head = lane_head(q_in[0].shape, HEAD_DEC)
+    scale = LOG2E / math.sqrt(HEAD_DEC)
     for copy in copies:
         copy.wait()
-    scale = 1.0 / math.sqrt(HEAD_DEC)
-    q_head = lane_head(q_in[0].shape, HEAD_DEC)
     for s in range(tiles):
         q = q_in[s][...]
-        acc = None
-        for head in range(LANES // HEAD_DEC):
-            sc = dot_t(jnp.where(q_head == head, q, jnp.zeros_like(q)), kv[:, :LANES]) * scale
-            e = jnp.exp(sc - jnp.max(sc, axis=-1, keepdims=True))
-            total = jnp.sum(e, axis=-1, keepdims=True)
-            out = dot(e.astype(BF16), kv[:, LANES:]) / total
-            acc = out if acc is None else jnp.where(q_head == head, out, acc)
-        outs[s][...] = acc.astype(BF16)
+        for h in range(LANES // HEAD_DEC):
+            ql[h * tokens : (h + 1) * tokens] = jnp.where(q_head == h, q, jnp.zeros_like(q))
+        sc = dot_t(ql[...], kv[:, :LANES])
+        e = jnp.exp2((sc - jnp.max(sc, axis=-1, keepdims=True)) * scale).astype(BF16)
+        o = dot(e, kv[:, LANES:])
+        o = o[:, :LANES] / o[:, LANES:]
+        outs[s][...] = jnp.where(q_head == 0, o[:tokens], o[tokens:]).astype(BF16)
 
 
 def out_kernel(tiles, *refs):
@@ -329,15 +350,23 @@
 ANY = pl.BlockSpec(memory_space=pl.ANY)
 
 
-def call(kernel, outs, scratch, *args, specs=None):
+def call(kernel, flops, outs, scratch, *args, specs=None):
+    moved = sum(math.prod(a.shape) * 2 for a in args) + sum(math.prod(s) * 2 for s, _ in outs)
     return pl.pallas_call(
         kernel,
         out_shape=[jax.ShapeDtypeStruct(shape, dtype) for shape, dtype in outs],
         in_specs=specs or [VM] * len(args),
         out_specs=[VM] * len(outs),
         scratch_shapes=scratch,
+        cost_estimate=pl.CostEstimate(flops=flops, transcendentals=0, bytes_accessed=moved)
+        if flops
+        else None,
         compiler_params=pltpu.CompilerParams(vmem_limit_bytes=VMEM_LIMIT),
     )(*args)
+
+
+def after(value, *earlier):
+    return lax.optimization_barrier((value,) + earlier)[0]
 
 
 def body(page_cells, text_states, enc_query, enc_keyval, enc_proj, dec_query, dec_keyval, dec_out):
@@ -360,43 +389,31 @@
     page = page_cells.reshape(rows, width)
     text = text_states.reshape(-1, width)
     tokens = text.shape[0]
-    wkv_enc = enc_keyval.reshape(width // 2, 2 * hq_enc)
-    wkv_dec = dec_keyval.reshape(width // 2, 2 * hq_dec)
     up = [(i, i + 1) for i in range(tiles - 1)]
     down = [(i + 1, i) for i in range(tiles - 1)]
+    upper, lower = page[:half_rows], page[half_rows:]
+    above = lax.ppermute(lower, "tile", up)
+    below = lax.ppermute(upper, "tile", down)
+    wkv_enc = enc_keyval.reshape(width // 2, 2 * hq_enc)
+    wkv_x = swapped(wkv_enc, "batch")
     wq_x = swapped(enc_query, "batch")
-    wkv_x = swapped(wkv_enc, "batch")
-    above = lax.ppermute(page[half_rows:], "tile", up)
-    below = lax.ppermute(page[:half_rows], "tile", down)
     wp_x = swapped(enc_proj, "batch")
-    dq_x = swapped(dec_query, "batch")
-    dkv_x = swapped(wkv_dec, "batch")
-    do_x = swapped(dec_out, "batch")
-
-    (part,) = call(
-        functools.partial(enc_kernel, columns),
-        [((rows, width), BF16)],
-        [
-            pltpu.VMEM((2 * rows, width), BF16),
-            pltpu.VMEM((rows, hq_enc), BF16),
-            pltpu.VMEM((2 * rows, 2 * hq_enc), BF16),
-            pltpu.VMEM((rows, hq_enc), BF16),
-            pltpu.VMEM((2, half_rows, rows), F32),
-        ],
+    dq_x = swapped(after(dec_query, wkv_x), "batch")
+
+    q_own, kv_own = call(
+        own_kernel,
+        1,
+        [((rows, hq_enc), BF16), ((rows, 2 * hq_enc), BF16)],
+        [pltpu.VMEM((rows, width), BF16)],
         page,
-        above,
-        below,
         enc_query,
         wq_x,
         wkv_enc,
         wkv_x,
-        enc_proj,
-        wp_x,
-    )
-    theirs = swapped(part, "mp")
-
+    )
     q_out = call(
         query_kernel,
+        1,
         [((tokens, LANES), BF16)] * tiles,
         [pltpu.VMEM((tokens, width), BF16), pltpu.VMEM((tokens, hq_dec), BF16)],
         text,
@@ -405,30 +422,76 @@
     )
     q_in = [q_out[0]] + [from_behind(q_out[s], "tile", s) for s in range(1, tiles)]
 
-    encoded, *kv_out = call(
-        kv_kernel,
-        [((rows, width), BF16)] + [((rows, 2 * LANES), BF16)] * tiles,
-        [pltpu.VMEM((rows, width), BF16), pltpu.VMEM((rows, 2 * hq_dec), BF16)],
-        page,
-        part,
-        theirs,
-        wkv_dec,
-        dkv_x,
-    )
-    kv_in = [kv_out[0]] + [from_behind(kv_out[s], "tile", s) for s in range(1, tiles)]
+    def window_half(half, halo):
+        (part,) = call(
+            functools.partial(win_kernel, columns, half),
+            2 * half_rows * width * 3 * hq_enc + 8 * half_rows * rows * LANES * hq_enc // HEAD_ENC,
+            [((half_rows, width), BF16)],
+            [
+                pltpu.VMEM((half_rows, width), BF16),
+                pltpu.VMEM((rows, 2 * hq_enc), BF16),
+                pltpu.VMEM((rows, 2 * hq_enc), BF16),
+                pltpu.VMEM((LANES // HEAD_ENC * half_rows, 2 * LANES), BF16),
+                pltpu.VMEM((half_rows, hq_enc), BF16),
+            ],
+            q_own,
+            kv_own,
+            halo,
+            wkv_enc,
+            wkv_x,
+            enc_proj,
+            wp_x,
+        )
+        return part
+
+    def key_values(half, part, theirs):
+        return call(
+            functools.partial(kv_kernel, half),
+            2 * half_rows * width * 2 * hq_dec,
+            [((half_rows, width), BF16)] + [((half_rows, 2 * LANES), BF16)] * tiles,
+            [pltpu.VMEM((half_rows, width), BF16), pltpu.VMEM((half_rows, 2 * hq_dec), BF16)],
+            page,
+            part,
+            theirs,
+            wkv_dec,
+            dkv_x,
+        )
+
+    above, below = lax.optimization_barrier((above, below, *q_out))[:2]
+    part_a = window_half(0, above)
+    theirs_a = swapped(part_a, "mp")
+    part_b = window_half(1, after(below, part_a))
+    wkv_dec = after(dec_keyval, part_b).reshape(width // 2, 2 * hq_dec)
+    dkv_x = swapped(wkv_dec, "batch")
+    theirs_b = swapped(part_b, "mp")
+    theirs_a, *q_in = lax.optimization_barrier((theirs_a, *q_in))
+    encoded_a, *kv_a = key_values(0, part_a, theirs_a)
+    kv_first = kv_a
+    kv_a = [kv_a[0]] + [from_behind(kv_a[s], "tile", s) for s in range(1, tiles)]
+    encoded_b, *kv_b = key_values(1, part_b, after(theirs_b, *kv_first))
+    kv_b = [kv_b[0]] + [from_behind(kv_b[s], "tile", s) for s in range(1, tiles)]
+    do_x = swapped(after(dec_out, encoded_b), "batch")
+    encoded = jnp.concatenate([encoded_a, encoded_b], axis=0)
 
     ctx_out = call(
         functools.partial(cross_kernel, tiles),
+        8 * tiles * tokens * tiles * rows * LANES,
         [((tokens, LANES), BF16)] * tiles,
-        [pltpu.VMEM((tiles * rows, 2 * LANES), BF16), pltpu.SemaphoreType.DMA((tiles,))],
+        [
+            pltpu.VMEM((tiles * rows, 3 * LANES), BF16),
+            pltpu.VMEM((LANES // HEAD_DEC * tokens, LANES), BF16),
+            pltpu.SemaphoreType.DMA((2 * tiles,)),
+        ],
         *q_in,
-        *kv_in,
-        specs=[VM] * tiles + [ANY] * tiles,
+        *kv_a,
+        *kv_b,
+        specs=[VM] * tiles + [ANY] * (2 * tiles),
     )
     ctx_in = [ctx_out[0]] + [from_behind(ctx_out[s], "tile", -s) for s in range(1, tiles)]
 
     keep, send = call(
         functools.partial(out_kernel, tiles),
+        2 * tokens * hq_dec * width,
         [((tokens // 2, width), F32), ((tokens // 2, width), BF16)],
         [pltpu.VMEM((tokens, hq_dec), BF16), pltpu.VMEM((tokens, width), F32)],
         *ctx_in,

time: 96.2 us -> 82.1 us (0.85)
  waiting for transfers between devices: 45.2 us -> 32 us
  Pallas kernels: 21.1 us -> 14 us
  starting transfers between devices: 26.3 us -> 31.3 us
    ppermute x2, waiting for transfers between devices: 15.6 us -> 7.3 us  [the longest x1 4.13 us: body(): below = lax.ppermute(upper, 'tile', down)]
    pallas_call x5 -> x8, Pallas kernels: 21.1 us -> 14 us  [call(): pl.pallas_call(kernel, out_shape=[jax.ShapeDtypeStruct(shape, dtype) for...]
    ppermute x8 -> x9, waiting for transfers between devices: 14.5 us -> 7.92 us  [swapped(): return lax.ppermute(value, axis, [(0, 1), (1, 0)])]
    ppermute x9 -> x12, starting transfers between devices: 15.5 us -> 20.2 us  [from_behind(): lax.ppermute(value, axis, [(i, (i + by) % devices) for i in range(devices)])]
    ppermute x9 -> x12, waiting for transfers between devices: 15.2 us -> 16.8 us  [from_behind(): lax.ppermute(value, axis, [(i, (i + by) % devices) for i in range(devices)])]
    ppermute x8 -> x9, starting transfers between devices: 4.86 us -> 5.12 us  [swapped(): return lax.ppermute(value, axis, [(0, 1), (1, 0)])]
  transfers between devices with their start and end apart: 19 -> 23, of which waited for: 9 -> 13; matrix products, arithmetic and copies ran while one was open for 0% -> 1% of each run, Pallas kernels for 21% -> 9%
where the time goes in v2:
time: 82.1 us; the launch traced here: 81.9 us
  waiting for transfers between devices  32 us (39%)
  starting transfers between devices  31.3 us (38%)
  Pallas kernels  14 us (17%)
  local copies, waits for them, and re-layouts  2.11 us (3%)
  other arithmetic  1.61 us (2%)
  between operations  0.84 us (1%)
    ppermute x12, starting transfers between devices, from_behind(): lax.ppermute(value, axis, [(i, (i + by) % devices) for i in range(devices)])  20.2 us
    ppermute x12, waiting for transfers between devices, from_behind(): lax.ppermute(value, axis, [(i, (i + by) % devices) for i in range(devices)])  16.8 us
    pallas_call x8, Pallas kernels, call(): pl.pallas_call(kernel, out_shape=[jax.ShapeDtypeStruct(shape, dtype) for...  14 us
    ppermute x9, waiting for transfers between devices, swapped(): return lax.ppermute(value, axis, [(0, 1), (1, 0)])  7.92 us
    ppermute x9, starting transfers between devices, swapped(): return lax.ppermute(value, axis, [(0, 1), (1, 0)])  5.12 us
    ppermute x1, starting transfers between devices, body(): above = lax.ppermute(lower, 'tile', up)  4.64 us
    ppermute x1, waiting for transfers between devices, body(): below = lax.ppermute(upper, 'tile', down)  4.13 us
    ppermute x1, waiting for transfers between devices, body(): above = lax.ppermute(lower, 'tile', up)  3.17 us
  transfers between devices with their start and end apart: 23, of which 13 were waited for; matrix products, arithmetic and copies ran while one was open for 1% of the time, Pallas kernels for 9%

profile of v2, /device:TPU:0, one launch (start us, length us, event | category | flops | bytes accessed | tf_op | source)
XLA Modules:
  0.0 81.9 jit_solution(12011070022417519031)
XLA Ops:
  0.7 1.6 %copy.10 = bf16[64,8,2,512]{3,1,2,0:T(8,128)(2,1)S(1)} copy(bf16[64,8,2,512]{3,2,1,0:T(2,128)(2,1)} %bitcast.23) | data formatting | bytes 2097152
  3.3 1.8 %collective-permute-done.1.wkv_x = bf16[512,1024]{1,0:T(8,128)(2,1)S(1)} collective-permute-done((bf16[512,1024]{1,0:T(8,128)(2,1)S(1)}, bf16[512,1024]{1,0:T(8,128)(2,1)S(1)}, u32[]{:S(2)}, u32[]{:S(2)}) %collective-permute-start.1) | collective-permute-done | bytes 1048608 | tf_op jit(solution)/shard_map/ppermute | solution.py:165
  5.5 4.6 %collective-permute-start.2 = (bf16[144,1024]{1,0:T(8,128)(2,1)S(1)}, bf16[144,1024]{1,0:T(8,128)(2,1)S(1)}, u32[]{:S(2)}, u32[]{:S(2)}) collective-permute-start(bf16[144,1024]{1,0:T(8,128)(2,1)S(1)} %bitcast.27), channel_id=1, source_target_pairs={{0,4},{4,8},{8,12},{1,5},{5,9},{9,13},{2,6},{6,10},{10,14},{3,7},{... | collective-permute-start | bytes 884744 | tf_op jit(solution)/shard_map/ppermute | solution.py:395
  11.5 1.4 %shard_map.95 = (bf16[288,512]{1,0:T(8,128)(2,1)S(1)}, bf16[288,1024]{1,0:T(8,128)(2,1)S(1)}) custom-call(bf16[288,1024]{1,0:T(8,128)(2,1)S(1)} %bitcast.18, bf16[512,512]{1,0:T(8,128)(2,1)S(1)} %copy-done.3, bf16[512,512]{1,0:T(8,128)(2,1)S(1)} %collective-permute-done.wq_x, bf16[512,1024]{1,0:T(8,128)(2,1)S(1)} %bitcast.12, ...), custom_call_target="tpu_custom_call" | custom-call | flops 1 | bytes 4620288 | tf_op jit(solution)/shard_map/pallas_call | solution.py:355
  13.7 3.2 %collective-permute-done.2.halo = bf16[144,1024]{1,0:T(8,128)(2,1)S(1)} collective-permute-done((bf16[144,1024]{1,0:T(8,128)(2,1)S(1)}, bf16[144,1024]{1,0:T(8,128)(2,1)S(1)}, u32[]{:S(2)}, u32[]{:S(2)}) %collective-permute-start.2) | collective-permute-done | bytes 294944 | tf_op jit(solution)/shard_map/ppermute | solution.py:395
  16.9 4.1 %collective-permute-done.3.halo = bf16[144,1024]{1,0:T(8,128)(2,1)S(1)} collective-permute-done((bf16[144,1024]{1,0:T(8,128)(2,1)S(1)}, bf16[144,1024]{1,0:T(8,128)(2,1)S(1)}, u32[]{:S(2)}, u32[]{:S(2)}) %collective-permute-start.3) | collective-permute-done | bytes 294944 | tf_op jit(solution)/shard_map/ppermute | solution.py:396
  21.0 2.8 %shard_map.97.mine = bf16[144,1024]{1,0:T(8,128)(2,1)S(1)} custom-call(bf16[288,512]{1,0:T(8,128)(2,1)S(1)} %get-tuple-element.36.q_own, bf16[288,1024]{1,0:T(8,128)(2,1)S(1)} %get-tuple-element.37.kv_own, bf16[144,1024]{1,0:T(8,128)(2,1)S(1)} %collective-permute-done.2.halo, bf16[512,1024]{1,0:T(8,128)(2,1)S(1)} %bitcast.13, ...), custom_call_target="tpu_custom_call" | custom-call | flops 1132462080 | bytes 4620288 | tf_op jit(solution)/shard_map/pallas_call | solution.py:355
  23.8 2.8 %shard_map.98.mine = bf16[144,1024]{1,0:T(8,128)(2,1)S(1)} custom-call(bf16[288,512]{1,0:T(8,128)(2,1)S(1)} %get-tuple-element.36.q_own, bf16[288,1024]{1,0:T(8,128)(2,1)S(1)} %get-tuple-element.37.kv_own, bf16[144,1024]{1,0:T(8,128)(2,1)S(1)} %collective-permute-done.3.halo, bf16[512,1024]{1,0:T(8,128)(2,1)S(1)} %bitcast.14, ...), custom_call_target="tpu_custom_call" | custom-call | flops 1132462080 | bytes 4620288 | tf_op jit(solution)/shard_map/pallas_call | solution.py:355
  27.0 1.6 %collective-permute-start.6 = (bf16[144,1024]{1,0:T(8,128)(2,1)S(1)}, bf16[144,1024]{1,0:T(8,128)(2,1)S(1)}, u32[]{:S(2)}, u32[]{:S(2)}) collective-permute-start(bf16[144,1024]{1,0:T(8,128)(2,1)S(1)} %shard_map.97.mine), channel_id=1, source_target_pairs={{0,2},{2,0},{1,3},{3,1},{4,6},{6,4},{5,7},{7,5},{8,10},{10,8},{9,1... | collective-permute-start | bytes 884744 | tf_op jit(solution)/shard_map/ppermute | solution.py:165
  29.1 1.6 %collective-permute-start.7 = (bf16[256,128]{1,0:T(8,128)(2,1)S(1)}, bf16[256,128]{1,0:T(8,128)(2,1)S(1)}, u32[]{:S(2)}, u32[]{:S(2)}) collective-permute-start(bf16[256,128]{1,0:T(8,128)(2,1)S(1)} %get-tuple-element.40), channel_id=1, source_target_pairs={{0,4},{4,8},{8,12},{12,0},{1,5},{5,9},{9,13},{13,1},{2,6},{6,10},{... | collective-permute-start | bytes 196616 | tf_op jit(solution)/shard_map/ppermute | solution.py:21
  31.6 3.9 %collective-permute-done.7.refs_1_ = bf16[256,128]{1,0:T(8,128)(2,1)S(1)} collective-permute-done((bf16[256,128]{1,0:T(8,128)(2,1)S(1)}, bf16[256,128]{1,0:T(8,128)(2,1)S(1)}, u32[]{:S(2)}, u32[]{:S(2)}) %collective-permute-start.7) | collective-permute-done | bytes 65568 | tf_op jit(solution)/shard_map/ppermute | solution.py:21
  35.5 2.5 %collective-permute-done.8.refs_2_ = bf16[256,128]{1,0:T(8,128)(2,1)S(1)} collective-permute-done((bf16[256,128]{1,0:T(8,128)(2,1)S(1)}, bf16[256,128]{1,0:T(8,128)(2,1)S(1)}, u32[]{:S(2)}, u32[]{:S(2)}) %collective-permute-start.8) | collective-permute-done | bytes 65568 | tf_op jit(solution)/shard_map/ppermute | solution.py:21
  38.0 1.8 %collective-permute-done.9.refs_3_ = bf16[256,128]{1,0:T(8,128)(2,1)S(1)} collective-permute-done((bf16[256,128]{1,0:T(8,128)(2,1)S(1)}, bf16[256,128]{1,0:T(8,128)(2,1)S(1)}, u32[]{:S(2)}, u32[]{:S(2)}) %collective-permute-start.9) | collective-permute-done | bytes 65568 | tf_op jit(solution)/shard_map/ppermute | solution.py:21
  40.6 2.1 %collective-permute-done.11.theirs = bf16[144,1024]{1,0:T(8,128)(2,1)S(1)} collective-permute-done((bf16[144,1024]{1,0:T(8,128)(2,1)S(1)}, bf16[144,1024]{1,0:T(8,128)(2,1)S(1)}, u32[]{:S(2)}, u32[]{:S(2)}) %collective-permute-start.11) | collective-permute-done | bytes 294944 | tf_op jit(solution)/shard_map/ppermute | solution.py:165
  43.8 1.6 %collective-permute-start.12 = (bf16[144,256]{1,0:T(8,128)(2,1)S(1)}, bf16[144,256]{1,0:T(8,128)(2,1)S(1)}, u32[]{:S(2)}, u32[]{:S(2)}) collective-permute-start(bf16[144,256]{1,0:T(8,128)(2,1)S(1)} %get-tuple-element.50), channel_id=1, source_target_pairs={{0,4},{4,8},{8,12},{12,0},{1,5},{5,9},{9,13},{13,1},{2,6},{6,10},{... | collective-permute-start | bytes 221192 | tf_op jit(solution)/shard_map/ppermute | solution.py:21
  46.3 2.9 %collective-permute-start.14 = (bf16[144,256]{1,0:T(8,128)(2,1)S(1)}, bf16[144,256]{1,0:T(8,128)(2,1)S(1)}, u32[]{:S(2)}, u32[]{:S(2)}) collective-permute-start(bf16[144,256]{1,0:T(8,128)(2,1)S(1)} %get-tuple-element.52), channel_id=1, source_target_pairs={{0,12},{4,0},{8,4},{12,8},{1,13},{5,1},{9,5},{13,9},{2,14},{6,2},{... | collective-permute-start | bytes 221192 | tf_op jit(solution)/shard_map/ppermute | solution.py:21
  50.5 3.3 %collective-permute-start.16 = (bf16[144,256]{1,0:T(8,128)(2,1)S(1)}, bf16[144,256]{1,0:T(8,128)(2,1)S(1)}, u32[]{:S(2)}, u32[]{:S(2)}) collective-permute-start(bf16[144,256]{1,0:T(8,128)(2,1)S(1)} %get-tuple-element.61), channel_id=1, source_target_pairs={{0,8},{4,12},{8,0},{12,4},{1,9},{5,13},{9,1},{13,5},{2,10},{6,14},... | collective-permute-start | bytes 221192 | tf_op jit(solution)/shard_map/ppermute | solution.py:21
  53.8 4.0 %collective-permute-start.17 = (bf16[144,256]{1,0:T(8,128)(2,1)S(1)}, bf16[144,256]{1,0:T(8,128)(2,1)S(1)}, u32[]{:S(2)}, u32[]{:S(2)}) collective-permute-start(bf16[144,256]{1,0:T(8,128)(2,1)S(1)} %get-tuple-element.62), channel_id=1, source_target_pairs={{0,12},{4,0},{8,4},{12,8},{1,13},{5,1},{9,5},{13,9},{2,14},{6,2},{... | collective-permute-start | bytes 221192 | tf_op jit(solution)/shard_map/ppermute | solution.py:21
  57.8 1.9 %collective-permute-done.16.refs_10_ = bf16[144,256]{1,0:T(8,128)(2,1)S(1)} collective-permute-done((bf16[144,256]{1,0:T(8,128)(2,1)S(1)}, bf16[144,256]{1,0:T(8,128)(2,1)S(1)}, u32[]{:S(2)}, u32[]{:S(2)}) %collective-permute-start.16) | collective-permute-done | bytes 73760 | tf_op jit(solution)/shard_map/ppermute | solution.py:21
  59.8 4.0 %shard_map.101 = (bf16[256,128]{1,0:T(8,128)(2,1)S(1)}, bf16[256,128]{1,0:T(8,128)(2,1)S(1)}, bf16[256,128]{1,0:T(8,128)(2,1)S(1)}, bf16[256,128]{1,0:T(8,128)(2,1)S(1)}) custom-call(bf16[256,128]{1,0:T(8,128)(2,1)S(1)} %get-tuple-element.55.refs_0_, bf16[256,128]{1,0:T(8,128)(2,1)S(1)} %collective-permute-done.7.refs_1_, ...), custom_call_target="tpu_custom_call" | custom-call | flops 1207959552 | bytes 1114112 | tf_op jit(solution)/shard_map/pallas_call | solution.py:355
  63.8 4.2 %collective-permute-start.18 = (bf16[256,128]{1,0:T(8,128)(2,1)S(1)}, bf16[256,128]{1,0:T(8,128)(2,1)S(1)}, u32[]{:S(2)}, u32[]{:S(2)}) collective-permute-start(bf16[256,128]{1,0:T(8,128)(2,1)S(1)} %get-tuple-element.64), channel_id=1, source_target_pairs={{0,12},{4,0},{8,4},{12,8},{1,13},{5,1},{9,5},{13,9},{2,14},{6,2},{... | collective-permute-start | bytes 196616 | tf_op jit(solution)/shard_map/ppermute | solution.py:21
  69.9 3.3 %collective-permute-done.19.refs_2_ = bf16[256,128]{1,0:T(8,128)(2,1)S(1)} collective-permute-done((bf16[256,128]{1,0:T(8,128)(2,1)S(1)}, bf16[256,128]{1,0:T(8,128)(2,1)S(1)}, u32[]{:S(2)}, u32[]{:S(2)}) %collective-permute-start.19) | collective-permute-done | bytes 65568 | tf_op jit(solution)/shard_map/ppermute | solution.py:21
  74.7 1.6 %collective-permute-start.22 = (bf16[128,1024]{1,0:T(8,128)(2,1)S(1)}, bf16[128,1024]{1,0:T(8,128)(2,1)S(1)}, u32[]{:S(2)}, u32[]{:S(2)}) collective-permute-start(bf16[128,1024]{1,0:T(8,128)(2,1)S(1)} %get-tuple-element.69), channel_id=1, source_target_pairs={{0,2},{2,0},{1,3},{3,1},{4,6},{6,4},{5,7},{7,5},{8,10},{10,8},{9,1... | collective-permute-start | bytes 786440 | tf_op jit(solution)/shard_map/ppermute | solution.py:165
  77.1 4.0 %collective-permute-done.22 = bf16[128,1024]{1,0:T(8,128)(2,1)S(1)} collective-permute-done((bf16[128,1024]{1,0:T(8,128)(2,1)S(1)}, bf16[128,1024]{1,0:T(8,128)(2,1)S(1)}, u32[]{:S(2)}, u32[]{:S(2)}) %collective-permute-start.22) | collective-permute-done | bytes 262176 | tf_op jit(solution)/shard_map/ppermute | solution.py:165
  (49 shorter events, 14.6 us)
Async XLA Ops:
  0.7 4.8 %copy-start = (bf16[1,12,24,1024]{3,2,1,0:T(8,128)(2,1)S(1)}, bf16[1,12,24,1024]{3,2,1,0:T(8,128)(2,1)}, u32[]{:S(2)}) copy-start(bf16[1,12,24,1024]{3,2,1,0:T(8,128)(2,1)} %param.8) | copy-start | bytes 1769476
  2.2 2.8 %collective-permute-start.1 = (bf16[512,1024]{1,0:T(8,128)(2,1)S(1)}, bf16[512,1024]{1,0:T(8,128)(2,1)S(1)}, u32[]{:S(2)}, u32[]{:S(2)}) collective-permute-start(bf16[512,1024]{1,0:T(8,128)(2,1)S(1)} %bitcast.11), channel_id=1, source_target_pairs={{0,1},{1,0},{2,3},{3,2},{4,5},{5,4},{6,7},{7,6},{8,9},{9,8},{10,11... | collective-permute-start | bytes 3145736 | tf_op jit(solution)/shard_map/ppermute | solution.py:165
  2.8 8.7 %collective-permute-start = (bf16[512,512]{1,0:T(8,128)(2,1)S(1)}, bf16[512,512]{1,0:T(8,128)(2,1)S(1)}, u32[]{:S(2)}, u32[]{:S(2)}) collective-permute-start(bf16[512,512]{1,0:T(8,128)(2,1)S(1)} %copy-done.3), channel_id=1, source_target_pairs={{0,1},{1,0},{2,3},{3,2},{4,5},{5,4},{6,7},{7,6},{8,9},{9,8},{10,11... | collective-permute-start | bytes 1572872 | tf_op jit(solution)/shard_map/ppermute | solution.py:165
  2.9 18.2 %collective-permute-start.5 = (bf16[512,512]{1,0:T(8,128)(2,1)S(1)}, bf16[512,512]{1,0:T(8,128)(2,1)S(1)}, u32[]{:S(2)}, u32[]{:S(2)}) collective-permute-start(bf16[512,512]{1,0:T(8,128)(2,1)S(1)} %copy-done.1), channel_id=1, source_target_pairs={{0,1},{1,0},{2,3},{3,2},{4,5},{5,4},{6,7},{7,6},{8,9},{9,8},{10,11... | collective-permute-start | bytes 1572872 | tf_op jit(solution)/shard_map/ppermute | solution.py:165
  5.1 7.8 %collective-permute-start.4 = (bf16[512,512]{1,0:T(8,128)(2,1)}, bf16[512,512]{1,0:T(8,128)(2,1)S(1)}, u32[]{:S(2)}, u32[]{:S(2)}) collective-permute-start(bf16[512,512]{1,0:T(8,128)(2,1)} %wq_o.3), channel_id=1, source_target_pairs={{0,1},{1,0},{2,3},{3,2},{4,5},{5,4},{6,7},{7,6},{8,9},{9,8},{10,11... | collective-permute-start | bytes 1572872 | tf_op jit(solution)/shard_map/ppermute | solution.py:165
  5.5 11.4 %collective-permute-start.2 = (bf16[144,1024]{1,0:T(8,128)(2,1)S(1)}, bf16[144,1024]{1,0:T(8,128)(2,1)S(1)}, u32[]{:S(2)}, u32[]{:S(2)}) collective-permute-start(bf16[144,1024]{1,0:T(8,128)(2,1)S(1)} %bitcast.27), channel_id=1, source_target_pairs={{0,4},{4,8},{8,12},{1,5},{5,9},{9,13},{2,6},{6,10},{10,14},{3,7},{... | collective-permute-start | bytes 884744 | tf_op jit(solution)/shard_map/ppermute | solution.py:395
  10.1 10.9 %collective-permute-start.3 = (bf16[144,1024]{1,0:T(8,128)(2,1)S(1)}, bf16[144,1024]{1,0:T(8,128)(2,1)S(1)}, u32[]{:S(2)}, u32[]{:S(2)}) collective-permute-start(bf16[144,1024]{1,0:T(8,128)(2,1)S(1)} %bitcast.26), channel_id=1, source_target_pairs={{4,0},{8,4},{12,8},{5,1},{9,5},{13,9},{6,2},{10,6},{14,10},{7,3},{... | collective-permute-start | bytes 884744 | tf_op jit(solution)/shard_map/ppermute | solution.py:396
  26.9 12.9 %collective-permute-start.10 = (bf16[512,1024]{1,0:T(8,128)(2,1)S(1)}, bf16[512,1024]{1,0:T(8,128)(2,1)S(1)}, u32[]{:S(2)}, u32[]{:S(2)}) collective-permute-start(bf16[512,1024]{1,0:T(8,128)(2,1)S(1)} %bitcast.15), channel_id=1, source_target_pairs={{0,1},{1,0},{2,3},{3,2},{4,5},{5,4},{6,7},{7,6},{8,9},{9,8},{10,11... | collective-permute-start | bytes 3145736 | tf_op jit(solution)/shard_map/ppermute | solution.py:165
  27.0 12.8 %collective-permute-start.6 = (bf16[144,1024]{1,0:T(8,128)(2,1)S(1)}, bf16[144,1024]{1,0:T(8,128)(2,1)S(1)}, u32[]{:S(2)}, u32[]{:S(2)}) collective-permute-start(bf16[144,1024]{1,0:T(8,128)(2,1)S(1)} %shard_map.97.mine), channel_id=1, source_target_pairs={{0,2},{2,0},{1,3},{3,1},{4,6},{6,4},{5,7},{7,5},{8,10},{10,8},{9,1... | collective-permute-start | bytes 884744 | tf_op jit(solution)/shard_map/ppermute | solution.py:165
  28.5 14.2 %collective-permute-start.11 = (bf16[144,1024]{1,0:T(8,128)(2,1)S(1)}, bf16[144,1024]{1,0:T(8,128)(2,1)S(1)}, u32[]{:S(2)}, u32[]{:S(2)}) collective-permute-start(bf16[144,1024]{1,0:T(8,128)(2,1)S(1)} %shard_map.98.mine), channel_id=1, source_target_pairs={{0,2},{2,0},{1,3},{3,1},{4,6},{6,4},{5,7},{7,5},{8,10},{10,8},{9,1... | collective-permute-start | bytes 884744 | tf_op jit(solution)/shard_map/ppermute | solution.py:165
  29.1 6.5 %collective-permute-start.7 = (bf16[256,128]{1,0:T(8,128)(2,1)S(1)}, bf16[256,128]{1,0:T(8,128)(2,1)S(1)}, u32[]{:S(2)}, u32[]{:S(2)}) collective-permute-start(bf16[256,128]{1,0:T(8,128)(2,1)S(1)} %get-tuple-element.40), channel_id=1, source_target_pairs={{0,4},{4,8},{8,12},{12,0},{1,5},{5,9},{9,13},{13,1},{2,6},{6,10},{... | collective-permute-start | bytes 196616 | tf_op jit(solution)/shard_map/ppermute | solution.py:21
  30.6 7.4 %collective-permute-start.8 = (bf16[256,128]{1,0:T(8,128)(2,1)S(1)}, bf16[256,128]{1,0:T(8,128)(2,1)S(1)}, u32[]{:S(2)}, u32[]{:S(2)}) collective-permute-start(bf16[256,128]{1,0:T(8,128)(2,1)S(1)} %get-tuple-element.41), channel_id=1, source_target_pairs={{0,8},{4,12},{8,0},{12,4},{1,9},{5,13},{9,1},{13,5},{2,10},{6,14},... | collective-permute-start | bytes 196616 | tf_op jit(solution)/shard_map/ppermute | solution.py:21
  35.5 4.3 %collective-permute-start.9 = (bf16[256,128]{1,0:T(8,128)(2,1)S(1)}, bf16[256,128]{1,0:T(8,128)(2,1)S(1)}, u32[]{:S(2)}, u32[]{:S(2)}) collective-permute-start(bf16[256,128]{1,0:T(8,128)(2,1)S(1)} %get-tuple-element.42), channel_id=1, source_target_pairs={{0,12},{4,0},{8,4},{12,8},{1,13},{5,1},{9,5},{13,9},{2,14},{6,2},{... | collective-permute-start | bytes 196616 | tf_op jit(solution)/shard_map/ppermute | solution.py:21
  43.8 30.4 %collective-permute-start.21 = (bf16[512,512]{1,0:T(8,128)(2,1)S(1)}, bf16[512,512]{1,0:T(8,128)(2,1)S(1)}, u32[]{:S(2)}, u32[]{:S(2)}) collective-permute-start(bf16[512,512]{1,0:T(8,128)(2,1)S(1)} %copy-done.5), channel_id=1, source_target_pairs={{0,1},{1,0},{2,3},{3,2},{4,5},{5,4},{6,7},{7,6},{8,9},{9,8},{10,11... | collective-permute-start | bytes 1572872 | tf_op jit(solution)/shard_map/ppermute | solution.py:165
  43.8 6.8 %collective-permute-start.12 = (bf16[144,256]{1,0:T(8,128)(2,1)S(1)}, bf16[144,256]{1,0:T(8,128)(2,1)S(1)}, u32[]{:S(2)}, u32[]{:S(2)}) collective-permute-start(bf16[144,256]{1,0:T(8,128)(2,1)S(1)} %get-tuple-element.50), channel_id=1, source_target_pairs={{0,4},{4,8},{8,12},{12,0},{1,5},{5,9},{9,13},{13,1},{2,6},{6,10},{... | collective-permute-start | bytes 221192 | tf_op jit(solution)/shard_map/ppermute | solution.py:21
  45.3 8.5 %collective-permute-start.13 = (bf16[144,256]{1,0:T(8,128)(2,1)S(1)}, bf16[144,256]{1,0:T(8,128)(2,1)S(1)}, u32[]{:S(2)}, u32[]{:S(2)}) collective-permute-start(bf16[144,256]{1,0:T(8,128)(2,1)S(1)} %get-tuple-element.51), channel_id=1, source_target_pairs={{0,8},{4,12},{8,0},{12,4},{1,9},{5,13},{9,1},{13,5},{2,10},{6,14},... | collective-permute-start | bytes 221192 | tf_op jit(solution)/shard_map/ppermute | solution.py:21
  46.3 11.5 %collective-permute-start.14 = (bf16[144,256]{1,0:T(8,128)(2,1)S(1)}, bf16[144,256]{1,0:T(8,128)(2,1)S(1)}, u32[]{:S(2)}, u32[]{:S(2)}) collective-permute-start(bf16[144,256]{1,0:T(8,128)(2,1)S(1)} %get-tuple-element.52), channel_id=1, source_target_pairs={{0,12},{4,0},{8,4},{12,8},{1,13},{5,1},{9,5},{13,9},{2,14},{6,2},{... | collective-permute-start | bytes 221192 | tf_op jit(solution)/shard_map/ppermute | solution.py:21
  49.3 8.6 %collective-permute-start.15 = (bf16[144,256]{1,0:T(8,128)(2,1)S(1)}, bf16[144,256]{1,0:T(8,128)(2,1)S(1)}, u32[]{:S(2)}, u32[]{:S(2)}) collective-permute-start(bf16[144,256]{1,0:T(8,128)(2,1)S(1)} %get-tuple-element.60), channel_id=1, source_target_pairs={{0,4},{4,8},{8,12},{12,0},{1,5},{5,9},{9,13},{13,1},{2,6},{6,10},{... | collective-permute-start | bytes 221192 | tf_op jit(solution)/shard_map/ppermute | solution.py:21
  50.5 9.3 %collective-permute-start.16 = (bf16[144,256]{1,0:T(8,128)(2,1)S(1)}, bf16[144,256]{1,0:T(8,128)(2,1)S(1)}, u32[]{:S(2)}, u32[]{:S(2)}) collective-permute-start(bf16[144,256]{1,0:T(8,128)(2,1)S(1)} %get-tuple-element.61), channel_id=1, source_target_pairs={{0,8},{4,12},{8,0},{12,4},{1,9},{5,13},{9,1},{13,5},{2,10},{6,14},... | collective-permute-start | bytes 221192 | tf_op jit(solution)/shard_map/ppermute | solution.py:21
  53.8 6.0 %collective-permute-start.17 = (bf16[144,256]{1,0:T(8,128)(2,1)S(1)}, bf16[144,256]{1,0:T(8,128)(2,1)S(1)}, u32[]{:S(2)}, u32[]{:S(2)}) collective-permute-start(bf16[144,256]{1,0:T(8,128)(2,1)S(1)} %get-tuple-element.62), channel_id=1, source_target_pairs={{0,12},{4,0},{8,4},{12,8},{1,13},{5,1},{9,5},{13,9},{2,14},{6,2},{... | collective-permute-start | bytes 221192 | tf_op jit(solution)/shard_map/ppermute | solution.py:21
  63.8 6.1 %collective-permute-start.18 = (bf16[256,128]{1,0:T(8,128)(2,1)S(1)}, bf16[256,128]{1,0:T(8,128)(2,1)S(1)}, u32[]{:S(2)}, u32[]{:S(2)}) collective-permute-start(bf16[256,128]{1,0:T(8,128)(2,1)S(1)} %get-tuple-element.64), channel_id=1, source_target_pairs={{0,12},{4,0},{8,4},{12,8},{1,13},{5,1},{9,5},{13,9},{2,14},{6,2},{... | collective-permute-start | bytes 196616 | tf_op jit(solution)/shard_map/ppermute | solution.py:21
  68.0 5.2 %collective-permute-start.19 = (bf16[256,128]{1,0:T(8,128)(2,1)S(1)}, bf16[256,128]{1,0:T(8,128)(2,1)S(1)}, u32[]{:S(2)}, u32[]{:S(2)}) collective-permute-start(bf16[256,128]{1,0:T(8,128)(2,1)S(1)} %get-tuple-element.65), channel_id=1, source_target_pairs={{0,8},{4,12},{8,0},{12,4},{1,9},{5,13},{9,1},{13,5},{2,10},{6,14},... | collective-permute-start | bytes 196616 | tf_op jit(solution)/shard_map/ppermute | solution.py:21
  68.0 6.1 %collective-permute-start.20 = (bf16[256,128]{1,0:T(8,128)(2,1)S(1)}, bf16[256,128]{1,0:T(8,128)(2,1)S(1)}, u32[]{:S(2)}, u32[]{:S(2)}) collective-permute-start(bf16[256,128]{1,0:T(8,128)(2,1)S(1)} %get-tuple-element.66), channel_id=1, source_target_pairs={{0,4},{4,8},{8,12},{12,0},{1,5},{5,9},{9,13},{13,1},{2,6},{6,10},{... | collective-permute-start | bytes 196616 | tf_op jit(solution)/shard_map/ppermute | solution.py:21
  74.7 6.4 %collective-permute-start.22 = (bf16[128,1024]{1,0:T(8,128)(2,1)S(1)}, bf16[128,1024]{1,0:T(8,128)(2,1)S(1)}, u32[]{:S(2)}, u32[]{:S(2)}) collective-permute-start(bf16[128,1024]{1,0:T(8,128)(2,1)S(1)} %get-tuple-element.69), channel_id=1, source_target_pairs={{0,2},{2,0},{1,3},{3,1},{4,6},{6,4},{5,7},{7,5},{8,10},{10,8},{9,1... | collective-permute-start | bytes 786440 | tf_op jit(solution)/shard_map/ppermute | solution.py:165
  (6 other events, 11.1 us)

commit v3 on v2

--- a/solution.py
+++ b/solution.py
@@ -296,17 +296,17 @@
     pieces(qs, 0, outs, 0)
 
 
-def cross_kernel(tiles, *refs):
-    q_in = refs[:tiles]
-    kv_in = refs[tiles : 3 * tiles]
-    outs = refs[3 * tiles : 4 * tiles]
-    kv, ql, sem = refs[4 * tiles :]
+def cross_kernel(count, strips, *refs):
+    q_in = refs[:count]
+    kv_in = refs[count : count + strips]
+    outs = refs[count + strips : 2 * count + strips]
+    kv, ql, sem = refs[2 * count + strips :]
     rows = kv_in[0].shape[0]
     copies = [
         pltpu.make_async_copy(
             kv_in[s], kv.at[pl.ds(s * rows, rows), pl.ds(0, 2 * LANES)], sem.at[s]
         )
-        for s in range(2 * tiles)
+        for s in range(strips)
     ]
     for copy in copies:
         copy.start()
@@ -316,7 +316,7 @@
     scale = LOG2E / math.sqrt(HEAD_DEC)
     for copy in copies:
         copy.wait()
-    for s in range(tiles):
+    for s in range(count):
         q = q_in[s][...]
         for h in range(LANES // HEAD_DEC):
             ql[h * tokens : (h + 1) * tokens] = jnp.where(q_head == h, q, jnp.zeros_like(q))
@@ -394,11 +394,10 @@
     upper, lower = page[:half_rows], page[half_rows:]
     above = lax.ppermute(lower, "tile", up)
     below = lax.ppermute(upper, "tile", down)
+    wkv_x = swapped(enc_keyval, "batch").reshape(width // 2, 2 * hq_enc)
     wkv_enc = enc_keyval.reshape(width // 2, 2 * hq_enc)
-    wkv_x = swapped(wkv_enc, "batch")
     wq_x = swapped(enc_query, "batch")
-    wp_x = swapped(enc_proj, "batch")
-    dq_x = swapped(after(dec_query, wkv_x), "batch")
+    dq_x = swapped(dec_query, "batch")
 
     q_own, kv_own = call(
         own_kernel,
@@ -416,11 +415,14 @@
         1,
         [((tokens, LANES), BF16)] * tiles,
         [pltpu.VMEM((tokens, width), BF16), pltpu.VMEM((tokens, hq_dec), BF16)],
-        text,
+        after(text, q_own),
         dec_query,
         dq_x,
     )
     q_in = [q_out[0]] + [from_behind(q_out[s], "tile", s) for s in range(1, tiles)]
+
+    wp_x = swapped(enc_proj, "batch")
+    above, below, *q_in = lax.optimization_barrier((above, below, *q_in))
 
     def window_half(half, halo):
         (part,) = call(
@@ -457,37 +459,43 @@
             dkv_x,
         )
 
-    above, below = lax.optimization_barrier((above, below, *q_out))[:2]
     part_a = window_half(0, above)
+    wkv_dec = after(dec_keyval, part_a).reshape(width // 2, 2 * hq_dec)
+    dkv_x = swapped(wkv_dec, "batch")
     theirs_a = swapped(part_a, "mp")
     part_b = window_half(1, after(below, part_a))
-    wkv_dec = after(dec_keyval, part_b).reshape(width // 2, 2 * hq_dec)
-    dkv_x = swapped(wkv_dec, "batch")
     theirs_b = swapped(part_b, "mp")
-    theirs_a, *q_in = lax.optimization_barrier((theirs_a, *q_in))
     encoded_a, *kv_a = key_values(0, part_a, theirs_a)
-    kv_first = kv_a
     kv_a = [kv_a[0]] + [from_behind(kv_a[s], "tile", s) for s in range(1, tiles)]
-    encoded_b, *kv_b = key_values(1, part_b, after(theirs_b, *kv_first))
+    theirs_b, *kv_a = lax.optimization_barrier((theirs_b, *kv_a))
+    encoded_b, *kv_b = key_values(1, part_b, theirs_b)
     kv_b = [kv_b[0]] + [from_behind(kv_b[s], "tile", s) for s in range(1, tiles)]
     do_x = swapped(after(dec_out, encoded_b), "batch")
     encoded = jnp.concatenate([encoded_a, encoded_b], axis=0)
 
-    ctx_out = call(
-        functools.partial(cross_kernel, tiles),
-        8 * tiles * tokens * tiles * rows * LANES,
-        [((tokens, LANES), BF16)] * tiles,
-        [
-            pltpu.VMEM((tiles * rows, 3 * LANES), BF16),
-            pltpu.VMEM((LANES // HEAD_DEC * tokens, LANES), BF16),
-            pltpu.SemaphoreType.DMA((2 * tiles,)),
-        ],
-        *q_in,
-        *kv_a,
-        *kv_b,
-        specs=[VM] * tiles + [ANY] * (2 * tiles),
-    )
-    ctx_in = [ctx_out[0]] + [from_behind(ctx_out[s], "tile", -s) for s in range(1, tiles)]
+    def attend(queries, *earlier):
+        count = len(queries)
+        return call(
+            functools.partial(cross_kernel, count, 2 * tiles),
+            1,
+            [((tokens, LANES), BF16)] * count,
+            [
+                pltpu.VMEM((tiles * rows, 3 * LANES), BF16),
+                pltpu.VMEM((LANES // HEAD_DEC * tokens, LANES), BF16),
+                pltpu.SemaphoreType.DMA((2 * tiles,)),
+            ],
+            *queries,
+            *kv_a,
+            *kv_b,
+            specs=[VM] * count + [ANY] * (2 * tiles),
+        )
+
+    near = tiles // 2
+    ctx_far = attend(q_in[near:])
+    ctx_far_in = [from_behind(ctx_far[s - near], "tile", -s) for s in range(near, tiles)]
+    ctx_near = attend([after(q_in[0], ctx_far[0]), *q_in[1:near]])
+    ctx_in = [ctx_near[0]] + [from_behind(ctx_near[s], "tile", -s) for s in range(1, near)]
+    ctx_in += ctx_far_in
 
     keep, send = call(
         functools.partial(out_kernel, tiles),

time: 82.1 us -> 80.9 us (0.985)
  waiting for transfers between devices: 32 us -> 30.7 us
  starting transfers between devices: 31.3 us -> 30.2 us
  local copies, waits for them, and re-layouts: 2.11 us -> 3 us
    ppermute x1, waiting for transfers between devices: 4.13 us -> 0.01 us  [body(): below = lax.ppermute(upper, 'tile', down)]
    ppermute x12, waiting for transfers between devices: 16.8 us -> 20.4 us  [from_behind(): lax.ppermute(value, axis, [(i, (i + by) % devices) for i in range(devices)])]
    ppermute x1, waiting for transfers between devices: 3.17 us -> 0.01 us  [body(): above = lax.ppermute(lower, 'tile', up)]
    ppermute x9, waiting for transfers between devices: 7.92 us -> 10.3 us  [swapped(): return lax.ppermute(value, axis, [(0, 1), (1, 0)])]
    ppermute x12, starting transfers between devices: 20.2 us -> 19.1 us  [from_behind(): lax.ppermute(value, axis, [(i, (i + by) % devices) for i in range(devices)])]
    slice x1, local copies, waits for them, and re-layouts: 0.04 us -> 1.09 us  [body(): upper, lower = (page[:half_rows], page[half_rows:])]
    pallas_call x8 -> x9, Pallas kernels: 14 us -> 14.3 us  [call(): pl.pallas_call(kernel, out_shape=[jax.ShapeDtypeStruct(shape, dtype) for...]
    unnamed x16 -> x19, local copies, waits for them, and re-layouts: 2.07 us -> 1.92 us
  transfers between devices with their start and end apart: 23 -> 23, of which waited for: 13 -> 11; matrix products, arithmetic and copies ran while one was open for 1% -> 3% of each run, Pallas kernels for 9% -> 13%
where the time goes in v3:
time: 80.9 us; the launch traced here: 80.7 us
  waiting for transfers between devices  30.7 us (38%)
  starting transfers between devices  30.2 us (37%)
  Pallas kernels  14.3 us (18%)
  local copies, waits for them, and re-layouts  3 us (4%)
  other arithmetic  1.61 us (2%)
  between operations  0.86 us (1%)
    ppermute x12, waiting for transfers between devices, from_behind(): lax.ppermute(value, axis, [(i, (i + by) % devices) for i in range(devices)])  20.4 us
    ppermute x12, starting transfers between devices, from_behind(): lax.ppermute(value, axis, [(i, (i + by) % devices) for i in range(devices)])  19.1 us
    pallas_call x9, Pallas kernels, call(): pl.pallas_call(kernel, out_shape=[jax.ShapeDtypeStruct(shape, dtype) for...  14.3 us
    ppermute x9, waiting for transfers between devices, swapped(): return lax.ppermute(value, axis, [(0, 1), (1, 0)])  10.3 us
    ppermute x1, starting transfers between devices, body(): above = lax.ppermute(lower, 'tile', up)  4.93 us
    ppermute x9, starting transfers between devices, swapped(): return lax.ppermute(value, axis, [(0, 1), (1, 0)])  4.89 us
    unnamed x19, local copies, waits for them, and re-layouts  1.92 us
  transfers between devices with their start and end apart: 23, of which 11 were waited for; matrix products, arithmetic and copies ran while one was open for 3% of the time, Pallas kernels for 13%

profile of v3, /device:TPU:0, one launch (start us, length us, event | category | flops | bytes accessed | tf_op | source)
XLA Modules:
  0.0 80.7 jit_solution(1283627559536344688)
XLA Ops:
  2.8 4.9 %collective-permute-start.2 = (bf16[144,1024]{1,0:T(8,128)(2,1)S(1)}, bf16[144,1024]{1,0:T(8,128)(2,1)S(1)}, u32[]{:S(2)}, u32[]{:S(2)}) collective-permute-start(bf16[144,1024]{1,0:T(8,128)(2,1)S(1)} %bitcast.32), channel_id=1, source_target_pairs={{0,4},{4,8},{8,12},{1,5},{5,9},{9,13},{2,6},{6,10},{10,14},{3,7},{... | collective-permute-start | bytes 884744 | tf_op jit(solution)/shard_map/ppermute | solution.py:395
  10.6 1.4 %shard_map.95 = (bf16[288,512]{1,0:T(8,128)(2,1)S(1)}, bf16[288,1024]{1,0:T(8,128)(2,1)S(1)}) custom-call(bf16[288,1024]{1,0:T(8,128)(2,1)S(1)} %bitcast.22, bf16[512,512]{1,0:T(8,128)(2,1)S(1)} %copy-done.3, bf16[512,512]{1,0:T(8,128)(2,1)S(1)} %collective-permute-done.wq_x, bf16[512,1024]{1,0:T(8,128)(2,1)S(1)} %bitcast.13, bf16[512,1024]{1,0:T(8,128)(2,1)S(1)} %bitcast.16), custom_call_target="tpu_custom_call" | custom-call | flops 1 | bytes 4620288 | tf_op jit(solution)/shard_map/pallas_call | solution.py:355
  12.8 2.7 %collective-permute-start.5 = (bf16[256,128]{1,0:T(8,128)(2,1)S(1)}, bf16[256,128]{1,0:T(8,128)(2,1)S(1)}, u32[]{:S(2)}, u32[]{:S(2)}) collective-permute-start(bf16[256,128]{1,0:T(8,128)(2,1)S(1)} %get-tuple-element.44), channel_id=1, source_target_pairs={{0,4},{4,8},{8,12},{12,0},{1,5},{5,9},{9,13},{13,1},{2,6},{6,10},{... | collective-permute-start | bytes 196616 | tf_op jit(solution)/shard_map/ppermute | solution.py:21
  15.5 2.6 %collective-permute-start.6 = (bf16[256,128]{1,0:T(8,128)(2,1)S(1)}, bf16[256,128]{1,0:T(8,128)(2,1)S(1)}, u32[]{:S(2)}, u32[]{:S(2)}) collective-permute-start(bf16[256,128]{1,0:T(8,128)(2,1)S(1)} %get-tuple-element.45), channel_id=1, source_target_pairs={{0,8},{4,12},{8,0},{12,4},{1,9},{5,13},{9,1},{13,5},{2,10},{6,14},... | collective-permute-start | bytes 196616 | tf_op jit(solution)/shard_map/ppermute | solution.py:21
  18.1 1.3 %collective-permute-start.7 = (bf16[256,128]{1,0:T(8,128)(2,1)S(1)}, bf16[256,128]{1,0:T(8,128)(2,1)S(1)}, u32[]{:S(2)}, u32[]{:S(2)}) collective-permute-start(bf16[256,128]{1,0:T(8,128)(2,1)S(1)} %get-tuple-element.46), channel_id=1, source_target_pairs={{0,12},{4,0},{8,4},{12,8},{1,13},{5,1},{9,5},{13,9},{2,14},{6,2},{... | collective-permute-start | bytes 196616 | tf_op jit(solution)/shard_map/ppermute | solution.py:21
  19.5 3.5 %collective-permute-done.5.refs_1_ = bf16[256,128]{1,0:T(8,128)(2,1)S(1)} collective-permute-done((bf16[256,128]{1,0:T(8,128)(2,1)S(1)}, bf16[256,128]{1,0:T(8,128)(2,1)S(1)}, u32[]{:S(2)}, u32[]{:S(2)}) %collective-permute-start.5) | collective-permute-done | bytes 65568 | tf_op jit(solution)/shard_map/ppermute | solution.py:21
  24.3 2.8 %shard_map.97.mine = bf16[144,1024]{1,0:T(8,128)(2,1)S(1)} custom-call(bf16[288,512]{1,0:T(8,128)(2,1)S(1)} %get-tuple-element.40.q_own, bf16[288,1024]{1,0:T(8,128)(2,1)S(1)} %get-tuple-element.41.kv_own, bf16[144,1024]{1,0:T(8,128)(2,1)S(1)} %collective-permute-done.2.halo, bf16[512,1024]{1,0:T(8,128)(2,1)S(1)} %bitcast.14, ...), custom_call_target="tpu_custom_call" | custom-call | flops 1132462080 | bytes 4620288 | tf_op jit(solution)/shard_map/pallas_call | solution.py:355
  27.5 1.6 %collective-permute-start.9 = (bf16[144,1024]{1,0:T(8,128)(2,1)S(1)}, bf16[144,1024]{1,0:T(8,128)(2,1)S(1)}, u32[]{:S(2)}, u32[]{:S(2)}) collective-permute-start(bf16[144,1024]{1,0:T(8,128)(2,1)S(1)} %shard_map.97.mine), channel_id=1, source_target_pairs={{0,2},{2,0},{1,3},{3,1},{4,6},{6,4},{5,7},{7,5},{8,10},{10,8},{9,1... | collective-permute-start | bytes 884744 | tf_op jit(solution)/shard_map/ppermute | solution.py:165
  29.0 2.8 %shard_map.99.mine = bf16[144,1024]{1,0:T(8,128)(2,1)S(1)} custom-call(bf16[288,512]{1,0:T(8,128)(2,1)S(1)} %get-tuple-element.40.q_own, bf16[288,1024]{1,0:T(8,128)(2,1)S(1)} %get-tuple-element.41.kv_own, bf16[144,1024]{1,0:T(8,128)(2,1)S(1)} %collective-permute-done.3.halo, bf16[512,1024]{1,0:T(8,128)(2,1)S(1)} %bitcast.15, ...), custom_call_target="tpu_custom_call" | custom-call | flops 1132462080 | bytes 4620288 | tf_op jit(solution)/shard_map/pallas_call | solution.py:355
  32.4 4.9 %collective-permute-done.9.theirs = bf16[144,1024]{1,0:T(8,128)(2,1)S(1)} collective-permute-done((bf16[144,1024]{1,0:T(8,128)(2,1)S(1)}, bf16[144,1024]{1,0:T(8,128)(2,1)S(1)}, u32[]{:S(2)}, u32[]{:S(2)}) %collective-permute-start.9) | collective-permute-done | bytes 294944 | tf_op jit(solution)/shard_map/ppermute | solution.py:165
  40.0 2.0 %collective-permute-start.14 = (bf16[144,256]{1,0:T(8,128)(2,1)S(1)}, bf16[144,256]{1,0:T(8,128)(2,1)S(1)}, u32[]{:S(2)}, u32[]{:S(2)}) collective-permute-start(bf16[144,256]{1,0:T(8,128)(2,1)S(1)} %get-tuple-element.55), channel_id=1, source_target_pairs={{0,12},{4,0},{8,4},{12,8},{1,13},{5,1},{9,5},{13,9},{2,14},{6,2},{... | collective-permute-start | bytes 221192 | tf_op jit(solution)/shard_map/ppermute | solution.py:21
  43.2 1.9 %collective-permute-done.12.refs_3_ = bf16[144,256]{1,0:T(8,128)(2,1)S(1)} collective-permute-done((bf16[144,256]{1,0:T(8,128)(2,1)S(1)}, bf16[144,256]{1,0:T(8,128)(2,1)S(1)}, u32[]{:S(2)}, u32[]{:S(2)}) %collective-permute-start.12) | collective-permute-done | bytes 73760 | tf_op jit(solution)/shard_map/ppermute | solution.py:21
  45.1 1.9 %collective-permute-done.13.refs_4_ = bf16[144,256]{1,0:T(8,128)(2,1)S(1)} collective-permute-done((bf16[144,256]{1,0:T(8,128)(2,1)S(1)}, bf16[144,256]{1,0:T(8,128)(2,1)S(1)}, u32[]{:S(2)}, u32[]{:S(2)}) %collective-permute-start.13) | collective-permute-done | bytes 73760 | tf_op jit(solution)/shard_map/ppermute | solution.py:21
  48.1 1.7 %collective-permute-start.15 = (bf16[144,256]{1,0:T(8,128)(2,1)S(1)}, bf16[144,256]{1,0:T(8,128)(2,1)S(1)}, u32[]{:S(2)}, u32[]{:S(2)}) collective-permute-start(bf16[144,256]{1,0:T(8,128)(2,1)S(1)} %get-tuple-element.66), channel_id=1, source_target_pairs={{0,4},{4,8},{8,12},{12,0},{1,5},{5,9},{9,13},{13,1},{2,6},{6,10},{... | collective-permute-start | bytes 221192 | tf_op jit(solution)/shard_map/ppermute | solution.py:21
  50.7 1.4 %collective-permute-start.17 = (bf16[144,256]{1,0:T(8,128)(2,1)S(1)}, bf16[144,256]{1,0:T(8,128)(2,1)S(1)}, u32[]{:S(2)}, u32[]{:S(2)}) collective-permute-start(bf16[144,256]{1,0:T(8,128)(2,1)S(1)} %get-tuple-element.68), channel_id=1, source_target_pairs={{0,12},{4,0},{8,4},{12,8},{1,13},{5,1},{9,5},{13,9},{2,14},{6,2},{... | collective-permute-start | bytes 221192 | tf_op jit(solution)/shard_map/ppermute | solution.py:21
  52.1 2.9 %collective-permute-done.15.refs_7_ = bf16[144,256]{1,0:T(8,128)(2,1)S(1)} collective-permute-done((bf16[144,256]{1,0:T(8,128)(2,1)S(1)}, bf16[144,256]{1,0:T(8,128)(2,1)S(1)}, u32[]{:S(2)}, u32[]{:S(2)}) %collective-permute-start.15) | collective-permute-done | bytes 73760 | tf_op jit(solution)/shard_map/ppermute | solution.py:21
  55.0 2.7 %collective-permute-done.16.refs_8_ = bf16[144,256]{1,0:T(8,128)(2,1)S(1)} collective-permute-done((bf16[144,256]{1,0:T(8,128)(2,1)S(1)}, bf16[144,256]{1,0:T(8,128)(2,1)S(1)}, u32[]{:S(2)}, u32[]{:S(2)}) %collective-permute-start.16) | collective-permute-done | bytes 73760 | tf_op jit(solution)/shard_map/ppermute | solution.py:21
  57.8 2.2 %shard_map.101 = (bf16[256,128]{1,0:T(8,128)(2,1)S(1)}, bf16[256,128]{1,0:T(8,128)(2,1)S(1)}) custom-call(bf16[256,128]{1,0:T(8,128)(2,1)S(1)} %collective-permute-done.6.refs_0_, bf16[256,128]{1,0:T(8,128)(2,1)S(1)} %collective-permute-done.7.refs_1_, bf16[144,256]{1,0:T(8,128)(2,1)S(1)} %get-tuple-element.61.refs_2_, ...), custom_call_target="tpu_custom_call" | custom-call | flops 1 | bytes 851968 | tf_op jit(solution)/shard_map/pallas_call | solution.py:355
  61.1 2.2 %shard_map.102 = (bf16[256,128]{1,0:T(8,128)(2,1)S(1)}, bf16[256,128]{1,0:T(8,128)(2,1)S(1)}) custom-call(bf16[256,128]{1,0:T(8,128)(2,1)S(1)} %get-tuple-element.70.refs_0_, bf16[256,128]{1,0:T(8,128)(2,1)S(1)} %collective-permute-done.5.refs_1_, bf16[144,256]{1,0:T(8,128)(2,1)S(1)} %get-tuple-element.61.refs_2_, ...), custom_call_target="tpu_custom_call" | custom-call | flops 1 | bytes 851968 | tf_op jit(solution)/shard_map/pallas_call | solution.py:355
  63.2 3.4 %collective-permute-start.18 = (bf16[256,128]{1,0:T(8,128)(2,1)S(1)}, bf16[256,128]{1,0:T(8,128)(2,1)S(1)}, u32[]{:S(2)}, u32[]{:S(2)}) collective-permute-start(bf16[256,128]{1,0:T(8,128)(2,1)S(1)} %get-tuple-element.73), channel_id=1, source_target_pairs={{0,12},{4,0},{8,4},{12,8},{1,13},{5,1},{9,5},{13,9},{2,14},{6,2},{... | collective-permute-start | bytes 196616 | tf_op jit(solution)/shard_map/ppermute | solution.py:21
  66.7 2.0 %collective-permute-done.18.refs_1_ = bf16[256,128]{1,0:T(8,128)(2,1)S(1)} collective-permute-done((bf16[256,128]{1,0:T(8,128)(2,1)S(1)}, bf16[256,128]{1,0:T(8,128)(2,1)S(1)}, u32[]{:S(2)}, u32[]{:S(2)}) %collective-permute-start.18) | collective-permute-done | bytes 65568 | tf_op jit(solution)/shard_map/ppermute | solution.py:21
  68.6 4.1 %collective-permute-done.20.refs_3_ = bf16[256,128]{1,0:T(8,128)(2,1)S(1)} collective-permute-done((bf16[256,128]{1,0:T(8,128)(2,1)S(1)}, bf16[256,128]{1,0:T(8,128)(2,1)S(1)}, u32[]{:S(2)}, u32[]{:S(2)}) %collective-permute-start.20) | collective-permute-done | bytes 65568 | tf_op jit(solution)/shard_map/ppermute | solution.py:21
  73.3 1.6 %collective-permute-start.22 = (bf16[128,1024]{1,0:T(8,128)(2,1)S(1)}, bf16[128,1024]{1,0:T(8,128)(2,1)S(1)}, u32[]{:S(2)}, u32[]{:S(2)}) collective-permute-start(bf16[128,1024]{1,0:T(8,128)(2,1)S(1)} %get-tuple-element.77), channel_id=1, source_target_pairs={{0,2},{2,0},{1,3},{3,1},{4,6},{6,4},{5,7},{7,5},{8,10},{10,8},{9,1... | collective-permute-start | bytes 786440 | tf_op jit(solution)/shard_map/ppermute | solution.py:165
  75.7 4.2 %collective-permute-done.22 = bf16[128,1024]{1,0:T(8,128)(2,1)S(1)} collective-permute-done((bf16[128,1024]{1,0:T(8,128)(2,1)S(1)}, bf16[128,1024]{1,0:T(8,128)(2,1)S(1)}, u32[]{:S(2)}, u32[]{:S(2)}) %collective-permute-start.22) | collective-permute-done | bytes 262176 | tf_op jit(solution)/shard_map/ppermute | solution.py:165
  (53 shorter events, 17.1 us)
Async XLA Ops:
  0.6 7.1 %collective-permute-start.1 = (bf16[512,2,512]{2,1,0:T(2,128)(2,1)}, bf16[512,2,512]{2,1,0:T(2,128)(2,1)S(1)}, u32[]{:S(2)}, u32[]{:S(2)}) collective-permute-start(bf16[512,2,512]{2,1,0:T(2,128)(2,1)} %param.11), channel_id=1, source_target_pairs={{0,1},{1,0},{2,3},{3,2},{4,5},{5,4},{6,7},{7,6},{8,9},{9,8},{10,11... | collective-permute-start | bytes 3145736 | tf_op jit(solution)/shard_map/ppermute | solution.py:165
  1.2 8.5 %collective-permute-start = (bf16[512,512]{1,0:T(8,128)(2,1)}, bf16[512,512]{1,0:T(8,128)(2,1)S(1)}, u32[]{:S(2)}, u32[]{:S(2)}) collective-permute-start(bf16[512,512]{1,0:T(8,128)(2,1)} %wq_o.2), channel_id=1, source_target_pairs={{0,1},{1,0},{2,3},{3,2},{4,5},{5,4},{6,7},{7,6},{8,9},{9,8},{10,11... | collective-permute-start | bytes 1572872 | tf_op jit(solution)/shard_map/ppermute | solution.py:165
  1.2 10.8 %collective-permute-start.4 = (bf16[512,512]{1,0:T(8,128)(2,1)}, bf16[512,512]{1,0:T(8,128)(2,1)S(1)}, u32[]{:S(2)}, u32[]{:S(2)}) collective-permute-start(bf16[512,512]{1,0:T(8,128)(2,1)} %wq_o.3), channel_id=1, source_target_pairs={{0,1},{1,0},{2,3},{3,2},{4,5},{5,4},{6,7},{7,6},{8,9},{9,8},{10,11... | collective-permute-start | bytes 1572872 | tf_op jit(solution)/shard_map/ppermute | solution.py:165
  1.7 22.6 %collective-permute-start.8 = (bf16[512,512]{1,0:T(8,128)(2,1)}, bf16[512,512]{1,0:T(8,128)(2,1)S(1)}, u32[]{:S(2)}, u32[]{:S(2)}) collective-permute-start(bf16[512,512]{1,0:T(8,128)(2,1)} %wp_o.3), channel_id=1, source_target_pairs={{0,1},{1,0},{2,3},{3,2},{4,5},{5,4},{6,7},{7,6},{8,9},{9,8},{10,11... | collective-permute-start | bytes 1572872 | tf_op jit(solution)/shard_map/ppermute | solution.py:165
  2.8 15.3 %collective-permute-start.2 = (bf16[144,1024]{1,0:T(8,128)(2,1)S(1)}, bf16[144,1024]{1,0:T(8,128)(2,1)S(1)}, u32[]{:S(2)}, u32[]{:S(2)}) collective-permute-start(bf16[144,1024]{1,0:T(8,128)(2,1)S(1)} %bitcast.32), channel_id=1, source_target_pairs={{0,4},{4,8},{8,12},{1,5},{5,9},{9,13},{2,6},{6,10},{10,14},{3,7},{... | collective-permute-start | bytes 884744 | tf_op jit(solution)/shard_map/ppermute | solution.py:395
  7.8 11.7 %collective-permute-start.3 = (bf16[144,1024]{1,0:T(8,128)(2,1)S(1)}, bf16[144,1024]{1,0:T(8,128)(2,1)S(1)}, u32[]{:S(2)}, u32[]{:S(2)}) collective-permute-start(bf16[144,1024]{1,0:T(8,128)(2,1)S(1)} %bitcast.31), channel_id=1, source_target_pairs={{4,0},{8,4},{12,8},{5,1},{9,5},{13,9},{6,2},{10,6},{14,10},{7,3},{... | collective-permute-start | bytes 884744 | tf_op jit(solution)/shard_map/ppermute | solution.py:396
  12.0 12.3 %copy-start.1 = (bf16[512,512]{1,0:T(8,128)(2,1)S(1)}, bf16[512,512]{1,0:T(8,128)(2,1)}, u32[]{:S(2)}) copy-start(bf16[512,512]{1,0:T(8,128)(2,1)} %wp_o.3) | copy-start | bytes 1572868
  12.8 10.2 %collective-permute-start.5 = (bf16[256,128]{1,0:T(8,128)(2,1)S(1)}, bf16[256,128]{1,0:T(8,128)(2,1)S(1)}, u32[]{:S(2)}, u32[]{:S(2)}) collective-permute-start(bf16[256,128]{1,0:T(8,128)(2,1)S(1)} %get-tuple-element.44), channel_id=1, source_target_pairs={{0,4},{4,8},{8,12},{12,0},{1,5},{5,9},{9,13},{13,1},{2,6},{6,10},{... | collective-permute-start | bytes 196616 | tf_op jit(solution)/shard_map/ppermute | solution.py:21
  15.5 8.8 %collective-permute-start.6 = (bf16[256,128]{1,0:T(8,128)(2,1)S(1)}, bf16[256,128]{1,0:T(8,128)(2,1)S(1)}, u32[]{:S(2)}, u32[]{:S(2)}) collective-permute-start(bf16[256,128]{1,0:T(8,128)(2,1)S(1)} %get-tuple-element.45), channel_id=1, source_target_pairs={{0,8},{4,12},{8,0},{12,4},{1,9},{5,13},{9,1},{13,5},{2,10},{6,14},... | collective-permute-start | bytes 196616 | tf_op jit(solution)/shard_map/ppermute | solution.py:21
  18.1 6.2 %collective-permute-start.7 = (bf16[256,128]{1,0:T(8,128)(2,1)S(1)}, bf16[256,128]{1,0:T(8,128)(2,1)S(1)}, u32[]{:S(2)}, u32[]{:S(2)}) collective-permute-start(bf16[256,128]{1,0:T(8,128)(2,1)S(1)} %get-tuple-element.46), channel_id=1, source_target_pairs={{0,12},{4,0},{8,4},{12,8},{1,13},{5,1},{9,5},{13,9},{2,14},{6,2},{... | collective-permute-start | bytes 196616 | tf_op jit(solution)/shard_map/ppermute | solution.py:21
  27.4 10.0 %collective-permute-start.10 = (bf16[512,1024]{1,0:T(8,128)(2,1)S(1)}, bf16[512,1024]{1,0:T(8,128)(2,1)S(1)}, u32[]{:S(2)}, u32[]{:S(2)}) collective-permute-start(bf16[512,1024]{1,0:T(8,128)(2,1)S(1)} %bitcast.19), channel_id=1, source_target_pairs={{0,1},{1,0},{2,3},{3,2},{4,5},{5,4},{6,7},{7,6},{8,9},{9,8},{10,11... | collective-permute-start | bytes 3145736 | tf_op jit(solution)/shard_map/ppermute | solution.py:165
  27.5 9.9 %collective-permute-start.9 = (bf16[144,1024]{1,0:T(8,128)(2,1)S(1)}, bf16[144,1024]{1,0:T(8,128)(2,1)S(1)}, u32[]{:S(2)}, u32[]{:S(2)}) collective-permute-start(bf16[144,1024]{1,0:T(8,128)(2,1)S(1)} %shard_map.97.mine), channel_id=1, source_target_pairs={{0,2},{2,0},{1,3},{3,1},{4,6},{6,4},{5,7},{7,5},{8,10},{10,8},{9,1... | collective-permute-start | bytes 884744 | tf_op jit(solution)/shard_map/ppermute | solution.py:165
  31.8 11.4 %collective-permute-start.11 = (bf16[144,1024]{1,0:T(8,128)(2,1)S(1)}, bf16[144,1024]{1,0:T(8,128)(2,1)S(1)}, u32[]{:S(2)}, u32[]{:S(2)}) collective-permute-start(bf16[144,1024]{1,0:T(8,128)(2,1)S(1)} %shard_map.99.mine), channel_id=1, source_target_pairs={{0,2},{2,0},{1,3},{3,1},{4,6},{6,4},{5,7},{7,5},{8,10},{10,8},{9,1... | collective-permute-start | bytes 884744 | tf_op jit(solution)/shard_map/ppermute | solution.py:165
  38.2 6.9 %collective-permute-start.12 = (bf16[144,256]{1,0:T(8,128)(2,1)S(1)}, bf16[144,256]{1,0:T(8,128)(2,1)S(1)}, u32[]{:S(2)}, u32[]{:S(2)}) collective-permute-start(bf16[144,256]{1,0:T(8,128)(2,1)S(1)} %get-tuple-element.53), channel_id=1, source_target_pairs={{0,4},{4,8},{8,12},{12,0},{1,5},{5,9},{9,13},{13,1},{2,6},{6,10},{... | collective-permute-start | bytes 221192 | tf_op jit(solution)/shard_map/ppermute | solution.py:21
  39.5 7.5 %collective-permute-start.13 = (bf16[144,256]{1,0:T(8,128)(2,1)S(1)}, bf16[144,256]{1,0:T(8,128)(2,1)S(1)}, u32[]{:S(2)}, u32[]{:S(2)}) collective-permute-start(bf16[144,256]{1,0:T(8,128)(2,1)S(1)} %get-tuple-element.54), channel_id=1, source_target_pairs={{0,8},{4,12},{8,0},{12,4},{1,9},{5,13},{9,1},{13,5},{2,10},{6,14},... | collective-permute-start | bytes 221192 | tf_op jit(solution)/shard_map/ppermute | solution.py:21
  40.0 7.0 %collective-permute-start.14 = (bf16[144,256]{1,0:T(8,128)(2,1)S(1)}, bf16[144,256]{1,0:T(8,128)(2,1)S(1)}, u32[]{:S(2)}, u32[]{:S(2)}) collective-permute-start(bf16[144,256]{1,0:T(8,128)(2,1)S(1)} %get-tuple-element.55), channel_id=1, source_target_pairs={{0,12},{4,0},{8,4},{12,8},{1,13},{5,1},{9,5},{13,9},{2,14},{6,2},{... | collective-permute-start | bytes 221192 | tf_op jit(solution)/shard_map/ppermute | solution.py:21
  48.1 24.7 %collective-permute-start.21 = (bf16[512,512]{1,0:T(8,128)(2,1)S(1)}, bf16[512,512]{1,0:T(8,128)(2,1)S(1)}, u32[]{:S(2)}, u32[]{:S(2)}) collective-permute-start(bf16[512,512]{1,0:T(8,128)(2,1)S(1)} %copy-done.5), channel_id=1, source_target_pairs={{0,1},{1,0},{2,3},{3,2},{4,5},{5,4},{6,7},{7,6},{8,9},{9,8},{10,11... | collective-permute-start | bytes 1572872 | tf_op jit(solution)/shard_map/ppermute | solution.py:165
  48.1 7.0 %collective-permute-start.15 = (bf16[144,256]{1,0:T(8,128)(2,1)S(1)}, bf16[144,256]{1,0:T(8,128)(2,1)S(1)}, u32[]{:S(2)}, u32[]{:S(2)}) collective-permute-start(bf16[144,256]{1,0:T(8,128)(2,1)S(1)} %get-tuple-element.66), channel_id=1, source_target_pairs={{0,4},{4,8},{8,12},{12,0},{1,5},{5,9},{9,13},{13,1},{2,6},{6,10},{... | collective-permute-start | bytes 221192 | tf_op jit(solution)/shard_map/ppermute | solution.py:21
  49.7 8.0 %collective-permute-start.16 = (bf16[144,256]{1,0:T(8,128)(2,1)S(1)}, bf16[144,256]{1,0:T(8,128)(2,1)S(1)}, u32[]{:S(2)}, u32[]{:S(2)}) collective-permute-start(bf16[144,256]{1,0:T(8,128)(2,1)S(1)} %get-tuple-element.67), channel_id=1, source_target_pairs={{0,8},{4,12},{8,0},{12,4},{1,9},{5,13},{9,1},{13,5},{2,10},{6,14},... | collective-permute-start | bytes 221192 | tf_op jit(solution)/shard_map/ppermute | solution.py:21
  50.7 7.1 %collective-permute-start.17 = (bf16[144,256]{1,0:T(8,128)(2,1)S(1)}, bf16[144,256]{1,0:T(8,128)(2,1)S(1)}, u32[]{:S(2)}, u32[]{:S(2)}) collective-permute-start(bf16[144,256]{1,0:T(8,128)(2,1)S(1)} %get-tuple-element.68), channel_id=1, source_target_pairs={{0,12},{4,0},{8,4},{12,8},{1,13},{5,1},{9,5},{13,9},{2,14},{6,2},{... | collective-permute-start | bytes 221192 | tf_op jit(solution)/shard_map/ppermute | solution.py:21
  59.9 8.7 %collective-permute-start.19 = (bf16[256,128]{1,0:T(8,128)(2,1)S(1)}, bf16[256,128]{1,0:T(8,128)(2,1)S(1)}, u32[]{:S(2)}, u32[]{:S(2)}) collective-permute-start(bf16[256,128]{1,0:T(8,128)(2,1)S(1)} %get-tuple-element.69), channel_id=1, source_target_pairs={{0,8},{4,12},{8,0},{12,4},{1,9},{5,13},{9,1},{13,5},{2,10},{6,14},... | collective-permute-start | bytes 196616 | tf_op jit(solution)/shard_map/ppermute | solution.py:21
  63.2 5.4 %collective-permute-start.18 = (bf16[256,128]{1,0:T(8,128)(2,1)S(1)}, bf16[256,128]{1,0:T(8,128)(2,1)S(1)}, u32[]{:S(2)}, u32[]{:S(2)}) collective-permute-start(bf16[256,128]{1,0:T(8,128)(2,1)S(1)} %get-tuple-element.73), channel_id=1, source_target_pairs={{0,12},{4,0},{8,4},{12,8},{1,13},{5,1},{9,5},{13,9},{2,14},{6,2},{... | collective-permute-start | bytes 196616 | tf_op jit(solution)/shard_map/ppermute | solution.py:21
  66.7 6.1 %collective-permute-start.20 = (bf16[256,128]{1,0:T(8,128)(2,1)S(1)}, bf16[256,128]{1,0:T(8,128)(2,1)S(1)}, u32[]{:S(2)}, u32[]{:S(2)}) collective-permute-start(bf16[256,128]{1,0:T(8,128)(2,1)S(1)} %get-tuple-element.74), channel_id=1, source_target_pairs={{0,4},{4,8},{8,12},{12,0},{1,5},{5,9},{9,13},{13,1},{2,6},{6,10},{... | collective-permute-start | bytes 196616 | tf_op jit(solution)/shard_map/ppermute | solution.py:21
  73.3 6.6 %collective-permute-start.22 = (bf16[128,1024]{1,0:T(8,128)(2,1)S(1)}, bf16[128,1024]{1,0:T(8,128)(2,1)S(1)}, u32[]{:S(2)}, u32[]{:S(2)}) collective-permute-start(bf16[128,1024]{1,0:T(8,128)(2,1)S(1)} %get-tuple-element.77), channel_id=1, source_target_pairs={{0,2},{2,0},{1,3},{3,1},{4,6},{6,4},{5,7},{7,5},{8,10},{10,8},{9,1... | collective-permute-start | bytes 786440 | tf_op jit(solution)/shard_map/ppermute | solution.py:165
  (7 other events, 17.5 us)

commit v4 on v3

--- a/solution.py
+++ b/solution.py
@@ -196,72 +196,121 @@
 EXCLUDED = -1e30
 
 
-def own_kernel(page, wq_o, wq_x, wkv_o, wkv_x, q_out, kv_out, xn):
+def col_group(col, offset):
+    window = 2 * offset
+    return jnp.where(col < offset, 0, 1 + jnp.maximum(col - offset, 0) // window)
+
+
+def attend_part(stacked, keys, values, head_of, scale):
+    rows = head_of.shape[0]
+    s = dot_t(stacked, keys)
+    top = jnp.max(s, axis=-1, keepdims=True)
+    o = dot(jnp.exp2((s - top) * scale).astype(BF16), values)
+    acc, total, highest = None, None, None
+    for h in range(stacked.shape[0] // rows):
+        block = slice(h * rows, (h + 1) * rows)
+        here = (o[block, :LANES], o[block, LANES:], jnp.broadcast_to(top[block], (rows, LANES)))
+        if acc is None:
+            acc, total, highest = here
+        else:
+            acc, total, highest = (
+                jnp.where(head_of == h, new, old) for new, old in zip(here, (acc, total, highest))
+            )
+    return acc, total, highest
+
+
+def merged(first, second, scale):
+    acc_1, total_1, top_1 = first
+    acc_2, total_2, top_2 = second
+    top = jnp.maximum(top_1, top_2)
+    keep_1 = jnp.exp2((top_1 - top) * scale)
+    keep_2 = jnp.exp2((top_2 - top) * scale)
+    return (acc_1 * keep_1 + acc_2 * keep_2) / (total_1 * keep_1 + total_2 * keep_2)
+
+
+def stack_heads(stacked, q, head_of):
+    rows = head_of.shape[0]
+    for h in range(stacked.shape[0] // rows):
+        stacked[h * rows : (h + 1) * rows, :LANES] = jnp.where(head_of == h, q, jnp.zeros_like(q))
+
+
+def window_marks(rows, columns, offset, edge):
+    groups = columns // (2 * offset) + 1
+    lane = lax.broadcasted_iota(jnp.int32, (rows, LANES), 1)
+    group = col_group(lax.broadcasted_iota(jnp.int32, (rows, LANES), 0) % columns, offset)
+    out = jnp.logical_and(lane < groups, lane != group)
+    if edge is not None:
+        out = jnp.logical_or(out, jnp.logical_and(lane == groups, edge))
+    k_marks = jnp.where(out, jnp.full((rows, LANES), EXCLUDED, F32), 0.0).astype(BF16)
+    q_marks = jnp.where(jnp.logical_or(lane == group, lane == groups), 1.0, 0.0).astype(BF16)
+    return q_marks, k_marks
+
+
+def spread(kx, vx, kv, marks):
+    rows = kx.shape[0]
+    hq = kv.shape[1] // 2
+    ones = jnp.ones((rows, LANES), BF16)
+    for g in range(hq // LANES):
+        cols = slice(g * LANES, (g + 1) * LANES)
+        wide = slice(2 * g * LANES, (2 * g + 1) * LANES)
+        extra = slice((2 * g + 1) * LANES, (2 * g + 2) * LANES)
+        kx[:, wide] = kv[:, cols]
+        kx[:, extra] = marks
+        vx[:, wide] = kv[:, hq + g * LANES : hq + (g + 1) * LANES]
+        vx[:, extra] = ones
+
+
+def own_kernel(
+    columns, page, wq_o, wq_x, wkv_o, wkv_x, q_out, acc, total, top, xn, kx, vx, ql
+):
+    rows = page.shape[0]
+    half_rows = rows // 2
+    hq = q_out.shape[1]
     own, other = halves(page.shape[1])
     xn[...] = norm_rows(page)
     q_out[...] = (dot(xn[:, own], wq_o[...]) + dot(xn[:, other], wq_x[...])).astype(BF16)
-    kv_out[...] = (dot(xn[:, own], wkv_o[...]) + dot(xn[:, other], wkv_x[...])).astype(BF16)
-
-
-def col_group(col, offset):
-    window = 2 * offset
-    return jnp.where(col < offset, 0, 1 + jnp.maximum(col - offset, 0) // window)
+    kv = (dot(xn[:, own], wkv_o[...]) + dot(xn[:, other], wkv_x[...])).astype(BF16)
+    offset = half_rows // columns
+    spread(kx, vx, kv, window_marks(rows, columns, offset, None)[1])
+    q_marks = window_marks(half_rows, columns, offset, None)[0]
+    head_of = lane_head((half_rows, LANES), HEAD_ENC)
+    scale = LOG2E / math.sqrt(HEAD_ENC)
+    for h in range(LANES // HEAD_ENC):
+        ql[h * half_rows : (h + 1) * half_rows, LANES:] = q_marks
+    for half in range(2):
+        here = slice(half * half_rows, (half + 1) * half_rows)
+        for g in range(hq // LANES):
+            cols = slice(g * LANES, (g + 1) * LANES)
+            both = slice(2 * g * LANES, (2 * g + 2) * LANES)
+            stack_heads(ql, q_out[here, cols], head_of)
+            state = attend_part(ql[...], kx[here, both], vx[here, both], head_of, scale)
+            acc[here, cols], total[here, cols], top[here, cols] = state
 
 
 def win_kernel(
-    columns, half, q_own, kv_own, halo, wkv_o, wkv_x, wp_o, wp_x, part, xn, kx, vx, ql, wo
+    columns, half, q_own, acc, total, top, halo, wkv_o, wkv_x, wp_o, wp_x, part, xn, kx, vx, ql, wo
 ):
     rows, width = halo.shape
     hq = q_own.shape[1]
-    offset = rows // columns
-    groups = columns // (2 * offset) + 1
     own, other = halves(width)
     xn[...] = norm_rows(halo)
-    kv_halo = (dot(xn[:, own], wkv_o[...]) + dot(xn[:, other], wkv_x[...])).astype(BF16)
-    kv_here = kv_own[half * rows : (half + 1) * rows, :]
-
+    kv = (dot(xn[:, own], wkv_o[...]) + dot(xn[:, other], wkv_x[...])).astype(BF16)
     tile = lax.axis_index("tile")
     edge = tile == (0 if half == 0 else lax.axis_size("tile") - 1)
-    lane = lax.broadcasted_iota(jnp.int32, (rows, LANES), 1)
-    group = col_group(lax.broadcasted_iota(jnp.int32, (rows, LANES), 0) % columns, offset)
-    unlike = jnp.logical_and(lane < groups, lane != group)
-    cut = jnp.logical_and(lane == groups, edge)
-    off = jnp.full((rows, LANES), EXCLUDED, F32)
-    here_marks = jnp.where(unlike, off, 0.0).astype(BF16)
-    halo_marks = jnp.where(jnp.logical_or(unlike, cut), off, 0.0).astype(BF16)
-    q_marks = jnp.where(jnp.logical_or(lane == group, lane == groups), 1.0, 0.0).astype(BF16)
-    ones = jnp.ones((2 * rows, LANES), BF16)
-    heads = LANES // HEAD_ENC
-    for h in range(heads):
+    q_marks, k_marks = window_marks(rows, columns, rows // columns, edge)
+    spread(kx, vx, kv, k_marks)
+    head_of = lane_head((rows, LANES), HEAD_ENC)
+    scale = LOG2E / math.sqrt(HEAD_ENC)
+    for h in range(LANES // HEAD_ENC):
         ql[h * rows : (h + 1) * rows, LANES:] = q_marks
+    here = slice(half * rows, (half + 1) * rows)
     for g in range(hq // LANES):
-        k_cols = slice(g * LANES, (g + 1) * LANES)
-        v_cols = slice(hq + g * LANES, hq + (g + 1) * LANES)
-        wide = slice(2 * g * LANES, (2 * g + 1) * LANES)
-        extra = slice((2 * g + 1) * LANES, (2 * g + 2) * LANES)
-        kx[:rows, wide] = kv_here[:, k_cols]
-        kx[rows:, wide] = kv_halo[:, k_cols]
-        kx[:rows, extra] = here_marks
-        kx[rows:, extra] = halo_marks
-        vx[:rows, wide] = kv_here[:, v_cols]
-        vx[rows:, wide] = kv_halo[:, v_cols]
-        vx[:, extra] = ones
-    scale = LOG2E / math.sqrt(HEAD_ENC)
-    q_head = lane // HEAD_ENC
-    for g in range(hq // LANES):
-        q = q_own[half * rows : (half + 1) * rows, g * LANES : (g + 1) * LANES]
+        cols = slice(g * LANES, (g + 1) * LANES)
         both = slice(2 * g * LANES, (2 * g + 2) * LANES)
-        for h in range(heads):
-            ql[h * rows : (h + 1) * rows, :LANES] = jnp.where(q_head == h, q, jnp.zeros_like(q))
-        s = dot_t(ql[...], kx[:, both])
-        e = jnp.exp2((s - jnp.max(s, axis=-1, keepdims=True)) * scale).astype(BF16)
-        o = dot(e, vx[:, both])
-        acc = None
-        for h in range(heads):
-            block = slice(h * rows, (h + 1) * rows)
-            one = o[block, :LANES] / o[block, LANES:]
-            acc = one if acc is None else jnp.where(q_head == h, one, acc)
-        wo[:, g * LANES : (g + 1) * LANES] = acc.astype(BF16)
+        stack_heads(ql, q_own[here, cols], head_of)
+        state = attend_part(ql[...], kx[:, both], vx[:, both], head_of, scale)
+        first = (acc[here, cols], total[here, cols], top[here, cols])
+        wo[:, cols] = merged(first, state, scale).astype(BF16)
     part[:, own] = dot(wo[...], wp_o[...]).astype(BF16)
     part[:, other] = dot(wo[...], wp_x[...]).astype(BF16)
 
@@ -296,54 +345,77 @@
     pieces(qs, 0, outs, 0)
 
 
-def cross_kernel(count, strips, *refs):
-    q_in = refs[:count]
-    kv_in = refs[count : count + strips]
-    outs = refs[count + strips : 2 * count + strips]
-    kv, ql, sem = refs[2 * count + strips :]
+def load_strips(kv_in, kv, sem):
     rows = kv_in[0].shape[0]
     copies = [
         pltpu.make_async_copy(
-            kv_in[s], kv.at[pl.ds(s * rows, rows), pl.ds(0, 2 * LANES)], sem.at[s]
+            strip, kv.at[pl.ds(s * rows, rows), pl.ds(0, 2 * LANES)], sem.at[s]
         )
-        for s in range(strips)
+        for s, strip in enumerate(kv_in)
     ]
     for copy in copies:
         copy.start()
     kv[:, 2 * LANES :] = jnp.ones((kv.shape[0], LANES), BF16)
-    tokens = q_in[0].shape[0]
-    q_head = lane_head(q_in[0].shape, HEAD_DEC)
-    scale = LOG2E / math.sqrt(HEAD_DEC)
     for copy in copies:
         copy.wait()
-    for s in range(count):
-        q = q_in[s][...]
-        for h in range(LANES // HEAD_DEC):
-            ql[h * tokens : (h + 1) * tokens] = jnp.where(q_head == h, q, jnp.zeros_like(q))
-        sc = dot_t(ql[...], kv[:, :LANES])
-        e = jnp.exp2((sc - jnp.max(sc, axis=-1, keepdims=True)) * scale).astype(BF16)
-        o = dot(e, kv[:, LANES:])
-        o = o[:, :LANES] / o[:, LANES:]
-        outs[s][...] = jnp.where(q_head == 0, o[:tokens], o[tokens:]).astype(BF16)
-
-
-def out_kernel(tiles, *refs):
-    ctx_in = refs[:tiles]
-    wo_o, wo_x, text, keep, send, ctx, acc = refs[tiles:]
-    tokens = ctx.shape[0]
-    own, other = halves(acc.shape[1])
-    tile = lax.axis_index("tile")
+
+
+def cross_first_kernel(tiles, *refs):
+    q_in = refs[:tiles]
+    kv_in = refs[tiles : 2 * tiles]
+    acc, total, top, kv, ql, sem = refs[2 * tiles :]
+    load_strips(kv_in, kv, sem)
+    tokens = q_in[0].shape[0]
+    head_of = lane_head(q_in[0].shape, HEAD_DEC)
+    scale = LOG2E / math.sqrt(HEAD_DEC)
     for s in range(tiles):
-        start = pl.multiple_of(lax.rem(tile + s, tiles) * LANES, LANES)
-        ctx[:, pl.ds(start, LANES)] = ctx_in[s][...]
-    acc[:, own] = dot(ctx[...], wo_o[...])
-    acc[:, other] = dot(ctx[...], wo_x[...])
+        here = slice(s * tokens, (s + 1) * tokens)
+        stack_heads(ql, q_in[s][...], head_of)
+        state = attend_part(ql[...], kv[:, :LANES], kv[:, LANES:], head_of, scale)
+        acc[here], total[here], top[here] = state
+
+
+def cross_kernel(first, count, tiles, *refs):
+    q_in = refs[:count]
+    kv_in = refs[count : count + tiles]
+    acc, total, top, keep, send, kv, ql, ctx, sem = refs[count + tiles :]
+    load_strips(kv_in, kv, sem)
+    tokens = q_in[0].shape[0]
+    head_of = lane_head(q_in[0].shape, HEAD_DEC)
+    scale = LOG2E / math.sqrt(HEAD_DEC)
     half = tokens // 2
     m = lax.axis_index("mp")
     own_rows = pl.ds(pl.multiple_of(m * half, half), half)
     send_rows = pl.ds(pl.multiple_of((1 - m) * half, half), half)
-    keep[...] = text[own_rows, :].astype(F32) + acc[own_rows, :]
-    send[...] = acc[send_rows, :].astype(BF16)
+    for s in range(count):
+        here = slice((first + s) * tokens, (first + s + 1) * tokens)
+        stack_heads(ql, q_in[s][...], head_of)
+        state = attend_part(ql[...], kv[:, :LANES], kv[:, LANES:], head_of, scale)
+        ctx[...] = merged((acc[here], total[here], top[here]), state, scale).astype(BF16)
+        keep[s * half : (s + 1) * half] = ctx[own_rows, :]
+        send[s * half : (s + 1) * half] = ctx[send_rows, :]
+
+
+def out_kernel(tiles, *refs):
+    ctx_in = refs[:tiles]
+    w_own, w_batch, w_mp, w_both, text, decoded, ctx = refs[tiles:]
+    half = decoded.shape[0]
+    width = decoded.shape[1]
+    own, other = halves(width)
+    tile = lax.axis_index("tile")
+    m = lax.axis_index("mp")
+    own_rows = pl.ds(pl.multiple_of(m * half, half), half)
+    for s in range(tiles):
+        start = lax.rem(tile + s, tiles) * LANES
+        here = pl.ds(pl.multiple_of(start, LANES), LANES)
+        there = pl.ds(pl.multiple_of(tiles * LANES + start, LANES), LANES)
+        ctx[:, here] = ctx_in[s][:half]
+        ctx[:, there] = ctx_in[s][half:]
+    mine = ctx[:, : tiles * LANES]
+    theirs = ctx[:, tiles * LANES :]
+    for cols, first, second in ((own, w_own, w_mp), (other, w_batch, w_both)):
+        mixed = dot(mine, first[...]) + dot(theirs, second[...])
+        decoded[:, cols] = (text[own_rows, cols].astype(F32) + mixed).astype(BF16)
 
 
 VM = pl.BlockSpec(memory_space=pltpu.VMEM)
@@ -399,11 +471,16 @@
     wq_x = swapped(enc_query, "batch")
     dq_x = swapped(dec_query, "batch")
 
-    q_own, kv_own = call(
-        own_kernel,
+    q_own, *win_state = call(
+        functools.partial(own_kernel, columns),
         1,
-        [((rows, hq_enc), BF16), ((rows, 2 * hq_enc), BF16)],
-        [pltpu.VMEM((rows, width), BF16)],
+        [((rows, hq_enc), BF16)] + [((rows, hq_enc), F32)] * 3,
+        [
+            pltpu.VMEM((rows, width), BF16),
+            pltpu.VMEM((rows, 2 * hq_enc), BF16),
+            pltpu.VMEM((rows, 2 * hq_enc), BF16),
+            pltpu.VMEM((LANES // HEAD_ENC * half_rows, 2 * LANES), BF16),
+        ],
         page,
         enc_query,
         wq_x,
@@ -422,7 +499,7 @@
     q_in = [q_out[0]] + [from_behind(q_out[s], "tile", s) for s in range(1, tiles)]
 
     wp_x = swapped(enc_proj, "batch")
-    above, below, *q_in = lax.optimization_barrier((above, below, *q_in))
+    above, below = lax.optimization_barrier((above, below, *q_out))[:2]
 
     def window_half(half, halo):
         (part,) = call(
@@ -431,13 +508,13 @@
             [((half_rows, width), BF16)],
             [
                 pltpu.VMEM((half_rows, width), BF16),
-                pltpu.VMEM((rows, 2 * hq_enc), BF16),
-                pltpu.VMEM((rows, 2 * hq_enc), BF16),
+                pltpu.VMEM((half_rows, 2 * hq_enc), BF16),
+                pltpu.VMEM((half_rows, 2 * hq_enc), BF16),
                 pltpu.VMEM((LANES // HEAD_ENC * half_rows, 2 * LANES), BF16),
                 pltpu.VMEM((half_rows, hq_enc), BF16),
             ],
             q_own,
-            kv_own,
+            *win_state,
             halo,
             wkv_enc,
             wkv_x,
@@ -466,49 +543,72 @@
     part_b = window_half(1, after(below, part_a))
     theirs_b = swapped(part_b, "mp")
     encoded_a, *kv_a = key_values(0, part_a, theirs_a)
+    kv_a, q_in = lax.optimization_barrier((list(kv_a), q_in))
     kv_a = [kv_a[0]] + [from_behind(kv_a[s], "tile", s) for s in range(1, tiles)]
     theirs_b, *kv_a = lax.optimization_barrier((theirs_b, *kv_a))
     encoded_b, *kv_b = key_values(1, part_b, theirs_b)
     kv_b = [kv_b[0]] + [from_behind(kv_b[s], "tile", s) for s in range(1, tiles)]
-    do_x = swapped(after(dec_out, encoded_b), "batch")
+    out_half = after(dec_out, encoded_b)
+    do_x = swapped(out_half, "batch")
+    do_m = swapped(out_half, "mp")
+    do_mx = swapped(do_m, "batch")
     encoded = jnp.concatenate([encoded_a, encoded_b], axis=0)
 
-    def attend(queries, *earlier):
+    cross_scratch = [
+        pltpu.VMEM((tiles * half_rows, 3 * LANES), BF16),
+        pltpu.VMEM((LANES // HEAD_DEC * tokens, LANES), BF16),
+    ]
+    arrivals = pltpu.SemaphoreType.DMA((tiles,))
+    cross_state = call(
+        functools.partial(cross_first_kernel, tiles),
+        1,
+        [((tiles * tokens, LANES), F32)] * 3,
+        cross_scratch + [arrivals],
+        *q_in,
+        *kv_a,
+        specs=[VM] * tiles + [ANY] * tiles,
+    )
+
+    def attend(first, queries):
         count = len(queries)
         return call(
-            functools.partial(cross_kernel, count, 2 * tiles),
+            functools.partial(cross_kernel, first, count, tiles),
             1,
-            [((tokens, LANES), BF16)] * count,
-            [
-                pltpu.VMEM((tiles * rows, 3 * LANES), BF16),
-                pltpu.VMEM((LANES // HEAD_DEC * tokens, LANES), BF16),
-                pltpu.SemaphoreType.DMA((2 * tiles,)),
-            ],
+            [((count * tokens // 2, LANES), BF16)] * 2,
+            cross_scratch + [pltpu.VMEM((tokens, LANES), BF16), arrivals],
             *queries,
-            *kv_a,
             *kv_b,
-            specs=[VM] * count + [ANY] * (2 * tiles),
+            *cross_state,
+            specs=[VM] * count + [ANY] * tiles + [VM] * 3,
         )
 
+    def joined(keep, other, index):
+        span = slice(index * tokens // 2, (index + 1) * tokens // 2)
+        return jnp.concatenate([keep[span], other[span]], axis=0)
+
     near = tiles // 2
-    ctx_far = attend(q_in[near:])
-    ctx_far_in = [from_behind(ctx_far[s - near], "tile", -s) for s in range(near, tiles)]
-    ctx_near = attend([after(q_in[0], ctx_far[0]), *q_in[1:near]])
-    ctx_in = [ctx_near[0]] + [from_behind(ctx_near[s], "tile", -s) for s in range(1, near)]
-    ctx_in += ctx_far_in
-
-    keep, send = call(
+    keep_far, send_far = attend(near, q_in[near:])
+    other_far = swapped(send_far, "mp")
+    keep_near, send_near = attend(0, [after(q_in[0], keep_far), *q_in[1:near]])
+    other_near = swapped(send_near, "mp")
+    ctx_in = [joined(keep_near, other_near, 0)]
+    for s in range(1, near):
+        ctx_in.append(from_behind(joined(keep_near, other_near, s), "tile", -s))
+    for s in range(near, tiles):
+        ctx_in.append(from_behind(joined(keep_far, other_far, s - near), "tile", -s))
+
+    (decoded,) = call(
         functools.partial(out_kernel, tiles),
         2 * tokens * hq_dec * width,
-        [((tokens // 2, width), F32), ((tokens // 2, width), BF16)],
-        [pltpu.VMEM((tokens, hq_dec), BF16), pltpu.VMEM((tokens, width), F32)],
+        [((tokens // 2, width), BF16)],
+        [pltpu.VMEM((tokens // 2, 2 * hq_dec), BF16)],
         *ctx_in,
         dec_out,
         do_x,
+        do_m,
+        do_mx,
         text,
     )
-    received = swapped(send, "mp")
-    decoded = (keep + received.astype(F32)).astype(BF16)
     return (
         encoded.reshape(page_cells.shape),
         decoded.reshape(1, tokens // 2, width),

time: 80.9 us -> 75.1 us (0.928)
  waiting for transfers between devices: 30.7 us -> 23.2 us
  Pallas kernels: 14.3 us -> 16.6 us
    ppermute x12, waiting for transfers between devices: 20.4 us -> 13.6 us  [from_behind(): lax.ppermute(value, axis, [(i, (i + by) % devices) for i in range(devices)])]
    ppermute x9 -> x12, waiting for transfers between devices: 10.3 us -> 5.75 us  [swapped(): return lax.ppermute(value, axis, [(0, 1), (1, 0)])]
    ppermute x1, waiting for transfers between devices: 0.01 us -> 3.87 us  [body(): below = lax.ppermute(upper, 'tile', down)]
    pallas_call x9 -> x10, Pallas kernels: 14.3 us -> 16.6 us  [call(): pl.pallas_call(kernel, out_shape=[jax.ShapeDtypeStruct(shape, dtype) for...]
    ppermute x9 -> x12, starting transfers between devices: 4.89 us -> 7.05 us  [swapped(): return lax.ppermute(value, axis, [(0, 1), (1, 0)])]
    ppermute x12, starting transfers between devices: 19.1 us -> 17.2 us  [from_behind(): lax.ppermute(value, axis, [(i, (i + by) % devices) for i in range(devices)])]
  transfers between devices with their start and end apart: 23 -> 26, of which waited for: 11 -> 11; matrix products, arithmetic and copies ran while one was open for 3% -> 3% of each run, Pallas kernels for 13% -> 17%
where the time goes in v4:
time: 75.1 us; the launch traced here: 74.9 us
  starting transfers between devices  30.4 us (40%)
  waiting for transfers between devices  23.2 us (31%)
  Pallas kernels  16.6 us (22%)
  local copies, waits for them, and re-layouts  2.81 us (4%)
  between operations  0.93 us (1%)
  other arithmetic  0.88 us (1%)
    ppermute x12, starting transfers between devices, from_behind(): lax.ppermute(value, axis, [(i, (i + by) % devices) for i in range(devices)])  17.2 us
    pallas_call x10, Pallas kernels, call(): pl.pallas_call(kernel, out_shape=[jax.ShapeDtypeStruct(shape, dtype) for...  16.6 us
    ppermute x12, waiting for transfers between devices, from_behind(): lax.ppermute(value, axis, [(i, (i + by) % devices) for i in range(devices)])  13.6 us
    ppermute x12, starting transfers between devices, swapped(): return lax.ppermute(value, axis, [(0, 1), (1, 0)])  7.05 us
    ppermute x12, waiting for transfers between devices, swapped(): return lax.ppermute(value, axis, [(0, 1), (1, 0)])  5.75 us
    ppermute x1, starting transfers between devices, body(): above = lax.ppermute(lower, 'tile', up)  4.93 us
    ppermute x1, waiting for transfers between devices, body(): below = lax.ppermute(upper, 'tile', down)  3.87 us
    unnamed x19, local copies, waits for them, and re-layouts  1.7 us
  transfers between devices with their start and end apart: 26, of which 11 were waited for; matrix products, arithmetic and copies ran while one was open for 3% of the time, Pallas kernels for 17%

profile of v4, /device:TPU:0, one launch (start us, length us, event | category | flops | bytes accessed | tf_op | source)
XLA Modules:
  0.0 74.9 jit_solution(10059337371836864185)
XLA Ops:
  2.8 4.9 %collective-permute-start.2 = (bf16[144,1024]{1,0:T(8,128)(2,1)S(1)}, bf16[144,1024]{1,0:T(8,128)(2,1)S(1)}, u32[]{:S(2)}, u32[]{:S(2)}) collective-permute-start(bf16[144,1024]{1,0:T(8,128)(2,1)S(1)} %bitcast.31), channel_id=1, source_target_pairs={{0,4},{4,8},{8,12},{1,5},{5,9},{9,13},{2,6},{6,10},{10,14},{3,7},{... | collective-permute-start | bytes 884744 | tf_op jit(solution)/shard_map/ppermute | solution.py:467
  10.6 3.1 %shard_map.95 = (bf16[288,512]{1,0:T(8,128)(2,1)S(1)}, f32[288,512]{1,0:T(8,128)S(1)}, f32[288,512]{1,0:T(8,128)S(1)}, f32[288,512]{1,0:T(8,128)S(1)}) custom-call(bf16[288,1024]{1,0:T(8,128)(2,1)S(1)} %bitcast.21, bf16[512,512]{1,0:T(8,128)(2,1)S(1)} %copy-done.3, bf16[512,512]{1,0:T(8,128)(2,1)S(1)} %collective-permute-done.wq_x, ...), custom_call_target="tpu_custom_call" | custom-call | flops 1 | bytes 4915200 | tf_op jit(solution)/shard_map/pallas_call | solution.py:427
  14.5 3.9 %collective-permute-done.3.halo = bf16[144,1024]{1,0:T(8,128)(2,1)S(1)} collective-permute-done((bf16[144,1024]{1,0:T(8,128)(2,1)S(1)}, bf16[144,1024]{1,0:T(8,128)(2,1)S(1)}, u32[]{:S(2)}, u32[]{:S(2)}) %collective-permute-start.3) | collective-permute-done | bytes 294944 | tf_op jit(solution)/shard_map/ppermute | solution.py:468
  18.4 2.0 %shard_map.97.mine = bf16[144,1024]{1,0:T(8,128)(2,1)S(1)} custom-call(bf16[288,512]{1,0:T(8,128)(2,1)S(1)} %get-tuple-element.47.q_own, f32[288,512]{1,0:T(8,128)S(1)} %get-tuple-element.48.acc, f32[288,512]{1,0:T(8,128)S(1)} %get-tuple-element.49.total, f32[288,512]{1,0:T(8,128)S(1)} %get-tuple-element.50.top, ...), custom_call_target="tpu_custom_call" | custom-call | flops 1132462080 | bytes 4915200 | tf_op jit(solution)/shard_map/pallas_call | solution.py:427
  20.7 1.6 %collective-permute-start.6 = (bf16[144,1024]{1,0:T(8,128)(2,1)S(1)}, bf16[144,1024]{1,0:T(8,128)(2,1)S(1)}, u32[]{:S(2)}, u32[]{:S(2)}) collective-permute-start(bf16[144,1024]{1,0:T(8,128)(2,1)S(1)} %shard_map.97.mine), channel_id=1, source_target_pairs={{0,2},{2,0},{1,3},{3,1},{4,6},{6,4},{5,7},{7,5},{8,10},{10,8},{9,1... | collective-permute-start | bytes 884744 | tf_op jit(solution)/shard_map/ppermute | solution.py:165
  22.3 2.0 %shard_map.99.mine = bf16[144,1024]{1,0:T(8,128)(2,1)S(1)} custom-call(bf16[288,512]{1,0:T(8,128)(2,1)S(1)} %get-tuple-element.47.q_own, f32[288,512]{1,0:T(8,128)S(1)} %get-tuple-element.48.acc, f32[288,512]{1,0:T(8,128)S(1)} %get-tuple-element.49.total, f32[288,512]{1,0:T(8,128)S(1)} %get-tuple-element.50.top, ...), custom_call_target="tpu_custom_call" | custom-call | flops 1132462080 | bytes 4915200 | tf_op jit(solution)/shard_map/pallas_call | solution.py:427
  24.9 1.6 %collective-permute-start.9 = (bf16[256,128]{1,0:T(8,128)(2,1)S(1)}, bf16[256,128]{1,0:T(8,128)(2,1)S(1)}, u32[]{:S(2)}, u32[]{:S(2)}) collective-permute-start(bf16[256,128]{1,0:T(8,128)(2,1)S(1)} %get-tuple-element.53), channel_id=1, source_target_pairs={{0,4},{4,8},{8,12},{12,0},{1,5},{5,9},{9,13},{13,1},{2,6},{6,10},{... | collective-permute-start | bytes 196616 | tf_op jit(solution)/shard_map/ppermute | solution.py:21
  27.5 3.1 %collective-permute-done.6.theirs = bf16[144,1024]{1,0:T(8,128)(2,1)S(1)} collective-permute-done((bf16[144,1024]{1,0:T(8,128)(2,1)S(1)}, bf16[144,1024]{1,0:T(8,128)(2,1)S(1)}, u32[]{:S(2)}, u32[]{:S(2)}) %collective-permute-start.6) | collective-permute-done | bytes 294944 | tf_op jit(solution)/shard_map/ppermute | solution.py:165
  30.6 1.6 %collective-permute-start.11 = (bf16[256,128]{1,0:T(8,128)(2,1)S(1)}, bf16[256,128]{1,0:T(8,128)(2,1)S(1)}, u32[]{:S(2)}, u32[]{:S(2)}) collective-permute-start(bf16[256,128]{1,0:T(8,128)(2,1)S(1)} %get-tuple-element.55), channel_id=1, source_target_pairs={{0,12},{4,0},{8,4},{12,8},{1,13},{5,1},{9,5},{13,9},{2,14},{6,2},{... | collective-permute-start | bytes 196616 | tf_op jit(solution)/shard_map/ppermute | solution.py:21
  34.9 1.6 %collective-permute-start.12 = (bf16[144,256]{1,0:T(8,128)(2,1)S(1)}, bf16[144,256]{1,0:T(8,128)(2,1)S(1)}, u32[]{:S(2)}, u32[]{:S(2)}) collective-permute-start(bf16[144,256]{1,0:T(8,128)(2,1)S(1)} %get-tuple-element.66), channel_id=1, source_target_pairs={{0,4},{4,8},{8,12},{12,0},{1,5},{5,9},{9,13},{13,1},{2,6},{6,10},{... | collective-permute-start | bytes 221192 | tf_op jit(solution)/shard_map/ppermute | solution.py:21
  36.4 2.4 %collective-permute-start.13 = (bf16[144,256]{1,0:T(8,128)(2,1)S(1)}, bf16[144,256]{1,0:T(8,128)(2,1)S(1)}, u32[]{:S(2)}, u32[]{:S(2)}) collective-permute-start(bf16[144,256]{1,0:T(8,128)(2,1)S(1)} %get-tuple-element.67), channel_id=1, source_target_pairs={{0,8},{4,12},{8,0},{12,4},{1,9},{5,13},{9,1},{13,5},{2,10},{6,14},... | collective-permute-start | bytes 221192 | tf_op jit(solution)/shard_map/ppermute | solution.py:21
  38.8 1.6 %collective-permute-start.14 = (bf16[144,256]{1,0:T(8,128)(2,1)S(1)}, bf16[144,256]{1,0:T(8,128)(2,1)S(1)}, u32[]{:S(2)}, u32[]{:S(2)}) collective-permute-start(bf16[144,256]{1,0:T(8,128)(2,1)S(1)} %get-tuple-element.68), channel_id=1, source_target_pairs={{0,12},{4,0},{8,4},{12,8},{1,13},{5,1},{9,5},{13,9},{2,14},{6,2},{... | collective-permute-start | bytes 221192 | tf_op jit(solution)/shard_map/ppermute | solution.py:21
  41.6 2.1 %collective-permute-done.13.refs_6_ = bf16[144,256]{1,0:T(8,128)(2,1)S(1)} collective-permute-done((bf16[144,256]{1,0:T(8,128)(2,1)S(1)}, bf16[144,256]{1,0:T(8,128)(2,1)S(1)}, u32[]{:S(2)}, u32[]{:S(2)}) %collective-permute-start.13) | collective-permute-done | bytes 73760 | tf_op jit(solution)/shard_map/ppermute | solution.py:21
  44.6 1.6 %collective-permute-start.24 = (bf16[512,512]{1,0:T(8,128)(2,1)S(1)}, bf16[512,512]{1,0:T(8,128)(2,1)S(1)}, u32[]{:S(2)}, u32[]{:S(2)}) collective-permute-start(bf16[512,512]{1,0:T(8,128)(2,1)S(1)} %copy-done.5), channel_id=1, source_target_pairs={{0,2},{2,0},{1,3},{3,1},{4,6},{6,4},{5,7},{7,5},{8,10},{10,8},{9,1... | collective-permute-start | bytes 1572872 | tf_op jit(solution)/shard_map/ppermute | solution.py:165
  47.4 2.2 %collective-permute-start.16 = (bf16[144,256]{1,0:T(8,128)(2,1)S(1)}, bf16[144,256]{1,0:T(8,128)(2,1)S(1)}, u32[]{:S(2)}, u32[]{:S(2)}) collective-permute-start(bf16[144,256]{1,0:T(8,128)(2,1)S(1)} %get-tuple-element.76), channel_id=1, source_target_pairs={{0,8},{4,12},{8,0},{12,4},{1,9},{5,13},{9,1},{13,5},{2,10},{6,14},... | collective-permute-start | bytes 221192 | tf_op jit(solution)/shard_map/ppermute | solution.py:21
  50.0 2.7 %shard_map.101 = (f32[1024,128]{1,0:T(8,128)S(1)}, f32[1024,128]{1,0:T(8,128)S(1)}, f32[1024,128]{1,0:T(8,128)S(1)}) custom-call(bf16[256,128]{1,0:T(8,128)(2,1)S(1)} %get-tuple-element.87.refs_0_, bf16[256,128]{1,0:T(8,128)(2,1)S(1)} %collective-permute-done.9.refs_1_, bf16[256,128]{1,0:T(8,128)(2,1)S(1)} %collective-permute-done.10.refs_2_.refs_0_, ...), custom_call_target="tpu_custom_call" | custom-call | flops 1 | bytes 1343488 | tf_op jit(solution)/shard_map/pallas_call | solution.py:427
  53.5 2.0 %collective-permute-done.16.refs_4_ = bf16[144,256]{1,0:T(8,128)(2,1)S(1)} collective-permute-done((bf16[144,256]{1,0:T(8,128)(2,1)S(1)}, bf16[144,256]{1,0:T(8,128)(2,1)S(1)}, u32[]{:S(2)}, u32[]{:S(2)}) %collective-permute-start.16) | collective-permute-done | bytes 73760 | tf_op jit(solution)/shard_map/ppermute | solution.py:21
  55.6 1.6 %shard_map.102 = (bf16[256,128]{1,0:T(8,128)(2,1)S(1)}, bf16[256,128]{1,0:T(8,128)(2,1)S(1)}) custom-call(bf16[256,128]{1,0:T(8,128)(2,1)S(1)} %collective-permute-done.10.refs_2_.refs_0_, bf16[256,128]{1,0:T(8,128)(2,1)S(1)} %collective-permute-done.11.refs_3_.refs_1_, bf16[144,256]{1,0:T(8,128)(2,1)S(1)} %get-tuple-element.74.refs_2_, ...), custom_call_target="tpu_custom_call" | custom-call | flops 1 | bytes 1343488 | tf_op jit(solution)/shard_map/pallas_call | solution.py:427
  57.2 1.6 %shard_map.103 = (bf16[256,128]{1,0:T(8,128)(2,1)S(1)}, bf16[256,128]{1,0:T(8,128)(2,1)S(1)}) custom-call(bf16[256,128]{1,0:T(8,128)(2,1)S(1)} %get-tuple-element.87.refs_0_, bf16[256,128]{1,0:T(8,128)(2,1)S(1)} %collective-permute-done.9.refs_1_, bf16[144,256]{1,0:T(8,128)(2,1)S(1)} %get-tuple-element.74.refs_2_, ...), custom_call_target="tpu_custom_call" | custom-call | flops 1 | bytes 1343488 | tf_op jit(solution)/shard_map/pallas_call | solution.py:427
  59.5 1.5 %collective-permute-start.20 = (bf16[256,128]{1,0:T(8,128)(2,1)S(1)}, bf16[256,128]{1,0:T(8,128)(2,1)S(1)}, u32[]{:S(2)}, u32[]{:S(2)}) collective-permute-start(bf16[256,128]{1,0:T(8,128)(2,1)S(1)} %get-tuple-element.90), channel_id=1, source_target_pairs={{0,2},{2,0},{1,3},{3,1},{4,6},{6,4},{5,7},{7,5},{8,10},{10,8},{9,1... | collective-permute-start | bytes 196616 | tf_op jit(solution)/shard_map/ppermute | solution.py:165
  61.0 2.6 %collective-permute-done.18 = bf16[256,128]{1,0:T(8,128)(2,1)S(1)} collective-permute-done((bf16[256,128]{1,0:T(8,128)(2,1)S(1)}, bf16[256,128]{1,0:T(8,128)(2,1)S(1)}, u32[]{:S(2)}, u32[]{:S(2)}) %collective-permute-start.18) | collective-permute-done | bytes 65568 | tf_op jit(solution)/shard_map/ppermute | solution.py:165
  63.6 2.2 %collective-permute-start.19 = (bf16[256,128]{1,0:T(8,128)(2,1)S(1)}, bf16[256,128]{1,0:T(8,128)(2,1)S(1)}, u32[]{:S(2)}, u32[]{:S(2)}) collective-permute-start(bf16[256,128]{1,0:T(8,128)(2,1)S(1)} %pad_maximum_fusion.2), channel_id=1, source_target_pairs={{0,12},{4,0},{8,4},{12,8},{1,13},{5,1},{9,5},{13,9},{2,14},{6,2},{... | collective-permute-start | bytes 196616 | tf_op jit(solution)/shard_map/ppermute | solution.py:21
  65.9 1.5 %collective-permute-start.21 = (bf16[256,128]{1,0:T(8,128)(2,1)S(1)}, bf16[256,128]{1,0:T(8,128)(2,1)S(1)}, u32[]{:S(2)}, u32[]{:S(2)}) collective-permute-start(bf16[256,128]{1,0:T(8,128)(2,1)S(1)} %pad_maximum_fusion.3), channel_id=1, source_target_pairs={{0,8},{4,12},{8,0},{12,4},{1,9},{5,13},{9,1},{13,5},{2,10},{6,14},... | collective-permute-start | bytes 196616 | tf_op jit(solution)/shard_map/ppermute | solution.py:21
  68.0 5.7 %collective-permute-done.21.refs_2_ = bf16[256,128]{1,0:T(8,128)(2,1)S(1)} collective-permute-done((bf16[256,128]{1,0:T(8,128)(2,1)S(1)}, bf16[256,128]{1,0:T(8,128)(2,1)S(1)}, u32[]{:S(2)}, u32[]{:S(2)}) %collective-permute-start.21) | collective-permute-done | bytes 65568 | tf_op jit(solution)/shard_map/ppermute | solution.py:21
  (67 shorter events, 17.5 us)
Async XLA Ops:
  0.6 7.1 %collective-permute-start.1 = (bf16[512,2,512]{2,1,0:T(2,128)(2,1)}, bf16[512,2,512]{2,1,0:T(2,128)(2,1)S(1)}, u32[]{:S(2)}, u32[]{:S(2)}) collective-permute-start(bf16[512,2,512]{2,1,0:T(2,128)(2,1)} %param.11), channel_id=1, source_target_pairs={{0,1},{1,0},{2,3},{3,2},{4,5},{5,4},{6,7},{7,6},{8,9},{9,8},{10,11... | collective-permute-start | bytes 3145736 | tf_op jit(solution)/shard_map/ppermute | solution.py:165
  1.2 8.5 %collective-permute-start = (bf16[512,512]{1,0:T(8,128)(2,1)}, bf16[512,512]{1,0:T(8,128)(2,1)S(1)}, u32[]{:S(2)}, u32[]{:S(2)}) collective-permute-start(bf16[512,512]{1,0:T(8,128)(2,1)} %wq_o.2), channel_id=1, source_target_pairs={{0,1},{1,0},{2,3},{3,2},{4,5},{5,4},{6,7},{7,6},{8,9},{9,8},{10,11... | collective-permute-start | bytes 1572872 | tf_op jit(solution)/shard_map/ppermute | solution.py:165
  1.2 12.4 %collective-permute-start.4 = (bf16[512,512]{1,0:T(8,128)(2,1)}, bf16[512,512]{1,0:T(8,128)(2,1)S(1)}, u32[]{:S(2)}, u32[]{:S(2)}) collective-permute-start(bf16[512,512]{1,0:T(8,128)(2,1)} %wq_o.3), channel_id=1, source_target_pairs={{0,1},{1,0},{2,3},{3,2},{4,5},{5,4},{6,7},{7,6},{8,9},{9,8},{10,11... | collective-permute-start | bytes 1572872 | tf_op jit(solution)/shard_map/ppermute | solution.py:165
  1.7 16.7 %collective-permute-start.5 = (bf16[512,512]{1,0:T(8,128)(2,1)}, bf16[512,512]{1,0:T(8,128)(2,1)S(1)}, u32[]{:S(2)}, u32[]{:S(2)}) collective-permute-start(bf16[512,512]{1,0:T(8,128)(2,1)} %wp_o.3), channel_id=1, source_target_pairs={{0,1},{1,0},{2,3},{3,2},{4,5},{5,4},{6,7},{7,6},{8,9},{9,8},{10,11... | collective-permute-start | bytes 1572872 | tf_op jit(solution)/shard_map/ppermute | solution.py:165
  2.8 11.7 %collective-permute-start.2 = (bf16[144,1024]{1,0:T(8,128)(2,1)S(1)}, bf16[144,1024]{1,0:T(8,128)(2,1)S(1)}, u32[]{:S(2)}, u32[]{:S(2)}) collective-permute-start(bf16[144,1024]{1,0:T(8,128)(2,1)S(1)} %bitcast.31), channel_id=1, source_target_pairs={{0,4},{4,8},{8,12},{1,5},{5,9},{9,13},{2,6},{6,10},{10,14},{3,7},{... | collective-permute-start | bytes 884744 | tf_op jit(solution)/shard_map/ppermute | solution.py:467
  7.8 10.6 %collective-permute-start.3 = (bf16[144,1024]{1,0:T(8,128)(2,1)S(1)}, bf16[144,1024]{1,0:T(8,128)(2,1)S(1)}, u32[]{:S(2)}, u32[]{:S(2)}) collective-permute-start(bf16[144,1024]{1,0:T(8,128)(2,1)S(1)} %bitcast.30), channel_id=1, source_target_pairs={{4,0},{8,4},{12,8},{5,1},{9,5},{13,9},{6,2},{10,6},{14,10},{7,3},{... | collective-permute-start | bytes 884744 | tf_op jit(solution)/shard_map/ppermute | solution.py:468
  20.7 11.5 %collective-permute-start.7 = (bf16[512,1024]{1,0:T(8,128)(2,1)S(1)}, bf16[512,1024]{1,0:T(8,128)(2,1)S(1)}, u32[]{:S(2)}, u32[]{:S(2)}) collective-permute-start(bf16[512,1024]{1,0:T(8,128)(2,1)S(1)} %bitcast.18), channel_id=1, source_target_pairs={{0,1},{1,0},{2,3},{3,2},{4,5},{5,4},{6,7},{7,6},{8,9},{9,8},{10,11... | collective-permute-start | bytes 3145736 | tf_op jit(solution)/shard_map/ppermute | solution.py:165
  20.7 9.9 %collective-permute-start.6 = (bf16[144,1024]{1,0:T(8,128)(2,1)S(1)}, bf16[144,1024]{1,0:T(8,128)(2,1)S(1)}, u32[]{:S(2)}, u32[]{:S(2)}) collective-permute-start(bf16[144,1024]{1,0:T(8,128)(2,1)S(1)} %shard_map.97.mine), channel_id=1, source_target_pairs={{0,2},{2,0},{1,3},{3,1},{4,6},{6,4},{5,7},{7,5},{8,10},{10,8},{9,1... | collective-permute-start | bytes 884744 | tf_op jit(solution)/shard_map/ppermute | solution.py:165
  24.3 16.1 %collective-permute-start.8 = (bf16[144,1024]{1,0:T(8,128)(2,1)S(1)}, bf16[144,1024]{1,0:T(8,128)(2,1)S(1)}, u32[]{:S(2)}, u32[]{:S(2)}) collective-permute-start(bf16[144,1024]{1,0:T(8,128)(2,1)S(1)} %shard_map.99.mine), channel_id=1, source_target_pairs={{0,2},{2,0},{1,3},{3,1},{4,6},{6,4},{5,7},{7,5},{8,10},{10,8},{9,1... | collective-permute-start | bytes 884744 | tf_op jit(solution)/shard_map/ppermute | solution.py:165
  24.9 8.1 %collective-permute-start.9 = (bf16[256,128]{1,0:T(8,128)(2,1)S(1)}, bf16[256,128]{1,0:T(8,128)(2,1)S(1)}, u32[]{:S(2)}, u32[]{:S(2)}) collective-permute-start(bf16[256,128]{1,0:T(8,128)(2,1)S(1)} %get-tuple-element.53), channel_id=1, source_target_pairs={{0,4},{4,8},{8,12},{12,0},{1,5},{5,9},{9,13},{13,1},{2,6},{6,10},{... | collective-permute-start | bytes 196616 | tf_op jit(solution)/shard_map/ppermute | solution.py:21
  26.5 7.0 %collective-permute-start.10 = (bf16[256,128]{1,0:T(8,128)(2,1)S(1)}, bf16[256,128]{1,0:T(8,128)(2,1)S(1)}, u32[]{:S(2)}, u32[]{:S(2)}) collective-permute-start(bf16[256,128]{1,0:T(8,128)(2,1)S(1)} %get-tuple-element.54), channel_id=1, source_target_pairs={{0,8},{4,12},{8,0},{12,4},{1,9},{5,13},{9,1},{13,5},{2,10},{6,14},... | collective-permute-start | bytes 196616 | tf_op jit(solution)/shard_map/ppermute | solution.py:21
  34.9 6.7 %collective-permute-start.12 = (bf16[144,256]{1,0:T(8,128)(2,1)S(1)}, bf16[144,256]{1,0:T(8,128)(2,1)S(1)}, u32[]{:S(2)}, u32[]{:S(2)}) collective-permute-start(bf16[144,256]{1,0:T(8,128)(2,1)S(1)} %get-tuple-element.66), channel_id=1, source_target_pairs={{0,4},{4,8},{8,12},{12,0},{1,5},{5,9},{9,13},{13,1},{2,6},{6,10},{... | collective-permute-start | bytes 221192 | tf_op jit(solution)/shard_map/ppermute | solution.py:21
  36.4 7.2 %collective-permute-start.13 = (bf16[144,256]{1,0:T(8,128)(2,1)S(1)}, bf16[144,256]{1,0:T(8,128)(2,1)S(1)}, u32[]{:S(2)}, u32[]{:S(2)}) collective-permute-start(bf16[144,256]{1,0:T(8,128)(2,1)S(1)} %get-tuple-element.67), channel_id=1, source_target_pairs={{0,8},{4,12},{8,0},{12,4},{1,9},{5,13},{9,1},{13,5},{2,10},{6,14},... | collective-permute-start | bytes 221192 | tf_op jit(solution)/shard_map/ppermute | solution.py:21
  38.8 4.9 %collective-permute-start.14 = (bf16[144,256]{1,0:T(8,128)(2,1)S(1)}, bf16[144,256]{1,0:T(8,128)(2,1)S(1)}, u32[]{:S(2)}, u32[]{:S(2)}) collective-permute-start(bf16[144,256]{1,0:T(8,128)(2,1)S(1)} %get-tuple-element.68), channel_id=1, source_target_pairs={{0,12},{4,0},{8,4},{12,8},{1,13},{5,1},{9,5},{13,9},{2,14},{6,2},{... | collective-permute-start | bytes 221192 | tf_op jit(solution)/shard_map/ppermute | solution.py:21
  44.5 29.1 %collective-permute-start.23 = (bf16[512,512]{1,0:T(8,128)(2,1)S(1)}, bf16[512,512]{1,0:T(8,128)(2,1)S(1)}, u32[]{:S(2)}, u32[]{:S(2)}) collective-permute-start(bf16[512,512]{1,0:T(8,128)(2,1)S(1)} %copy-done.5), channel_id=1, source_target_pairs={{0,1},{1,0},{2,3},{3,2},{4,5},{5,4},{6,7},{7,6},{8,9},{9,8},{10,11... | collective-permute-start | bytes 1572872 | tf_op jit(solution)/shard_map/ppermute | solution.py:165
  44.6 21.2 %collective-permute-start.24 = (bf16[512,512]{1,0:T(8,128)(2,1)S(1)}, bf16[512,512]{1,0:T(8,128)(2,1)S(1)}, u32[]{:S(2)}, u32[]{:S(2)}) collective-permute-start(bf16[512,512]{1,0:T(8,128)(2,1)S(1)} %copy-done.5), channel_id=1, source_target_pairs={{0,2},{2,0},{1,3},{3,1},{4,6},{6,4},{5,7},{7,5},{8,10},{10,8},{9,1... | collective-permute-start | bytes 1572872 | tf_op jit(solution)/shard_map/ppermute | solution.py:165
  46.2 7.4 %collective-permute-start.15 = (bf16[144,256]{1,0:T(8,128)(2,1)S(1)}, bf16[144,256]{1,0:T(8,128)(2,1)S(1)}, u32[]{:S(2)}, u32[]{:S(2)}) collective-permute-start(bf16[144,256]{1,0:T(8,128)(2,1)S(1)} %get-tuple-element.75), channel_id=1, source_target_pairs={{0,4},{4,8},{8,12},{12,0},{1,5},{5,9},{9,13},{13,1},{2,6},{6,10},{... | collective-permute-start | bytes 221192 | tf_op jit(solution)/shard_map/ppermute | solution.py:21
  47.4 8.2 %collective-permute-start.16 = (bf16[144,256]{1,0:T(8,128)(2,1)S(1)}, bf16[144,256]{1,0:T(8,128)(2,1)S(1)}, u32[]{:S(2)}, u32[]{:S(2)}) collective-permute-start(bf16[144,256]{1,0:T(8,128)(2,1)S(1)} %get-tuple-element.76), channel_id=1, source_target_pairs={{0,8},{4,12},{8,0},{12,4},{1,9},{5,13},{9,1},{13,5},{2,10},{6,14},... | collective-permute-start | bytes 221192 | tf_op jit(solution)/shard_map/ppermute | solution.py:21
  49.6 6.0 %collective-permute-start.17 = (bf16[144,256]{1,0:T(8,128)(2,1)S(1)}, bf16[144,256]{1,0:T(8,128)(2,1)S(1)}, u32[]{:S(2)}, u32[]{:S(2)}) collective-permute-start(bf16[144,256]{1,0:T(8,128)(2,1)S(1)} %get-tuple-element.77), channel_id=1, source_target_pairs={{0,12},{4,0},{8,4},{12,8},{1,13},{5,1},{9,5},{13,9},{2,14},{6,2},{... | collective-permute-start | bytes 221192 | tf_op jit(solution)/shard_map/ppermute | solution.py:21
  58.9 4.7 %collective-permute-start.18 = (bf16[256,128]{1,0:T(8,128)(2,1)S(1)}, bf16[256,128]{1,0:T(8,128)(2,1)S(1)}, u32[]{:S(2)}, u32[]{:S(2)}) collective-permute-start(bf16[256,128]{1,0:T(8,128)(2,1)S(1)} %get-tuple-element.89), channel_id=1, source_target_pairs={{0,2},{2,0},{1,3},{3,1},{4,6},{6,4},{5,7},{7,5},{8,10},{10,8},{9,1... | collective-permute-start | bytes 196616 | tf_op jit(solution)/shard_map/ppermute | solution.py:165
  59.5 6.3 %collective-permute-start.20 = (bf16[256,128]{1,0:T(8,128)(2,1)S(1)}, bf16[256,128]{1,0:T(8,128)(2,1)S(1)}, u32[]{:S(2)}, u32[]{:S(2)}) collective-permute-start(bf16[256,128]{1,0:T(8,128)(2,1)S(1)} %get-tuple-element.90), channel_id=1, source_target_pairs={{0,2},{2,0},{1,3},{3,1},{4,6},{6,4},{5,7},{7,5},{8,10},{10,8},{9,1... | collective-permute-start | bytes 196616 | tf_op jit(solution)/shard_map/ppermute | solution.py:165
  65.8 7.9 %collective-permute-start.25 = (bf16[512,512]{1,0:T(8,128)(2,1)S(1)}, bf16[512,512]{1,0:T(8,128)(2,1)S(1)}, u32[]{:S(2)}, u32[]{:S(2)}) collective-permute-start(bf16[512,512]{1,0:T(8,128)(2,1)S(1)} %collective-permute-done.24.refs_6_), channel_id=1, source_target_pairs={{0,1},{1,0},{2,3},{3,2},{4,5},{5,4},{6,7},{7,6},{8,9},{9,8},{10,11... | collective-permute-start | bytes 1572872 | tf_op jit(solution)/shard_map/ppermute | solution.py:165
  65.9 7.8 %collective-permute-start.21 = (bf16[256,128]{1,0:T(8,128)(2,1)S(1)}, bf16[256,128]{1,0:T(8,128)(2,1)S(1)}, u32[]{:S(2)}, u32[]{:S(2)}) collective-permute-start(bf16[256,128]{1,0:T(8,128)(2,1)S(1)} %pad_maximum_fusion.3), channel_id=1, source_target_pairs={{0,8},{4,12},{8,0},{12,4},{1,9},{5,13},{9,1},{13,5},{2,10},{6,14},... | collective-permute-start | bytes 196616 | tf_op jit(solution)/shard_map/ppermute | solution.py:21
  67.3 6.3 %collective-permute-start.22 = (bf16[256,128]{1,0:T(8,128)(2,1)S(1)}, bf16[256,128]{1,0:T(8,128)(2,1)S(1)}, u32[]{:S(2)}, u32[]{:S(2)}) collective-permute-start(bf16[256,128]{1,0:T(8,128)(2,1)S(1)} %pad_maximum_fusion.4), channel_id=1, source_target_pairs={{0,4},{4,8},{8,12},{12,0},{1,5},{5,9},{9,13},{13,1},{2,6},{6,10},{... | collective-permute-start | bytes 196616 | tf_op jit(solution)/shard_map/ppermute | solution.py:21
  (10 other events, 42.1 us)

commit v5 on v4

--- a/solution.py
+++ b/solution.py
@@ -470,6 +470,8 @@
     wkv_enc = enc_keyval.reshape(width // 2, 2 * hq_enc)
     wq_x = swapped(enc_query, "batch")
     dq_x = swapped(dec_query, "batch")
+    dkv_x = swapped(dec_keyval, "batch").reshape(width // 2, 2 * hq_dec)
+    wkv_dec = dec_keyval.reshape(width // 2, 2 * hq_dec)
 
     q_own, *win_state = call(
         functools.partial(own_kernel, columns),
@@ -499,7 +501,7 @@
     q_in = [q_out[0]] + [from_behind(q_out[s], "tile", s) for s in range(1, tiles)]
 
     wp_x = swapped(enc_proj, "batch")
-    above, below = lax.optimization_barrier((above, below, *q_out))[:2]
+    above = after(above, *q_out)
 
     def window_half(half, halo):
         (part,) = call(
@@ -537,8 +539,6 @@
         )
 
     part_a = window_half(0, above)
-    wkv_dec = after(dec_keyval, part_a).reshape(width // 2, 2 * hq_dec)
-    dkv_x = swapped(wkv_dec, "batch")
     theirs_a = swapped(part_a, "mp")
     part_b = window_half(1, after(below, part_a))
     theirs_b = swapped(part_b, "mp")

time: 75.1 us -> 72 us (0.959)
  waiting for transfers between devices: 23.2 us -> 18.6 us
  starting transfers between devices: 30.4 us -> 31.5 us
    ppermute x1, waiting for transfers between devices: 3.87 us -> 0.16 us  [body(): below = lax.ppermute(upper, 'tile', down)]
    ppermute x12, waiting for transfers between devices: 5.75 us -> 3.52 us  [swapped(): return lax.ppermute(value, axis, [(0, 1), (1, 0)])]
    ppermute x12, waiting for transfers between devices: 13.6 us -> 14.9 us  [from_behind(): lax.ppermute(value, axis, [(i, (i + by) % devices) for i in range(devices)])]
    ppermute x12, starting transfers between devices: 7.05 us -> 8.35 us  [swapped(): return lax.ppermute(value, axis, [(0, 1), (1, 0)])]
    unnamed x19 -> x20, local copies, waits for them, and re-layouts: 1.7 us -> 2.13 us
  transfers between devices with their start and end apart: 26 -> 26, of which waited for: 11 -> 11; matrix products, arithmetic and copies ran while one was open for 3% -> 4% of each run, Pallas kernels for 17% -> 20%
where the time goes in v5:
time: 72 us; the launch traced here: 71.8 us
  starting transfers between devices  31.5 us (44%)
  waiting for transfers between devices  18.6 us (26%)
  Pallas kernels  16.6 us (23%)
  local copies, waits for them, and re-layouts  3.24 us (4%)
  between operations  0.92 us (1%)
  other arithmetic  0.88 us (1%)
    ppermute x12, starting transfers between devices, from_behind(): lax.ppermute(value, axis, [(i, (i + by) % devices) for i in range(devices)])  17 us
    pallas_call x10, Pallas kernels, call(): pl.pallas_call(kernel, out_shape=[jax.ShapeDtypeStruct(shape, dtype) for...  16.6 us
    ppermute x12, waiting for transfers between devices, from_behind(): lax.ppermute(value, axis, [(i, (i + by) % devices) for i in range(devices)])  14.9 us
    ppermute x12, starting transfers between devices, swapped(): return lax.ppermute(value, axis, [(0, 1), (1, 0)])  8.35 us
    ppermute x1, starting transfers between devices, body(): above = lax.ppermute(lower, 'tile', up)  4.85 us
    ppermute x12, waiting for transfers between devices, swapped(): return lax.ppermute(value, axis, [(0, 1), (1, 0)])  3.52 us
    unnamed x20, local copies, waits for them, and re-layouts  2.13 us
  transfers between devices with their start and end apart: 26, of which 11 were waited for; matrix products, arithmetic and copies ran while one was open for 4% of the time, Pallas kernels for 20%

profile of v5, /device:TPU:0, one launch (start us, length us, event | category | flops | bytes accessed | tf_op | source)
XLA Modules:
  0.0 71.8 jit_solution(12641796696132930992)
XLA Ops:
  4.4 4.9 %collective-permute-start.2 = (bf16[144,1024]{1,0:T(8,128)(2,1)S(1)}, bf16[144,1024]{1,0:T(8,128)(2,1)S(1)}, u32[]{:S(2)}, u32[]{:S(2)}) collective-permute-start(bf16[144,1024]{1,0:T(8,128)(2,1)S(1)} %bitcast.35), channel_id=1, source_target_pairs={{0,4},{4,8},{8,12},{1,5},{5,9},{9,13},{2,6},{6,10},{10,14},{3,7},{... | collective-permute-start | bytes 884744 | tf_op jit(solution)/shard_map/ppermute | solution.py:467
  9.3 1.3 %collective-permute-start.7 = (bf16[144,1024]{1,0:T(8,128)(2,1)S(1)}, bf16[144,1024]{1,0:T(8,128)(2,1)S(1)}, u32[]{:S(2)}, u32[]{:S(2)}) collective-permute-start(bf16[144,1024]{1,0:T(8,128)(2,1)S(1)} %bitcast.34), channel_id=1, source_target_pairs={{4,0},{8,4},{12,8},{5,1},{9,5},{13,9},{6,2},{10,6},{14,10},{7,3},{... | collective-permute-start | bytes 884744 | tf_op jit(solution)/shard_map/ppermute | solution.py:468
  12.1 3.1 %shard_map.95 = (bf16[288,512]{1,0:T(8,128)(2,1)S(1)}, f32[288,512]{1,0:T(8,128)S(1)}, f32[288,512]{1,0:T(8,128)S(1)}, f32[288,512]{1,0:T(8,128)S(1)}) custom-call(bf16[288,1024]{1,0:T(8,128)(2,1)S(1)} %bitcast.24, bf16[512,512]{1,0:T(8,128)(2,1)S(1)} %copy-done.3, bf16[512,512]{1,0:T(8,128)(2,1)S(1)} %collective-permute-done.wq_x, ...), custom_call_target="tpu_custom_call" | custom-call | flops 1 | bytes 4915200 | tf_op jit(solution)/shard_map/pallas_call | solution.py:427
  16.2 2.0 %shard_map.97.mine = bf16[144,1024]{1,0:T(8,128)(2,1)S(1)} custom-call(bf16[288,512]{1,0:T(8,128)(2,1)S(1)} %get-tuple-element.45.q_own, f32[288,512]{1,0:T(8,128)S(1)} %get-tuple-element.46.acc, f32[288,512]{1,0:T(8,128)S(1)} %get-tuple-element.47.total, f32[288,512]{1,0:T(8,128)S(1)} %get-tuple-element.48.top, ...), custom_call_target="tpu_custom_call" | custom-call | flops 1132462080 | bytes 4915200 | tf_op jit(solution)/shard_map/pallas_call | solution.py:427
  18.2 1.6 %collective-permute-start.5 = (bf16[144,1024]{1,0:T(8,128)(2,1)S(1)}, bf16[144,1024]{1,0:T(8,128)(2,1)S(1)}, u32[]{:S(2)}, u32[]{:S(2)}) collective-permute-start(bf16[144,1024]{1,0:T(8,128)(2,1)S(1)} %shard_map.97.mine), channel_id=1, source_target_pairs={{0,2},{2,0},{1,3},{3,1},{4,6},{6,4},{5,7},{7,5},{8,10},{10,8},{9,1... | collective-permute-start | bytes 884744 | tf_op jit(solution)/shard_map/ppermute | solution.py:165
  19.9 2.0 %shard_map.99.mine = bf16[144,1024]{1,0:T(8,128)(2,1)S(1)} custom-call(bf16[288,512]{1,0:T(8,128)(2,1)S(1)} %get-tuple-element.45.q_own, f32[288,512]{1,0:T(8,128)S(1)} %get-tuple-element.46.acc, f32[288,512]{1,0:T(8,128)S(1)} %get-tuple-element.47.total, f32[288,512]{1,0:T(8,128)S(1)} %get-tuple-element.48.top, ...), custom_call_target="tpu_custom_call" | custom-call | flops 1132462080 | bytes 4915200 | tf_op jit(solution)/shard_map/pallas_call | solution.py:427
  21.9 1.6 %collective-permute-start.8 = (bf16[144,1024]{1,0:T(8,128)(2,1)S(1)}, bf16[144,1024]{1,0:T(8,128)(2,1)S(1)}, u32[]{:S(2)}, u32[]{:S(2)}) collective-permute-start(bf16[144,1024]{1,0:T(8,128)(2,1)S(1)} %shard_map.99.mine), channel_id=1, source_target_pairs={{0,2},{2,0},{1,3},{3,1},{4,6},{6,4},{5,7},{7,5},{8,10},{10,8},{9,1... | collective-permute-start | bytes 884744 | tf_op jit(solution)/shard_map/ppermute | solution.py:165
  23.5 1.6 %collective-permute-start.9 = (bf16[256,128]{1,0:T(8,128)(2,1)S(1)}, bf16[256,128]{1,0:T(8,128)(2,1)S(1)}, u32[]{:S(2)}, u32[]{:S(2)}) collective-permute-start(bf16[256,128]{1,0:T(8,128)(2,1)S(1)} %get-tuple-element.51), channel_id=1, source_target_pairs={{0,4},{4,8},{8,12},{12,0},{1,5},{5,9},{9,13},{13,1},{2,6},{6,10},{... | collective-permute-start | bytes 196616 | tf_op jit(solution)/shard_map/ppermute | solution.py:21
  25.1 2.6 %collective-permute-start.10 = (bf16[256,128]{1,0:T(8,128)(2,1)S(1)}, bf16[256,128]{1,0:T(8,128)(2,1)S(1)}, u32[]{:S(2)}, u32[]{:S(2)}) collective-permute-start(bf16[256,128]{1,0:T(8,128)(2,1)S(1)} %get-tuple-element.52), channel_id=1, source_target_pairs={{0,8},{4,12},{8,0},{12,4},{1,9},{5,13},{9,1},{13,5},{2,10},{6,14},... | collective-permute-start | bytes 196616 | tf_op jit(solution)/shard_map/ppermute | solution.py:21
  27.6 1.4 %collective-permute-start.11 = (bf16[256,128]{1,0:T(8,128)(2,1)S(1)}, bf16[256,128]{1,0:T(8,128)(2,1)S(1)}, u32[]{:S(2)}, u32[]{:S(2)}) collective-permute-start(bf16[256,128]{1,0:T(8,128)(2,1)S(1)} %get-tuple-element.53), channel_id=1, source_target_pairs={{0,12},{4,0},{8,4},{12,8},{1,13},{5,1},{9,5},{13,9},{2,14},{6,2},{... | collective-permute-start | bytes 196616 | tf_op jit(solution)/shard_map/ppermute | solution.py:21
  30.4 1.6 %collective-permute-done.10.refs_2_.refs_0_ = bf16[256,128]{1,0:T(8,128)(2,1)S(1)} collective-permute-done((bf16[256,128]{1,0:T(8,128)(2,1)S(1)}, bf16[256,128]{1,0:T(8,128)(2,1)S(1)}, u32[]{:S(2)}, u32[]{:S(2)}) %collective-permute-start.10) | collective-permute-done | bytes 65568 | tf_op jit(solution)/shard_map/ppermute | solution.py:21
  33.1 2.5 %collective-permute-start.13 = (bf16[144,256]{1,0:T(8,128)(2,1)S(1)}, bf16[144,256]{1,0:T(8,128)(2,1)S(1)}, u32[]{:S(2)}, u32[]{:S(2)}) collective-permute-start(bf16[144,256]{1,0:T(8,128)(2,1)S(1)} %get-tuple-element.63), channel_id=1, source_target_pairs={{0,8},{4,12},{8,0},{12,4},{1,9},{5,13},{9,1},{13,5},{2,10},{6,14},... | collective-permute-start | bytes 221192 | tf_op jit(solution)/shard_map/ppermute | solution.py:21
  36.1 2.4 %collective-permute-done.12.refs_5_ = bf16[144,256]{1,0:T(8,128)(2,1)S(1)} collective-permute-done((bf16[144,256]{1,0:T(8,128)(2,1)S(1)}, bf16[144,256]{1,0:T(8,128)(2,1)S(1)}, u32[]{:S(2)}, u32[]{:S(2)}) %collective-permute-start.12) | collective-permute-done | bytes 73760 | tf_op jit(solution)/shard_map/ppermute | solution.py:21
  38.5 1.9 %collective-permute-done.13.refs_6_ = bf16[144,256]{1,0:T(8,128)(2,1)S(1)} collective-permute-done((bf16[144,256]{1,0:T(8,128)(2,1)S(1)}, bf16[144,256]{1,0:T(8,128)(2,1)S(1)}, u32[]{:S(2)}, u32[]{:S(2)}) %collective-permute-start.13) | collective-permute-done | bytes 73760 | tf_op jit(solution)/shard_map/ppermute | solution.py:21
  41.6 1.5 %collective-permute-start.24 = (bf16[512,512]{1,0:T(8,128)(2,1)S(1)}, bf16[512,512]{1,0:T(8,128)(2,1)S(1)}, u32[]{:S(2)}, u32[]{:S(2)}) collective-permute-start(bf16[512,512]{1,0:T(8,128)(2,1)S(1)} %copy-done.5), channel_id=1, source_target_pairs={{0,2},{2,0},{1,3},{3,1},{4,6},{6,4},{5,7},{7,5},{8,10},{10,8},{9,1... | collective-permute-start | bytes 1572872 | tf_op jit(solution)/shard_map/ppermute | solution.py:165
  44.2 1.6 %collective-permute-start.16 = (bf16[144,256]{1,0:T(8,128)(2,1)S(1)}, bf16[144,256]{1,0:T(8,128)(2,1)S(1)}, u32[]{:S(2)}, u32[]{:S(2)}) collective-permute-start(bf16[144,256]{1,0:T(8,128)(2,1)S(1)} %get-tuple-element.72), channel_id=1, source_target_pairs={{0,8},{4,12},{8,0},{12,4},{1,9},{5,13},{9,1},{13,5},{2,10},{6,14},... | collective-permute-start | bytes 221192 | tf_op jit(solution)/shard_map/ppermute | solution.py:21
  47.0 2.7 %shard_map.101 = (f32[1024,128]{1,0:T(8,128)S(1)}, f32[1024,128]{1,0:T(8,128)S(1)}, f32[1024,128]{1,0:T(8,128)S(1)}) custom-call(bf16[256,128]{1,0:T(8,128)(2,1)S(1)} %get-tuple-element.83.refs_0_, bf16[256,128]{1,0:T(8,128)(2,1)S(1)} %collective-permute-done.9.refs_1_, bf16[256,128]{1,0:T(8,128)(2,1)S(1)} %collective-permute-done.10.refs_2_.refs_0_, ...), custom_call_target="tpu_custom_call" | custom-call | flops 1 | bytes 1343488 | tf_op jit(solution)/shard_map/pallas_call | solution.py:427
  50.6 2.0 %collective-permute-done.16.refs_4_ = bf16[144,256]{1,0:T(8,128)(2,1)S(1)} collective-permute-done((bf16[144,256]{1,0:T(8,128)(2,1)S(1)}, bf16[144,256]{1,0:T(8,128)(2,1)S(1)}, u32[]{:S(2)}, u32[]{:S(2)}) %collective-permute-start.16) | collective-permute-done | bytes 73760 | tf_op jit(solution)/shard_map/ppermute | solution.py:21
  52.6 1.6 %shard_map.102 = (bf16[256,128]{1,0:T(8,128)(2,1)S(1)}, bf16[256,128]{1,0:T(8,128)(2,1)S(1)}) custom-call(bf16[256,128]{1,0:T(8,128)(2,1)S(1)} %collective-permute-done.10.refs_2_.refs_0_, bf16[256,128]{1,0:T(8,128)(2,1)S(1)} %collective-permute-done.11.refs_3_.refs_1_, bf16[144,256]{1,0:T(8,128)(2,1)S(1)} %get-tuple-element.70.refs_2_, ...), custom_call_target="tpu_custom_call" | custom-call | flops 1 | bytes 1343488 | tf_op jit(solution)/shard_map/pallas_call | solution.py:427
  54.2 1.6 %shard_map.103 = (bf16[256,128]{1,0:T(8,128)(2,1)S(1)}, bf16[256,128]{1,0:T(8,128)(2,1)S(1)}) custom-call(bf16[256,128]{1,0:T(8,128)(2,1)S(1)} %get-tuple-element.83.refs_0_, bf16[256,128]{1,0:T(8,128)(2,1)S(1)} %collective-permute-done.9.refs_1_, bf16[144,256]{1,0:T(8,128)(2,1)S(1)} %get-tuple-element.70.refs_2_, ...), custom_call_target="tpu_custom_call" | custom-call | flops 1 | bytes 1343488 | tf_op jit(solution)/shard_map/pallas_call | solution.py:427
  56.5 1.5 %collective-permute-start.20 = (bf16[256,128]{1,0:T(8,128)(2,1)S(1)}, bf16[256,128]{1,0:T(8,128)(2,1)S(1)}, u32[]{:S(2)}, u32[]{:S(2)}) collective-permute-start(bf16[256,128]{1,0:T(8,128)(2,1)S(1)} %get-tuple-element.86), channel_id=1, source_target_pairs={{0,2},{2,0},{1,3},{3,1},{4,6},{6,4},{5,7},{7,5},{8,10},{10,8},{9,1... | collective-permute-start | bytes 196616 | tf_op jit(solution)/shard_map/ppermute | solution.py:165
  58.0 2.4 %collective-permute-done.18 = bf16[256,128]{1,0:T(8,128)(2,1)S(1)} collective-permute-done((bf16[256,128]{1,0:T(8,128)(2,1)S(1)}, bf16[256,128]{1,0:T(8,128)(2,1)S(1)}, u32[]{:S(2)}, u32[]{:S(2)}) %collective-permute-start.18) | collective-permute-done | bytes 65568 | tf_op jit(solution)/shard_map/ppermute | solution.py:165
  60.3 2.6 %collective-permute-start.19 = (bf16[256,128]{1,0:T(8,128)(2,1)S(1)}, bf16[256,128]{1,0:T(8,128)(2,1)S(1)}, u32[]{:S(2)}, u32[]{:S(2)}) collective-permute-start(bf16[256,128]{1,0:T(8,128)(2,1)S(1)} %pad_maximum_fusion.2), channel_id=1, source_target_pairs={{0,12},{4,0},{8,4},{12,8},{1,13},{5,1},{9,5},{13,9},{2,14},{6,2},{... | collective-permute-start | bytes 196616 | tf_op jit(solution)/shard_map/ppermute | solution.py:21
  64.9 5.7 %collective-permute-done.21.refs_2_ = bf16[256,128]{1,0:T(8,128)(2,1)S(1)} collective-permute-done((bf16[256,128]{1,0:T(8,128)(2,1)S(1)}, bf16[256,128]{1,0:T(8,128)(2,1)S(1)}, u32[]{:S(2)}, u32[]{:S(2)}) %collective-permute-start.21) | collective-permute-done | bytes 65568 | tf_op jit(solution)/shard_map/ppermute | solution.py:21
  (68 shorter events, 17.3 us)
Async XLA Ops:
  0.6 8.6 %collective-permute-start.1 = (bf16[512,2,512]{2,1,0:T(2,128)(2,1)}, bf16[512,2,512]{2,1,0:T(2,128)(2,1)S(1)}, u32[]{:S(2)}, u32[]{:S(2)}) collective-permute-start(bf16[512,2,512]{2,1,0:T(2,128)(2,1)} %param.11), channel_id=1, source_target_pairs={{0,1},{1,0},{2,3},{3,2},{4,5},{5,4},{6,7},{7,6},{8,9},{9,8},{10,11... | collective-permute-start | bytes 3145736 | tf_op jit(solution)/shard_map/ppermute | solution.py:165
  1.2 26.4 %collective-permute-start.6 = (bf16[512,2,512]{2,1,0:T(2,128)(2,1)}, bf16[512,2,512]{2,1,0:T(2,128)(2,1)S(1)}, u32[]{:S(2)}, u32[]{:S(2)}) collective-permute-start(bf16[512,2,512]{2,1,0:T(2,128)(2,1)} %param.14), channel_id=1, source_target_pairs={{0,1},{1,0},{2,3},{3,2},{4,5},{5,4},{6,7},{7,6},{8,9},{9,8},{10,11... | collective-permute-start | bytes 3145736 | tf_op jit(solution)/shard_map/ppermute | solution.py:165
  1.7 13.5 %collective-permute-start.3 = (bf16[512,512]{1,0:T(8,128)(2,1)}, bf16[512,512]{1,0:T(8,128)(2,1)S(1)}, u32[]{:S(2)}, u32[]{:S(2)}) collective-permute-start(bf16[512,512]{1,0:T(8,128)(2,1)} %wq_o.3), channel_id=1, source_target_pairs={{0,1},{1,0},{2,3},{3,2},{4,5},{5,4},{6,7},{7,6},{8,9},{9,8},{10,11... | collective-permute-start | bytes 1572872 | tf_op jit(solution)/shard_map/ppermute | solution.py:165
  1.7 14.3 %collective-permute-start.4 = (bf16[512,512]{1,0:T(8,128)(2,1)}, bf16[512,512]{1,0:T(8,128)(2,1)S(1)}, u32[]{:S(2)}, u32[]{:S(2)}) collective-permute-start(bf16[512,512]{1,0:T(8,128)(2,1)} %wp_o.3), channel_id=1, source_target_pairs={{0,1},{1,0},{2,3},{3,2},{4,5},{5,4},{6,7},{7,6},{8,9},{9,8},{10,11... | collective-permute-start | bytes 1572872 | tf_op jit(solution)/shard_map/ppermute | solution.py:165
  4.4 11.6 %collective-permute-start.2 = (bf16[144,1024]{1,0:T(8,128)(2,1)S(1)}, bf16[144,1024]{1,0:T(8,128)(2,1)S(1)}, u32[]{:S(2)}, u32[]{:S(2)}) collective-permute-start(bf16[144,1024]{1,0:T(8,128)(2,1)S(1)} %bitcast.35), channel_id=1, source_target_pairs={{0,4},{4,8},{8,12},{1,5},{5,9},{9,13},{2,6},{6,10},{10,14},{3,7},{... | collective-permute-start | bytes 884744 | tf_op jit(solution)/shard_map/ppermute | solution.py:467
  9.3 10.7 %collective-permute-start.7 = (bf16[144,1024]{1,0:T(8,128)(2,1)S(1)}, bf16[144,1024]{1,0:T(8,128)(2,1)S(1)}, u32[]{:S(2)}, u32[]{:S(2)}) collective-permute-start(bf16[144,1024]{1,0:T(8,128)(2,1)S(1)} %bitcast.34), channel_id=1, source_target_pairs={{4,0},{8,4},{12,8},{5,1},{9,5},{13,9},{6,2},{10,6},{14,10},{7,3},{... | collective-permute-start | bytes 884744 | tf_op jit(solution)/shard_map/ppermute | solution.py:468
  18.2 11.3 %collective-permute-start.5 = (bf16[144,1024]{1,0:T(8,128)(2,1)S(1)}, bf16[144,1024]{1,0:T(8,128)(2,1)S(1)}, u32[]{:S(2)}, u32[]{:S(2)}) collective-permute-start(bf16[144,1024]{1,0:T(8,128)(2,1)S(1)} %shard_map.97.mine), channel_id=1, source_target_pairs={{0,2},{2,0},{1,3},{3,1},{4,6},{6,4},{5,7},{7,5},{8,10},{10,8},{9,1... | collective-permute-start | bytes 884744 | tf_op jit(solution)/shard_map/ppermute | solution.py:165
  21.9 14.1 %collective-permute-start.8 = (bf16[144,1024]{1,0:T(8,128)(2,1)S(1)}, bf16[144,1024]{1,0:T(8,128)(2,1)S(1)}, u32[]{:S(2)}, u32[]{:S(2)}) collective-permute-start(bf16[144,1024]{1,0:T(8,128)(2,1)S(1)} %shard_map.99.mine), channel_id=1, source_target_pairs={{0,2},{2,0},{1,3},{3,1},{4,6},{6,4},{5,7},{7,5},{8,10},{10,8},{9,1... | collective-permute-start | bytes 884744 | tf_op jit(solution)/shard_map/ppermute | solution.py:165
  23.5 6.8 %collective-permute-start.9 = (bf16[256,128]{1,0:T(8,128)(2,1)S(1)}, bf16[256,128]{1,0:T(8,128)(2,1)S(1)}, u32[]{:S(2)}, u32[]{:S(2)}) collective-permute-start(bf16[256,128]{1,0:T(8,128)(2,1)S(1)} %get-tuple-element.51), channel_id=1, source_target_pairs={{0,4},{4,8},{8,12},{12,0},{1,5},{5,9},{9,13},{13,1},{2,6},{6,10},{... | collective-permute-start | bytes 196616 | tf_op jit(solution)/shard_map/ppermute | solution.py:21
  25.1 6.9 %collective-permute-start.10 = (bf16[256,128]{1,0:T(8,128)(2,1)S(1)}, bf16[256,128]{1,0:T(8,128)(2,1)S(1)}, u32[]{:S(2)}, u32[]{:S(2)}) collective-permute-start(bf16[256,128]{1,0:T(8,128)(2,1)S(1)} %get-tuple-element.52), channel_id=1, source_target_pairs={{0,8},{4,12},{8,0},{12,4},{1,9},{5,13},{9,1},{13,5},{2,10},{6,14},... | collective-permute-start | bytes 196616 | tf_op jit(solution)/shard_map/ppermute | solution.py:21
  27.6 4.6 %collective-permute-start.11 = (bf16[256,128]{1,0:T(8,128)(2,1)S(1)}, bf16[256,128]{1,0:T(8,128)(2,1)S(1)}, u32[]{:S(2)}, u32[]{:S(2)}) collective-permute-start(bf16[256,128]{1,0:T(8,128)(2,1)S(1)} %get-tuple-element.53), channel_id=1, source_target_pairs={{0,12},{4,0},{8,4},{12,8},{1,13},{5,1},{9,5},{13,9},{2,14},{6,2},{... | collective-permute-start | bytes 196616 | tf_op jit(solution)/shard_map/ppermute | solution.py:21
  32.3 6.3 %collective-permute-start.12 = (bf16[144,256]{1,0:T(8,128)(2,1)S(1)}, bf16[144,256]{1,0:T(8,128)(2,1)S(1)}, u32[]{:S(2)}, u32[]{:S(2)}) collective-permute-start(bf16[144,256]{1,0:T(8,128)(2,1)S(1)} %get-tuple-element.62), channel_id=1, source_target_pairs={{0,4},{4,8},{8,12},{12,0},{1,5},{5,9},{9,13},{13,1},{2,6},{6,10},{... | collective-permute-start | bytes 221192 | tf_op jit(solution)/shard_map/ppermute | solution.py:21
  33.1 7.3 %collective-permute-start.13 = (bf16[144,256]{1,0:T(8,128)(2,1)S(1)}, bf16[144,256]{1,0:T(8,128)(2,1)S(1)}, u32[]{:S(2)}, u32[]{:S(2)}) collective-permute-start(bf16[144,256]{1,0:T(8,128)(2,1)S(1)} %get-tuple-element.63), channel_id=1, source_target_pairs={{0,8},{4,12},{8,0},{12,4},{1,9},{5,13},{9,1},{13,5},{2,10},{6,14},... | collective-permute-start | bytes 221192 | tf_op jit(solution)/shard_map/ppermute | solution.py:21
  35.6 5.1 %collective-permute-start.14 = (bf16[144,256]{1,0:T(8,128)(2,1)S(1)}, bf16[144,256]{1,0:T(8,128)(2,1)S(1)}, u32[]{:S(2)}, u32[]{:S(2)}) collective-permute-start(bf16[144,256]{1,0:T(8,128)(2,1)S(1)} %get-tuple-element.64), channel_id=1, source_target_pairs={{0,12},{4,0},{8,4},{12,8},{1,13},{5,1},{9,5},{13,9},{2,14},{6,2},{... | collective-permute-start | bytes 221192 | tf_op jit(solution)/shard_map/ppermute | solution.py:21
  41.6 29.0 %collective-permute-start.23 = (bf16[512,512]{1,0:T(8,128)(2,1)S(1)}, bf16[512,512]{1,0:T(8,128)(2,1)S(1)}, u32[]{:S(2)}, u32[]{:S(2)}) collective-permute-start(bf16[512,512]{1,0:T(8,128)(2,1)S(1)} %copy-done.5), channel_id=1, source_target_pairs={{0,1},{1,0},{2,3},{3,2},{4,5},{5,4},{6,7},{7,6},{8,9},{9,8},{10,11... | collective-permute-start | bytes 1572872 | tf_op jit(solution)/shard_map/ppermute | solution.py:165
  41.6 21.3 %collective-permute-start.24 = (bf16[512,512]{1,0:T(8,128)(2,1)S(1)}, bf16[512,512]{1,0:T(8,128)(2,1)S(1)}, u32[]{:S(2)}, u32[]{:S(2)}) collective-permute-start(bf16[512,512]{1,0:T(8,128)(2,1)S(1)} %copy-done.5), channel_id=1, source_target_pairs={{0,2},{2,0},{1,3},{3,1},{4,6},{6,4},{5,7},{7,5},{8,10},{10,8},{9,1... | collective-permute-start | bytes 1572872 | tf_op jit(solution)/shard_map/ppermute | solution.py:165
  43.2 7.4 %collective-permute-start.15 = (bf16[144,256]{1,0:T(8,128)(2,1)S(1)}, bf16[144,256]{1,0:T(8,128)(2,1)S(1)}, u32[]{:S(2)}, u32[]{:S(2)}) collective-permute-start(bf16[144,256]{1,0:T(8,128)(2,1)S(1)} %get-tuple-element.71), channel_id=1, source_target_pairs={{0,4},{4,8},{8,12},{12,0},{1,5},{5,9},{9,13},{13,1},{2,6},{6,10},{... | collective-permute-start | bytes 221192 | tf_op jit(solution)/shard_map/ppermute | solution.py:21
  44.2 8.3 %collective-permute-start.16 = (bf16[144,256]{1,0:T(8,128)(2,1)S(1)}, bf16[144,256]{1,0:T(8,128)(2,1)S(1)}, u32[]{:S(2)}, u32[]{:S(2)}) collective-permute-start(bf16[144,256]{1,0:T(8,128)(2,1)S(1)} %get-tuple-element.72), channel_id=1, source_target_pairs={{0,8},{4,12},{8,0},{12,4},{1,9},{5,13},{9,1},{13,5},{2,10},{6,14},... | collective-permute-start | bytes 221192 | tf_op jit(solution)/shard_map/ppermute | solution.py:21
  45.9 6.7 %collective-permute-start.17 = (bf16[144,256]{1,0:T(8,128)(2,1)S(1)}, bf16[144,256]{1,0:T(8,128)(2,1)S(1)}, u32[]{:S(2)}, u32[]{:S(2)}) collective-permute-start(bf16[144,256]{1,0:T(8,128)(2,1)S(1)} %get-tuple-element.73), channel_id=1, source_target_pairs={{0,12},{4,0},{8,4},{12,8},{1,13},{5,1},{9,5},{13,9},{2,14},{6,2},{... | collective-permute-start | bytes 221192 | tf_op jit(solution)/shard_map/ppermute | solution.py:21
  56.5 6.5 %collective-permute-start.20 = (bf16[256,128]{1,0:T(8,128)(2,1)S(1)}, bf16[256,128]{1,0:T(8,128)(2,1)S(1)}, u32[]{:S(2)}, u32[]{:S(2)}) collective-permute-start(bf16[256,128]{1,0:T(8,128)(2,1)S(1)} %get-tuple-element.86), channel_id=1, source_target_pairs={{0,2},{2,0},{1,3},{3,1},{4,6},{6,4},{5,7},{7,5},{8,10},{10,8},{9,1... | collective-permute-start | bytes 196616 | tf_op jit(solution)/shard_map/ppermute | solution.py:165
  60.3 4.5 %collective-permute-start.19 = (bf16[256,128]{1,0:T(8,128)(2,1)S(1)}, bf16[256,128]{1,0:T(8,128)(2,1)S(1)}, u32[]{:S(2)}, u32[]{:S(2)}) collective-permute-start(bf16[256,128]{1,0:T(8,128)(2,1)S(1)} %pad_maximum_fusion.2), channel_id=1, source_target_pairs={{0,12},{4,0},{8,4},{12,8},{1,13},{5,1},{9,5},{13,9},{2,14},{6,2},{... | collective-permute-start | bytes 196616 | tf_op jit(solution)/shard_map/ppermute | solution.py:21
  63.0 7.6 %collective-permute-start.25 = (bf16[512,512]{1,0:T(8,128)(2,1)S(1)}, bf16[512,512]{1,0:T(8,128)(2,1)S(1)}, u32[]{:S(2)}, u32[]{:S(2)}) collective-permute-start(bf16[512,512]{1,0:T(8,128)(2,1)S(1)} %collective-permute-done.24.refs_6_), channel_id=1, source_target_pairs={{0,1},{1,0},{2,3},{3,2},{4,5},{5,4},{6,7},{7,6},{8,9},{9,8},{10,11... | collective-permute-start | bytes 1572872 | tf_op jit(solution)/shard_map/ppermute | solution.py:165
  63.0 7.6 %collective-permute-start.21 = (bf16[256,128]{1,0:T(8,128)(2,1)S(1)}, bf16[256,128]{1,0:T(8,128)(2,1)S(1)}, u32[]{:S(2)}, u32[]{:S(2)}) collective-permute-start(bf16[256,128]{1,0:T(8,128)(2,1)S(1)} %pad_maximum_fusion.3), channel_id=1, source_target_pairs={{0,8},{4,12},{8,0},{12,4},{1,9},{5,13},{9,1},{13,5},{2,10},{6,14},... | collective-permute-start | bytes 196616 | tf_op jit(solution)/shard_map/ppermute | solution.py:21
  64.1 6.5 %collective-permute-start.22 = (bf16[256,128]{1,0:T(8,128)(2,1)S(1)}, bf16[256,128]{1,0:T(8,128)(2,1)S(1)}, u32[]{:S(2)}, u32[]{:S(2)}) collective-permute-start(bf16[256,128]{1,0:T(8,128)(2,1)S(1)} %pad_maximum_fusion.4), channel_id=1, source_target_pairs={{0,4},{4,8},{8,12},{12,0},{1,5},{5,9},{9,13},{13,1},{2,6},{6,10},{... | collective-permute-start | bytes 196616 | tf_op jit(solution)/shard_map/ppermute | solution.py:21
  (10 other events, 47.3 us)

commit v6 on v5

--- a/solution.py
+++ b/solution.py
@@ -543,12 +543,11 @@
     part_b = window_half(1, after(below, part_a))
     theirs_b = swapped(part_b, "mp")
     encoded_a, *kv_a = key_values(0, part_a, theirs_a)
-    kv_a, q_in = lax.optimization_barrier((list(kv_a), q_in))
     kv_a = [kv_a[0]] + [from_behind(kv_a[s], "tile", s) for s in range(1, tiles)]
-    theirs_b, *kv_a = lax.optimization_barrier((theirs_b, *kv_a))
+    theirs_b, kv_a, q_in = lax.optimization_barrier((theirs_b, kv_a, q_in))
     encoded_b, *kv_b = key_values(1, part_b, theirs_b)
     kv_b = [kv_b[0]] + [from_behind(kv_b[s], "tile", s) for s in range(1, tiles)]
-    out_half = after(dec_out, encoded_b)
+    out_half = after(dec_out, kv_a[1])
     do_x = swapped(out_half, "batch")
     do_m = swapped(out_half, "mp")
     do_mx = swapped(do_m, "batch")

time: 72 us -> 70.8 us (0.983)
  waiting for transfers between devices: 18.6 us -> 15.2 us
  starting transfers between devices: 31.5 us -> 33.7 us
    ppermute x12, waiting for transfers between devices: 14.9 us -> 11.6 us  [from_behind(): lax.ppermute(value, axis, [(i, (i + by) % devices) for i in range(devices)])]
    ppermute x12, starting transfers between devices: 17 us -> 19.2 us  [from_behind(): lax.ppermute(value, axis, [(i, (i + by) % devices) for i in range(devices)])]
  transfers between devices with their start and end apart: 26 -> 26, of which waited for: 11 -> 8; matrix products, arithmetic and copies ran while one was open for 4% -> 4% of each run, Pallas kernels for 20% -> 22%
where the time goes in v6:
time: 70.8 us; the launch traced here: 70.5 us
  starting transfers between devices  33.7 us (48%)
  Pallas kernels  16.6 us (23%)
  waiting for transfers between devices  15.2 us (21%)
  local copies, waits for them, and re-layouts  3.24 us (5%)
  between operations  0.93 us (1%)
  other arithmetic  0.88 us (1%)
    ppermute x12, starting transfers between devices, from_behind(): lax.ppermute(value, axis, [(i, (i + by) % devices) for i in range(devices)])  19.2 us
    pallas_call x10, Pallas kernels, call(): pl.pallas_call(kernel, out_shape=[jax.ShapeDtypeStruct(shape, dtype) for...  16.6 us
    ppermute x12, waiting for transfers between devices, from_behind(): lax.ppermute(value, axis, [(i, (i + by) % devices) for i in range(devices)])  11.6 us
    ppermute x12, starting transfers between devices, swapped(): return lax.ppermute(value, axis, [(0, 1), (1, 0)])  8.36 us
    ppermute x1, starting transfers between devices, body(): above = lax.ppermute(lower, 'tile', up)  4.85 us
    ppermute x12, waiting for transfers between devices, swapped(): return lax.ppermute(value, axis, [(0, 1), (1, 0)])  3.44 us
    unnamed x20, local copies, waits for them, and re-layouts  2.12 us
  transfers between devices with their start and end apart: 26, of which 8 were waited for; matrix products, arithmetic and copies ran while one was open for 4% of the time, Pallas kernels for 22%

profile of v6, /device:TPU:0, one launch (start us, length us, event | category | flops | bytes accessed | tf_op | source)
XLA Modules:
  0.0 70.5 jit_solution(7477182712181614486)
XLA Ops:
  4.4 4.9 %collective-permute-start.2 = (bf16[144,1024]{1,0:T(8,128)(2,1)S(1)}, bf16[144,1024]{1,0:T(8,128)(2,1)S(1)}, u32[]{:S(2)}, u32[]{:S(2)}) collective-permute-start(bf16[144,1024]{1,0:T(8,128)(2,1)S(1)} %bitcast.35), channel_id=1, source_target_pairs={{0,4},{4,8},{8,12},{1,5},{5,9},{9,13},{2,6},{6,10},{10,14},{3,7},{... | collective-permute-start | bytes 884744 | tf_op jit(solution)/shard_map/ppermute | solution.py:467
  9.3 1.3 %collective-permute-start.7 = (bf16[144,1024]{1,0:T(8,128)(2,1)S(1)}, bf16[144,1024]{1,0:T(8,128)(2,1)S(1)}, u32[]{:S(2)}, u32[]{:S(2)}) collective-permute-start(bf16[144,1024]{1,0:T(8,128)(2,1)S(1)} %bitcast.34), channel_id=1, source_target_pairs={{4,0},{8,4},{12,8},{5,1},{9,5},{13,9},{6,2},{10,6},{14,10},{7,3},{... | collective-permute-start | bytes 884744 | tf_op jit(solution)/shard_map/ppermute | solution.py:468
  12.1 3.1 %shard_map.95 = (bf16[288,512]{1,0:T(8,128)(2,1)S(1)}, f32[288,512]{1,0:T(8,128)S(1)}, f32[288,512]{1,0:T(8,128)S(1)}, f32[288,512]{1,0:T(8,128)S(1)}) custom-call(bf16[288,1024]{1,0:T(8,128)(2,1)S(1)} %bitcast.24, bf16[512,512]{1,0:T(8,128)(2,1)S(1)} %copy-done.3, bf16[512,512]{1,0:T(8,128)(2,1)S(1)} %collective-permute-done.wq_x, ...), custom_call_target="tpu_custom_call" | custom-call | flops 1 | bytes 4915200 | tf_op jit(solution)/shard_map/pallas_call | solution.py:427
  16.2 2.0 %shard_map.97.mine = bf16[144,1024]{1,0:T(8,128)(2,1)S(1)} custom-call(bf16[288,512]{1,0:T(8,128)(2,1)S(1)} %get-tuple-element.41.q_own, f32[288,512]{1,0:T(8,128)S(1)} %get-tuple-element.42.acc, f32[288,512]{1,0:T(8,128)S(1)} %get-tuple-element.43.total, f32[288,512]{1,0:T(8,128)S(1)} %get-tuple-element.44.top, ...), custom_call_target="tpu_custom_call" | custom-call | flops 1132462080 | bytes 4915200 | tf_op jit(solution)/shard_map/pallas_call | solution.py:427
  18.2 1.6 %collective-permute-start.5 = (bf16[144,1024]{1,0:T(8,128)(2,1)S(1)}, bf16[144,1024]{1,0:T(8,128)(2,1)S(1)}, u32[]{:S(2)}, u32[]{:S(2)}) collective-permute-start(bf16[144,1024]{1,0:T(8,128)(2,1)S(1)} %shard_map.97.mine), channel_id=1, source_target_pairs={{0,2},{2,0},{1,3},{3,1},{4,6},{6,4},{5,7},{7,5},{8,10},{10,8},{9,1... | collective-permute-start | bytes 884744 | tf_op jit(solution)/shard_map/ppermute | solution.py:165
  19.9 2.0 %shard_map.99.mine = bf16[144,1024]{1,0:T(8,128)(2,1)S(1)} custom-call(bf16[288,512]{1,0:T(8,128)(2,1)S(1)} %get-tuple-element.41.q_own, f32[288,512]{1,0:T(8,128)S(1)} %get-tuple-element.42.acc, f32[288,512]{1,0:T(8,128)S(1)} %get-tuple-element.43.total, f32[288,512]{1,0:T(8,128)S(1)} %get-tuple-element.44.top, ...), custom_call_target="tpu_custom_call" | custom-call | flops 1132462080 | bytes 4915200 | tf_op jit(solution)/shard_map/pallas_call | solution.py:427
  21.9 1.6 %collective-permute-start.8 = (bf16[144,1024]{1,0:T(8,128)(2,1)S(1)}, bf16[144,1024]{1,0:T(8,128)(2,1)S(1)}, u32[]{:S(2)}, u32[]{:S(2)}) collective-permute-start(bf16[144,1024]{1,0:T(8,128)(2,1)S(1)} %shard_map.99.mine), channel_id=1, source_target_pairs={{0,2},{2,0},{1,3},{3,1},{4,6},{6,4},{5,7},{7,5},{8,10},{10,8},{9,1... | collective-permute-start | bytes 884744 | tf_op jit(solution)/shard_map/ppermute | solution.py:165
  23.5 1.6 %collective-permute-start.12 = (bf16[256,128]{1,0:T(8,128)(2,1)S(1)}, bf16[256,128]{1,0:T(8,128)(2,1)S(1)}, u32[]{:S(2)}, u32[]{:S(2)}) collective-permute-start(bf16[256,128]{1,0:T(8,128)(2,1)S(1)} %get-tuple-element.47), channel_id=1, source_target_pairs={{0,4},{4,8},{8,12},{12,0},{1,5},{5,9},{9,13},{13,1},{2,6},{6,10},{... | collective-permute-start | bytes 196616 | tf_op jit(solution)/shard_map/ppermute | solution.py:21
  25.1 2.6 %collective-permute-start.13 = (bf16[256,128]{1,0:T(8,128)(2,1)S(1)}, bf16[256,128]{1,0:T(8,128)(2,1)S(1)}, u32[]{:S(2)}, u32[]{:S(2)}) collective-permute-start(bf16[256,128]{1,0:T(8,128)(2,1)S(1)} %get-tuple-element.48), channel_id=1, source_target_pairs={{0,8},{4,12},{8,0},{12,4},{1,9},{5,13},{9,1},{13,5},{2,10},{6,14},... | collective-permute-start | bytes 196616 | tf_op jit(solution)/shard_map/ppermute | solution.py:21
  29.0 2.7 %collective-permute-start.9 = (bf16[144,256]{1,0:T(8,128)(2,1)S(1)}, bf16[144,256]{1,0:T(8,128)(2,1)S(1)}, u32[]{:S(2)}, u32[]{:S(2)}) collective-permute-start(bf16[144,256]{1,0:T(8,128)(2,1)S(1)} %get-tuple-element.54), channel_id=1, source_target_pairs={{0,4},{4,8},{8,12},{12,0},{1,5},{5,9},{9,13},{13,1},{2,6},{6,10},{... | collective-permute-start | bytes 221192 | tf_op jit(solution)/shard_map/ppermute | solution.py:21
  31.7 2.6 %collective-permute-start.10 = (bf16[144,256]{1,0:T(8,128)(2,1)S(1)}, bf16[144,256]{1,0:T(8,128)(2,1)S(1)}, u32[]{:S(2)}, u32[]{:S(2)}) collective-permute-start(bf16[144,256]{1,0:T(8,128)(2,1)S(1)} %get-tuple-element.55), channel_id=1, source_target_pairs={{0,8},{4,12},{8,0},{12,4},{1,9},{5,13},{9,1},{13,5},{2,10},{6,14},... | collective-permute-start | bytes 221192 | tf_op jit(solution)/shard_map/ppermute | solution.py:21
  34.3 1.3 %collective-permute-start.11 = (bf16[144,256]{1,0:T(8,128)(2,1)S(1)}, bf16[144,256]{1,0:T(8,128)(2,1)S(1)}, u32[]{:S(2)}, u32[]{:S(2)}) collective-permute-start(bf16[144,256]{1,0:T(8,128)(2,1)S(1)} %get-tuple-element.56), channel_id=1, source_target_pairs={{0,12},{4,0},{8,4},{12,8},{1,13},{5,1},{9,5},{13,9},{2,14},{6,2},{... | collective-permute-start | bytes 221192 | tf_op jit(solution)/shard_map/ppermute | solution.py:21
  36.1 3.8 %collective-permute-done.14.refs_3_.refs_1_ = bf16[256,128]{1,0:T(8,128)(2,1)S(1)} collective-permute-done((bf16[256,128]{1,0:T(8,128)(2,1)S(1)}, bf16[256,128]{1,0:T(8,128)(2,1)S(1)}, u32[]{:S(2)}, u32[]{:S(2)}) %collective-permute-start.14) | collective-permute-done | bytes 65568 | tf_op jit(solution)/shard_map/ppermute | solution.py:21
  40.1 1.5 %collective-permute-start.24 = (bf16[512,512]{1,0:T(8,128)(2,1)S(1)}, bf16[512,512]{1,0:T(8,128)(2,1)S(1)}, u32[]{:S(2)}, u32[]{:S(2)}) collective-permute-start(bf16[512,512]{1,0:T(8,128)(2,1)S(1)} %copy-done.5), channel_id=1, source_target_pairs={{0,2},{2,0},{1,3},{3,1},{4,6},{6,4},{5,7},{7,5},{8,10},{10,8},{9,1... | collective-permute-start | bytes 1572872 | tf_op jit(solution)/shard_map/ppermute | solution.py:165
  43.2 2.5 %collective-permute-start.16 = (bf16[144,256]{1,0:T(8,128)(2,1)S(1)}, bf16[144,256]{1,0:T(8,128)(2,1)S(1)}, u32[]{:S(2)}, u32[]{:S(2)}) collective-permute-start(bf16[144,256]{1,0:T(8,128)(2,1)S(1)} %get-tuple-element.64), channel_id=1, source_target_pairs={{0,8},{4,12},{8,0},{12,4},{1,9},{5,13},{9,1},{13,5},{2,10},{6,14},... | collective-permute-start | bytes 221192 | tf_op jit(solution)/shard_map/ppermute | solution.py:21
  46.3 2.7 %shard_map.101 = (f32[1024,128]{1,0:T(8,128)S(1)}, f32[1024,128]{1,0:T(8,128)S(1)}, f32[1024,128]{1,0:T(8,128)S(1)}) custom-call(bf16[256,128]{1,0:T(8,128)(2,1)S(1)} %get-tuple-element.75.refs_0_, bf16[256,128]{1,0:T(8,128)(2,1)S(1)} %collective-permute-done.12.refs_1_, bf16[256,128]{1,0:T(8,128)(2,1)S(1)} %collective-permute-done.13.refs_2_.refs_0_, ...), custom_call_target="tpu_custom_call" | custom-call | flops 1 | bytes 1343488 | tf_op jit(solution)/shard_map/pallas_call | solution.py:427
  49.8 2.0 %collective-permute-done.16.refs_4_ = bf16[144,256]{1,0:T(8,128)(2,1)S(1)} collective-permute-done((bf16[144,256]{1,0:T(8,128)(2,1)S(1)}, bf16[144,256]{1,0:T(8,128)(2,1)S(1)}, u32[]{:S(2)}, u32[]{:S(2)}) %collective-permute-start.16) | collective-permute-done | bytes 73760 | tf_op jit(solution)/shard_map/ppermute | solution.py:21
  51.9 1.6 %shard_map.102 = (bf16[256,128]{1,0:T(8,128)(2,1)S(1)}, bf16[256,128]{1,0:T(8,128)(2,1)S(1)}) custom-call(bf16[256,128]{1,0:T(8,128)(2,1)S(1)} %collective-permute-done.13.refs_2_.refs_0_, bf16[256,128]{1,0:T(8,128)(2,1)S(1)} %collective-permute-done.14.refs_3_.refs_1_, bf16[144,256]{1,0:T(8,128)(2,1)S(1)} %get-tuple-element.62.refs_2_, ...), custom_call_target="tpu_custom_call" | custom-call | flops 1 | bytes 1343488 | tf_op jit(solution)/shard_map/pallas_call | solution.py:427
  53.5 1.6 %shard_map.103 = (bf16[256,128]{1,0:T(8,128)(2,1)S(1)}, bf16[256,128]{1,0:T(8,128)(2,1)S(1)}) custom-call(bf16[256,128]{1,0:T(8,128)(2,1)S(1)} %get-tuple-element.75.refs_0_, bf16[256,128]{1,0:T(8,128)(2,1)S(1)} %collective-permute-done.12.refs_1_, bf16[144,256]{1,0:T(8,128)(2,1)S(1)} %get-tuple-element.62.refs_2_, ...), custom_call_target="tpu_custom_call" | custom-call | flops 1 | bytes 1343488 | tf_op jit(solution)/shard_map/pallas_call | solution.py:427
  55.8 1.5 %collective-permute-start.20 = (bf16[256,128]{1,0:T(8,128)(2,1)S(1)}, bf16[256,128]{1,0:T(8,128)(2,1)S(1)}, u32[]{:S(2)}, u32[]{:S(2)}) collective-permute-start(bf16[256,128]{1,0:T(8,128)(2,1)S(1)} %get-tuple-element.78), channel_id=1, source_target_pairs={{0,2},{2,0},{1,3},{3,1},{4,6},{6,4},{5,7},{7,5},{8,10},{10,8},{9,1... | collective-permute-start | bytes 196616 | tf_op jit(solution)/shard_map/ppermute | solution.py:165
  57.3 2.2 %collective-permute-done.18 = bf16[256,128]{1,0:T(8,128)(2,1)S(1)} collective-permute-done((bf16[256,128]{1,0:T(8,128)(2,1)S(1)}, bf16[256,128]{1,0:T(8,128)(2,1)S(1)}, u32[]{:S(2)}, u32[]{:S(2)}) %collective-permute-start.18) | collective-permute-done | bytes 65568 | tf_op jit(solution)/shard_map/ppermute | solution.py:165
  59.5 2.8 %collective-permute-start.19 = (bf16[256,128]{1,0:T(8,128)(2,1)S(1)}, bf16[256,128]{1,0:T(8,128)(2,1)S(1)}, u32[]{:S(2)}, u32[]{:S(2)}) collective-permute-start(bf16[256,128]{1,0:T(8,128)(2,1)S(1)} %pad_maximum_fusion.2), channel_id=1, source_target_pairs={{0,12},{4,0},{8,4},{12,8},{1,13},{5,1},{9,5},{13,9},{2,14},{6,2},{... | collective-permute-start | bytes 196616 | tf_op jit(solution)/shard_map/ppermute | solution.py:21
  63.6 1.2 %collective-permute-done.19.refs_1_ = bf16[256,128]{1,0:T(8,128)(2,1)S(1)} collective-permute-done((bf16[256,128]{1,0:T(8,128)(2,1)S(1)}, bf16[256,128]{1,0:T(8,128)(2,1)S(1)}, u32[]{:S(2)}, u32[]{:S(2)}) %collective-permute-start.19) | collective-permute-done | bytes 65568 | tf_op jit(solution)/shard_map/ppermute | solution.py:21
  64.9 4.5 %collective-permute-done.21.refs_2_ = bf16[256,128]{1,0:T(8,128)(2,1)S(1)} collective-permute-done((bf16[256,128]{1,0:T(8,128)(2,1)S(1)}, bf16[256,128]{1,0:T(8,128)(2,1)S(1)}, u32[]{:S(2)}, u32[]{:S(2)}) %collective-permute-start.21) | collective-permute-done | bytes 65568 | tf_op jit(solution)/shard_map/ppermute | solution.py:21
  (68 shorter events, 14.4 us)
Async XLA Ops:
  0.6 8.6 %collective-permute-start.1 = (bf16[512,2,512]{2,1,0:T(2,128)(2,1)}, bf16[512,2,512]{2,1,0:T(2,128)(2,1)S(1)}, u32[]{:S(2)}, u32[]{:S(2)}) collective-permute-start(bf16[512,2,512]{2,1,0:T(2,128)(2,1)} %param.11), channel_id=1, source_target_pairs={{0,1},{1,0},{2,3},{3,2},{4,5},{5,4},{6,7},{7,6},{8,9},{9,8},{10,11... | collective-permute-start | bytes 3145736 | tf_op jit(solution)/shard_map/ppermute | solution.py:165
  1.2 26.6 %collective-permute-start.6 = (bf16[512,2,512]{2,1,0:T(2,128)(2,1)}, bf16[512,2,512]{2,1,0:T(2,128)(2,1)S(1)}, u32[]{:S(2)}, u32[]{:S(2)}) collective-permute-start(bf16[512,2,512]{2,1,0:T(2,128)(2,1)} %param.14), channel_id=1, source_target_pairs={{0,1},{1,0},{2,3},{3,2},{4,5},{5,4},{6,7},{7,6},{8,9},{9,8},{10,11... | collective-permute-start | bytes 3145736 | tf_op jit(solution)/shard_map/ppermute | solution.py:165
  1.7 13.5 %collective-permute-start.3 = (bf16[512,512]{1,0:T(8,128)(2,1)}, bf16[512,512]{1,0:T(8,128)(2,1)S(1)}, u32[]{:S(2)}, u32[]{:S(2)}) collective-permute-start(bf16[512,512]{1,0:T(8,128)(2,1)} %wq_o.3), channel_id=1, source_target_pairs={{0,1},{1,0},{2,3},{3,2},{4,5},{5,4},{6,7},{7,6},{8,9},{9,8},{10,11... | collective-permute-start | bytes 1572872 | tf_op jit(solution)/shard_map/ppermute | solution.py:165
  1.7 14.3 %collective-permute-start.4 = (bf16[512,512]{1,0:T(8,128)(2,1)}, bf16[512,512]{1,0:T(8,128)(2,1)S(1)}, u32[]{:S(2)}, u32[]{:S(2)}) collective-permute-start(bf16[512,512]{1,0:T(8,128)(2,1)} %wp_o.3), channel_id=1, source_target_pairs={{0,1},{1,0},{2,3},{3,2},{4,5},{5,4},{6,7},{7,6},{8,9},{9,8},{10,11... | collective-permute-start | bytes 1572872 | tf_op jit(solution)/shard_map/ppermute | solution.py:165
  4.4 11.6 %collective-permute-start.2 = (bf16[144,1024]{1,0:T(8,128)(2,1)S(1)}, bf16[144,1024]{1,0:T(8,128)(2,1)S(1)}, u32[]{:S(2)}, u32[]{:S(2)}) collective-permute-start(bf16[144,1024]{1,0:T(8,128)(2,1)S(1)} %bitcast.35), channel_id=1, source_target_pairs={{0,4},{4,8},{8,12},{1,5},{5,9},{9,13},{2,6},{6,10},{10,14},{3,7},{... | collective-permute-start | bytes 884744 | tf_op jit(solution)/shard_map/ppermute | solution.py:467
  9.3 10.7 %collective-permute-start.7 = (bf16[144,1024]{1,0:T(8,128)(2,1)S(1)}, bf16[144,1024]{1,0:T(8,128)(2,1)S(1)}, u32[]{:S(2)}, u32[]{:S(2)}) collective-permute-start(bf16[144,1024]{1,0:T(8,128)(2,1)S(1)} %bitcast.34), channel_id=1, source_target_pairs={{4,0},{8,4},{12,8},{5,1},{9,5},{13,9},{6,2},{10,6},{14,10},{7,3},{... | collective-permute-start | bytes 884744 | tf_op jit(solution)/shard_map/ppermute | solution.py:468
  18.2 10.0 %collective-permute-start.5 = (bf16[144,1024]{1,0:T(8,128)(2,1)S(1)}, bf16[144,1024]{1,0:T(8,128)(2,1)S(1)}, u32[]{:S(2)}, u32[]{:S(2)}) collective-permute-start(bf16[144,1024]{1,0:T(8,128)(2,1)S(1)} %shard_map.97.mine), channel_id=1, source_target_pairs={{0,2},{2,0},{1,3},{3,1},{4,6},{6,4},{5,7},{7,5},{8,10},{10,8},{9,1... | collective-permute-start | bytes 884744 | tf_op jit(solution)/shard_map/ppermute | solution.py:165
  21.9 18.0 %collective-permute-start.8 = (bf16[144,1024]{1,0:T(8,128)(2,1)S(1)}, bf16[144,1024]{1,0:T(8,128)(2,1)S(1)}, u32[]{:S(2)}, u32[]{:S(2)}) collective-permute-start(bf16[144,1024]{1,0:T(8,128)(2,1)S(1)} %shard_map.99.mine), channel_id=1, source_target_pairs={{0,2},{2,0},{1,3},{3,1},{4,6},{6,4},{5,7},{7,5},{8,10},{10,8},{9,1... | collective-permute-start | bytes 884744 | tf_op jit(solution)/shard_map/ppermute | solution.py:165
  23.5 10.8 %collective-permute-start.12 = (bf16[256,128]{1,0:T(8,128)(2,1)S(1)}, bf16[256,128]{1,0:T(8,128)(2,1)S(1)}, u32[]{:S(2)}, u32[]{:S(2)}) collective-permute-start(bf16[256,128]{1,0:T(8,128)(2,1)S(1)} %get-tuple-element.47), channel_id=1, source_target_pairs={{0,4},{4,8},{8,12},{12,0},{1,5},{5,9},{9,13},{13,1},{2,6},{6,10},{... | collective-permute-start | bytes 196616 | tf_op jit(solution)/shard_map/ppermute | solution.py:21
  25.1 10.6 %collective-permute-start.13 = (bf16[256,128]{1,0:T(8,128)(2,1)S(1)}, bf16[256,128]{1,0:T(8,128)(2,1)S(1)}, u32[]{:S(2)}, u32[]{:S(2)}) collective-permute-start(bf16[256,128]{1,0:T(8,128)(2,1)S(1)} %get-tuple-element.48), channel_id=1, source_target_pairs={{0,8},{4,12},{8,0},{12,4},{1,9},{5,13},{9,1},{13,5},{2,10},{6,14},... | collective-permute-start | bytes 196616 | tf_op jit(solution)/shard_map/ppermute | solution.py:21
  29.0 10.9 %collective-permute-start.9 = (bf16[144,256]{1,0:T(8,128)(2,1)S(1)}, bf16[144,256]{1,0:T(8,128)(2,1)S(1)}, u32[]{:S(2)}, u32[]{:S(2)}) collective-permute-start(bf16[144,256]{1,0:T(8,128)(2,1)S(1)} %get-tuple-element.54), channel_id=1, source_target_pairs={{0,4},{4,8},{8,12},{12,0},{1,5},{5,9},{9,13},{13,1},{2,6},{6,10},{... | collective-permute-start | bytes 221192 | tf_op jit(solution)/shard_map/ppermute | solution.py:21
  31.7 8.2 %collective-permute-start.10 = (bf16[144,256]{1,0:T(8,128)(2,1)S(1)}, bf16[144,256]{1,0:T(8,128)(2,1)S(1)}, u32[]{:S(2)}, u32[]{:S(2)}) collective-permute-start(bf16[144,256]{1,0:T(8,128)(2,1)S(1)} %get-tuple-element.55), channel_id=1, source_target_pairs={{0,8},{4,12},{8,0},{12,4},{1,9},{5,13},{9,1},{13,5},{2,10},{6,14},... | collective-permute-start | bytes 221192 | tf_op jit(solution)/shard_map/ppermute | solution.py:21
  34.3 5.6 %collective-permute-start.11 = (bf16[144,256]{1,0:T(8,128)(2,1)S(1)}, bf16[144,256]{1,0:T(8,128)(2,1)S(1)}, u32[]{:S(2)}, u32[]{:S(2)}) collective-permute-start(bf16[144,256]{1,0:T(8,128)(2,1)S(1)} %get-tuple-element.56), channel_id=1, source_target_pairs={{0,12},{4,0},{8,4},{12,8},{1,13},{5,1},{9,5},{13,9},{2,14},{6,2},{... | collective-permute-start | bytes 221192 | tf_op jit(solution)/shard_map/ppermute | solution.py:21
  40.0 29.4 %collective-permute-start.23 = (bf16[512,512]{1,0:T(8,128)(2,1)S(1)}, bf16[512,512]{1,0:T(8,128)(2,1)S(1)}, u32[]{:S(2)}, u32[]{:S(2)}) collective-permute-start(bf16[512,512]{1,0:T(8,128)(2,1)S(1)} %copy-done.5), channel_id=1, source_target_pairs={{0,1},{1,0},{2,3},{3,2},{4,5},{5,4},{6,7},{7,6},{8,9},{9,8},{10,11... | collective-permute-start | bytes 1572872 | tf_op jit(solution)/shard_map/ppermute | solution.py:165
  40.1 22.3 %collective-permute-start.24 = (bf16[512,512]{1,0:T(8,128)(2,1)S(1)}, bf16[512,512]{1,0:T(8,128)(2,1)S(1)}, u32[]{:S(2)}, u32[]{:S(2)}) collective-permute-start(bf16[512,512]{1,0:T(8,128)(2,1)S(1)} %copy-done.5), channel_id=1, source_target_pairs={{0,2},{2,0},{1,3},{3,1},{4,6},{6,4},{5,7},{7,5},{8,10},{10,8},{9,1... | collective-permute-start | bytes 1572872 | tf_op jit(solution)/shard_map/ppermute | solution.py:165
  42.4 7.4 %collective-permute-start.15 = (bf16[144,256]{1,0:T(8,128)(2,1)S(1)}, bf16[144,256]{1,0:T(8,128)(2,1)S(1)}, u32[]{:S(2)}, u32[]{:S(2)}) collective-permute-start(bf16[144,256]{1,0:T(8,128)(2,1)S(1)} %get-tuple-element.63), channel_id=1, source_target_pairs={{0,4},{4,8},{8,12},{12,0},{1,5},{5,9},{9,13},{13,1},{2,6},{6,10},{... | collective-permute-start | bytes 221192 | tf_op jit(solution)/shard_map/ppermute | solution.py:21
  43.2 8.7 %collective-permute-start.16 = (bf16[144,256]{1,0:T(8,128)(2,1)S(1)}, bf16[144,256]{1,0:T(8,128)(2,1)S(1)}, u32[]{:S(2)}, u32[]{:S(2)}) collective-permute-start(bf16[144,256]{1,0:T(8,128)(2,1)S(1)} %get-tuple-element.64), channel_id=1, source_target_pairs={{0,8},{4,12},{8,0},{12,4},{1,9},{5,13},{9,1},{13,5},{2,10},{6,14},... | collective-permute-start | bytes 221192 | tf_op jit(solution)/shard_map/ppermute | solution.py:21
  45.6 6.3 %collective-permute-start.17 = (bf16[144,256]{1,0:T(8,128)(2,1)S(1)}, bf16[144,256]{1,0:T(8,128)(2,1)S(1)}, u32[]{:S(2)}, u32[]{:S(2)}) collective-permute-start(bf16[144,256]{1,0:T(8,128)(2,1)S(1)} %get-tuple-element.65), channel_id=1, source_target_pairs={{0,12},{4,0},{8,4},{12,8},{1,13},{5,1},{9,5},{13,9},{2,14},{6,2},{... | collective-permute-start | bytes 221192 | tf_op jit(solution)/shard_map/ppermute | solution.py:21
  55.2 4.3 %collective-permute-start.18 = (bf16[256,128]{1,0:T(8,128)(2,1)S(1)}, bf16[256,128]{1,0:T(8,128)(2,1)S(1)}, u32[]{:S(2)}, u32[]{:S(2)}) collective-permute-start(bf16[256,128]{1,0:T(8,128)(2,1)S(1)} %get-tuple-element.77), channel_id=1, source_target_pairs={{0,2},{2,0},{1,3},{3,1},{4,6},{6,4},{5,7},{7,5},{8,10},{10,8},{9,1... | collective-permute-start | bytes 196616 | tf_op jit(solution)/shard_map/ppermute | solution.py:165
  55.8 6.6 %collective-permute-start.20 = (bf16[256,128]{1,0:T(8,128)(2,1)S(1)}, bf16[256,128]{1,0:T(8,128)(2,1)S(1)}, u32[]{:S(2)}, u32[]{:S(2)}) collective-permute-start(bf16[256,128]{1,0:T(8,128)(2,1)S(1)} %get-tuple-element.78), channel_id=1, source_target_pairs={{0,2},{2,0},{1,3},{3,1},{4,6},{6,4},{5,7},{7,5},{8,10},{10,8},{9,1... | collective-permute-start | bytes 196616 | tf_op jit(solution)/shard_map/ppermute | solution.py:165
  59.5 5.4 %collective-permute-start.19 = (bf16[256,128]{1,0:T(8,128)(2,1)S(1)}, bf16[256,128]{1,0:T(8,128)(2,1)S(1)}, u32[]{:S(2)}, u32[]{:S(2)}) collective-permute-start(bf16[256,128]{1,0:T(8,128)(2,1)S(1)} %pad_maximum_fusion.2), channel_id=1, source_target_pairs={{0,12},{4,0},{8,4},{12,8},{1,13},{5,1},{9,5},{13,9},{2,14},{6,2},{... | collective-permute-start | bytes 196616 | tf_op jit(solution)/shard_map/ppermute | solution.py:21
  62.3 7.0 %collective-permute-start.25 = (bf16[512,512]{1,0:T(8,128)(2,1)S(1)}, bf16[512,512]{1,0:T(8,128)(2,1)S(1)}, u32[]{:S(2)}, u32[]{:S(2)}) collective-permute-start(bf16[512,512]{1,0:T(8,128)(2,1)S(1)} %collective-permute-done.24.refs_6_), channel_id=1, source_target_pairs={{0,1},{1,0},{2,3},{3,2},{4,5},{5,4},{6,7},{7,6},{8,9},{9,8},{10,11... | collective-permute-start | bytes 1572872 | tf_op jit(solution)/shard_map/ppermute | solution.py:165
  62.4 7.0 %collective-permute-start.21 = (bf16[256,128]{1,0:T(8,128)(2,1)S(1)}, bf16[256,128]{1,0:T(8,128)(2,1)S(1)}, u32[]{:S(2)}, u32[]{:S(2)}) collective-permute-start(bf16[256,128]{1,0:T(8,128)(2,1)S(1)} %pad_maximum_fusion.3), channel_id=1, source_target_pairs={{0,8},{4,12},{8,0},{12,4},{1,9},{5,13},{9,1},{13,5},{2,10},{6,14},... | collective-permute-start | bytes 196616 | tf_op jit(solution)/shard_map/ppermute | solution.py:21
  62.7 6.7 %collective-permute-start.22 = (bf16[256,128]{1,0:T(8,128)(2,1)S(1)}, bf16[256,128]{1,0:T(8,128)(2,1)S(1)}, u32[]{:S(2)}, u32[]{:S(2)}) collective-permute-start(bf16[256,128]{1,0:T(8,128)(2,1)S(1)} %pad_maximum_fusion.4), channel_id=1, source_target_pairs={{0,4},{4,8},{8,12},{12,0},{1,5},{5,9},{9,13},{13,1},{2,6},{6,10},{... | collective-permute-start | bytes 196616 | tf_op jit(solution)/shard_map/ppermute | solution.py:21
  (10 other events, 48.2 us)

commit v7 on v6

--- a/solution.py
+++ b/solution.py
@@ -501,7 +501,6 @@
     q_in = [q_out[0]] + [from_behind(q_out[s], "tile", s) for s in range(1, tiles)]
 
     wp_x = swapped(enc_proj, "batch")
-    above = after(above, *q_out)
 
     def window_half(half, halo):
         (part,) = call(
@@ -547,7 +546,7 @@
     theirs_b, kv_a, q_in = lax.optimization_barrier((theirs_b, kv_a, q_in))
     encoded_b, *kv_b = key_values(1, part_b, theirs_b)
     kv_b = [kv_b[0]] + [from_behind(kv_b[s], "tile", s) for s in range(1, tiles)]
-    out_half = after(dec_out, kv_a[1])
+    out_half = after(dec_out, encoded_a)
     do_x = swapped(out_half, "batch")
     do_m = swapped(out_half, "mp")
     do_mx = swapped(do_m, "batch")

time: 70.8 us -> 70.4 us (level)
  local copies, waits for them, and re-layouts: 3.24 us -> 4.28 us
  starting transfers between devices: 33.7 us -> 32.8 us
    unnamed x20 -> x18, local copies, waits for them, and re-layouts: 2.12 us -> 3.17 us
    ppermute x12, waiting for transfers between devices: 3.44 us -> 2.62 us  [swapped(): return lax.ppermute(value, axis, [(0, 1), (1, 0)])]
  transfers between devices with their start and end apart: 26 -> 26, of which waited for: 8 -> 5; matrix products, arithmetic and copies ran while one was open for 4% -> 6% of each run, Pallas kernels for 22% -> 22%
where the time goes in v7:
time: 70.4 us; the launch traced here: 70.1 us
  starting transfers between devices  32.8 us (47%)
  Pallas kernels  16.7 us (24%)
  waiting for transfers between devices  14.6 us (21%)
  local copies, waits for them, and re-layouts  4.28 us (6%)
  between operations  0.93 us (1%)
  other arithmetic  0.88 us (1%)
    ppermute x12, starting transfers between devices, from_behind(): lax.ppermute(value, axis, [(i, (i + by) % devices) for i in range(devices)])  18.8 us
    pallas_call x10, Pallas kernels, call(): pl.pallas_call(kernel, out_shape=[jax.ShapeDtypeStruct(shape, dtype) for...  16.7 us
    ppermute x12, waiting for transfers between devices, from_behind(): lax.ppermute(value, axis, [(i, (i + by) % devices) for i in range(devices)])  12 us
    ppermute x12, starting transfers between devices, swapped(): return lax.ppermute(value, axis, [(0, 1), (1, 0)])  7.76 us
    ppermute x1, starting transfers between devices, body(): above = lax.ppermute(lower, 'tile', up)  4.92 us
    unnamed x18, local copies, waits for them, and re-layouts  3.17 us
    ppermute x12, waiting for transfers between devices, swapped(): return lax.ppermute(value, axis, [(0, 1), (1, 0)])  2.62 us
  transfers between devices with their start and end apart: 26, of which 5 were waited for; matrix products, arithmetic and copies ran while one was open for 6% of the time, Pallas kernels for 22%

profile of v7, /device:TPU:0, one launch (start us, length us, event | category | flops | bytes accessed | tf_op | source)
XLA Modules:
  0.0 70.1 jit_solution(17789710007219049892)
XLA Ops:
  2.8 4.9 %collective-permute-start.2 = (bf16[144,1024]{1,0:T(8,128)(2,1)S(1)}, bf16[144,1024]{1,0:T(8,128)(2,1)S(1)}, u32[]{:S(2)}, u32[]{:S(2)}) collective-permute-start(bf16[144,1024]{1,0:T(8,128)(2,1)S(1)} %bitcast.35), channel_id=1, source_target_pairs={{0,4},{4,8},{8,12},{1,5},{5,9},{9,13},{2,6},{6,10},{10,14},{3,7},{... | collective-permute-start | bytes 884744 | tf_op jit(solution)/shard_map/ppermute | solution.py:467
  9.2 1.5 %copy.10 = bf16[64,8,2,512]{3,1,2,0:T(8,128)(2,1)S(1)} copy(bf16[64,8,2,512]{3,2,1,0:T(2,128)(2,1)} %bitcast.29) | data formatting | bytes 2097152
  11.9 3.1 %shard_map.95 = (bf16[288,512]{1,0:T(8,128)(2,1)S(1)}, f32[288,512]{1,0:T(8,128)S(1)}, f32[288,512]{1,0:T(8,128)S(1)}, f32[288,512]{1,0:T(8,128)S(1)}) custom-call(bf16[288,1024]{1,0:T(8,128)(2,1)S(1)} %bitcast.24, bf16[512,512]{1,0:T(8,128)(2,1)S(1)} %copy-done.3, bf16[512,512]{1,0:T(8,128)(2,1)S(1)} %collective-permute-done.wq_x, ...), custom_call_target="tpu_custom_call" | custom-call | flops 1 | bytes 4915200 | tf_op jit(solution)/shard_map/pallas_call | solution.py:427
  15.0 2.0 %shard_map.96.mine = bf16[144,1024]{1,0:T(8,128)(2,1)S(1)} custom-call(bf16[288,512]{1,0:T(8,128)(2,1)S(1)} %get-tuple-element.40.q_own, f32[288,512]{1,0:T(8,128)S(1)} %get-tuple-element.41.acc, f32[288,512]{1,0:T(8,128)S(1)} %get-tuple-element.42.total, f32[288,512]{1,0:T(8,128)S(1)} %get-tuple-element.43.top, ...), custom_call_target="tpu_custom_call" | custom-call | flops 1132462080 | bytes 4915200 | tf_op jit(solution)/shard_map/pallas_call | solution.py:427
  17.0 1.6 %collective-permute-start.4 = (bf16[144,1024]{1,0:T(8,128)(2,1)S(1)}, bf16[144,1024]{1,0:T(8,128)(2,1)S(1)}, u32[]{:S(2)}, u32[]{:S(2)}) collective-permute-start(bf16[144,1024]{1,0:T(8,128)(2,1)S(1)} %shard_map.96.mine), channel_id=1, source_target_pairs={{0,2},{2,0},{1,3},{3,1},{4,6},{6,4},{5,7},{7,5},{8,10},{10,8},{9,1... | collective-permute-start | bytes 884744 | tf_op jit(solution)/shard_map/ppermute | solution.py:165
  18.6 2.0 %shard_map.98.mine = bf16[144,1024]{1,0:T(8,128)(2,1)S(1)} custom-call(bf16[288,512]{1,0:T(8,128)(2,1)S(1)} %get-tuple-element.40.q_own, f32[288,512]{1,0:T(8,128)S(1)} %get-tuple-element.41.acc, f32[288,512]{1,0:T(8,128)S(1)} %get-tuple-element.42.total, f32[288,512]{1,0:T(8,128)S(1)} %get-tuple-element.43.top, ...), custom_call_target="tpu_custom_call" | custom-call | flops 1132462080 | bytes 4915200 | tf_op jit(solution)/shard_map/pallas_call | solution.py:427
  20.6 1.4 %collective-permute-start.7 = (bf16[144,1024]{1,0:T(8,128)(2,1)S(1)}, bf16[144,1024]{1,0:T(8,128)(2,1)S(1)}, u32[]{:S(2)}, u32[]{:S(2)}) collective-permute-start(bf16[144,1024]{1,0:T(8,128)(2,1)S(1)} %shard_map.98.mine), channel_id=1, source_target_pairs={{0,2},{2,0},{1,3},{3,1},{4,6},{6,4},{5,7},{7,5},{8,10},{10,8},{9,1... | collective-permute-start | bytes 884744 | tf_op jit(solution)/shard_map/ppermute | solution.py:165
  22.8 1.9 %collective-permute-start.12 = (bf16[256,128]{1,0:T(8,128)(2,1)S(1)}, bf16[256,128]{1,0:T(8,128)(2,1)S(1)}, u32[]{:S(2)}, u32[]{:S(2)}) collective-permute-start(bf16[256,128]{1,0:T(8,128)(2,1)S(1)} %get-tuple-element.52), channel_id=1, source_target_pairs={{0,4},{4,8},{8,12},{12,0},{1,5},{5,9},{9,13},{13,1},{2,6},{6,10},{... | collective-permute-start | bytes 196616 | tf_op jit(solution)/shard_map/ppermute | solution.py:21
  24.7 2.6 %collective-permute-start.13 = (bf16[256,128]{1,0:T(8,128)(2,1)S(1)}, bf16[256,128]{1,0:T(8,128)(2,1)S(1)}, u32[]{:S(2)}, u32[]{:S(2)}) collective-permute-start(bf16[256,128]{1,0:T(8,128)(2,1)S(1)} %get-tuple-element.53), channel_id=1, source_target_pairs={{0,8},{4,12},{8,0},{12,4},{1,9},{5,13},{9,1},{13,5},{2,10},{6,14},... | collective-permute-start | bytes 196616 | tf_op jit(solution)/shard_map/ppermute | solution.py:21
  28.6 1.8 %collective-permute-start.8 = (bf16[144,256]{1,0:T(8,128)(2,1)S(1)}, bf16[144,256]{1,0:T(8,128)(2,1)S(1)}, u32[]{:S(2)}, u32[]{:S(2)}) collective-permute-start(bf16[144,256]{1,0:T(8,128)(2,1)S(1)} %get-tuple-element.47), channel_id=1, source_target_pairs={{0,4},{4,8},{8,12},{12,0},{1,5},{5,9},{9,13},{13,1},{2,6},{6,10},{... | collective-permute-start | bytes 221192 | tf_op jit(solution)/shard_map/ppermute | solution.py:21
  30.4 2.6 %collective-permute-start.9 = (bf16[144,256]{1,0:T(8,128)(2,1)S(1)}, bf16[144,256]{1,0:T(8,128)(2,1)S(1)}, u32[]{:S(2)}, u32[]{:S(2)}) collective-permute-start(bf16[144,256]{1,0:T(8,128)(2,1)S(1)} %get-tuple-element.48), channel_id=1, source_target_pairs={{0,8},{4,12},{8,0},{12,4},{1,9},{5,13},{9,1},{13,5},{2,10},{6,14},... | collective-permute-start | bytes 221192 | tf_op jit(solution)/shard_map/ppermute | solution.py:21
  34.8 4.1 %collective-permute-done.14.refs_3_.refs_1_ = bf16[256,128]{1,0:T(8,128)(2,1)S(1)} collective-permute-done((bf16[256,128]{1,0:T(8,128)(2,1)S(1)}, bf16[256,128]{1,0:T(8,128)(2,1)S(1)}, u32[]{:S(2)}, u32[]{:S(2)}) %collective-permute-start.14) | collective-permute-done | bytes 65568 | tf_op jit(solution)/shard_map/ppermute | solution.py:21
  39.0 1.6 %collective-permute-start.24 = (bf16[512,512]{1,0:T(8,128)(2,1)S(1)}, bf16[512,512]{1,0:T(8,128)(2,1)S(1)}, u32[]{:S(2)}, u32[]{:S(2)}) collective-permute-start(bf16[512,512]{1,0:T(8,128)(2,1)S(1)} %copy-done.5), channel_id=1, source_target_pairs={{0,2},{2,0},{1,3},{3,1},{4,6},{6,4},{5,7},{7,5},{8,10},{10,8},{9,1... | collective-permute-start | bytes 1572872 | tf_op jit(solution)/shard_map/ppermute | solution.py:165
  41.4 2.0 %collective-permute-start.15 = (bf16[144,256]{1,0:T(8,128)(2,1)S(1)}, bf16[144,256]{1,0:T(8,128)(2,1)S(1)}, u32[]{:S(2)}, u32[]{:S(2)}) collective-permute-start(bf16[144,256]{1,0:T(8,128)(2,1)S(1)} %get-tuple-element.61), channel_id=1, source_target_pairs={{0,4},{4,8},{8,12},{12,0},{1,5},{5,9},{9,13},{13,1},{2,6},{6,10},{... | collective-permute-start | bytes 221192 | tf_op jit(solution)/shard_map/ppermute | solution.py:21
  44.3 1.4 %collective-permute-start.17 = (bf16[144,256]{1,0:T(8,128)(2,1)S(1)}, bf16[144,256]{1,0:T(8,128)(2,1)S(1)}, u32[]{:S(2)}, u32[]{:S(2)}) collective-permute-start(bf16[144,256]{1,0:T(8,128)(2,1)S(1)} %get-tuple-element.63), channel_id=1, source_target_pairs={{0,12},{4,0},{8,4},{12,8},{1,13},{5,1},{9,5},{13,9},{2,14},{6,2},{... | collective-permute-start | bytes 221192 | tf_op jit(solution)/shard_map/ppermute | solution.py:21
  45.8 2.7 %shard_map.101 = (f32[1024,128]{1,0:T(8,128)S(1)}, f32[1024,128]{1,0:T(8,128)S(1)}, f32[1024,128]{1,0:T(8,128)S(1)}) custom-call(bf16[256,128]{1,0:T(8,128)(2,1)S(1)} %get-tuple-element.73.refs_0_, bf16[256,128]{1,0:T(8,128)(2,1)S(1)} %collective-permute-done.12.refs_1_, bf16[256,128]{1,0:T(8,128)(2,1)S(1)} %collective-permute-done.13.refs_2_.refs_0_, ...), custom_call_target="tpu_custom_call" | custom-call | flops 1 | bytes 1343488 | tf_op jit(solution)/shard_map/pallas_call | solution.py:427
  49.3 1.5 %collective-permute-done.16.refs_4_ = bf16[144,256]{1,0:T(8,128)(2,1)S(1)} collective-permute-done((bf16[144,256]{1,0:T(8,128)(2,1)S(1)}, bf16[144,256]{1,0:T(8,128)(2,1)S(1)}, u32[]{:S(2)}, u32[]{:S(2)}) %collective-permute-start.16) | collective-permute-done | bytes 73760 | tf_op jit(solution)/shard_map/ppermute | solution.py:21
  50.8 1.6 %shard_map.102 = (bf16[256,128]{1,0:T(8,128)(2,1)S(1)}, bf16[256,128]{1,0:T(8,128)(2,1)S(1)}) custom-call(bf16[256,128]{1,0:T(8,128)(2,1)S(1)} %collective-permute-done.13.refs_2_.refs_0_, bf16[256,128]{1,0:T(8,128)(2,1)S(1)} %collective-permute-done.14.refs_3_.refs_1_, bf16[144,256]{1,0:T(8,128)(2,1)S(1)} %get-tuple-element.60.refs_2_, ...), custom_call_target="tpu_custom_call" | custom-call | flops 1 | bytes 1343488 | tf_op jit(solution)/shard_map/pallas_call | solution.py:427
  52.5 1.6 %shard_map.103 = (bf16[256,128]{1,0:T(8,128)(2,1)S(1)}, bf16[256,128]{1,0:T(8,128)(2,1)S(1)}) custom-call(bf16[256,128]{1,0:T(8,128)(2,1)S(1)} %get-tuple-element.73.refs_0_, bf16[256,128]{1,0:T(8,128)(2,1)S(1)} %collective-permute-done.12.refs_1_, bf16[144,256]{1,0:T(8,128)(2,1)S(1)} %get-tuple-element.60.refs_2_, ...), custom_call_target="tpu_custom_call" | custom-call | flops 1 | bytes 1343488 | tf_op jit(solution)/shard_map/pallas_call | solution.py:427
  54.7 1.5 %collective-permute-start.20 = (bf16[256,128]{1,0:T(8,128)(2,1)S(1)}, bf16[256,128]{1,0:T(8,128)(2,1)S(1)}, u32[]{:S(2)}, u32[]{:S(2)}) collective-permute-start(bf16[256,128]{1,0:T(8,128)(2,1)S(1)} %get-tuple-element.76), channel_id=1, source_target_pairs={{0,2},{2,0},{1,3},{3,1},{4,6},{6,4},{5,7},{7,5},{8,10},{10,8},{9,1... | collective-permute-start | bytes 196616 | tf_op jit(solution)/shard_map/ppermute | solution.py:165
  56.2 2.6 %collective-permute-done.18 = bf16[256,128]{1,0:T(8,128)(2,1)S(1)} collective-permute-done((bf16[256,128]{1,0:T(8,128)(2,1)S(1)}, bf16[256,128]{1,0:T(8,128)(2,1)S(1)}, u32[]{:S(2)}, u32[]{:S(2)}) %collective-permute-start.18) | collective-permute-done | bytes 65568 | tf_op jit(solution)/shard_map/ppermute | solution.py:165
  58.8 2.2 %collective-permute-start.19 = (bf16[256,128]{1,0:T(8,128)(2,1)S(1)}, bf16[256,128]{1,0:T(8,128)(2,1)S(1)}, u32[]{:S(2)}, u32[]{:S(2)}) collective-permute-start(bf16[256,128]{1,0:T(8,128)(2,1)S(1)} %pad_maximum_fusion.2), channel_id=1, source_target_pairs={{0,12},{4,0},{8,4},{12,8},{1,13},{5,1},{9,5},{13,9},{2,14},{6,2},{... | collective-permute-start | bytes 196616 | tf_op jit(solution)/shard_map/ppermute | solution.py:21
  61.1 1.5 %collective-permute-start.21 = (bf16[256,128]{1,0:T(8,128)(2,1)S(1)}, bf16[256,128]{1,0:T(8,128)(2,1)S(1)}, u32[]{:S(2)}, u32[]{:S(2)}) collective-permute-start(bf16[256,128]{1,0:T(8,128)(2,1)S(1)} %pad_maximum_fusion.3), channel_id=1, source_target_pairs={{0,8},{4,12},{8,0},{12,4},{1,9},{5,13},{9,1},{13,5},{2,10},{6,14},... | collective-permute-start | bytes 196616 | tf_op jit(solution)/shard_map/ppermute | solution.py:21
  63.2 5.7 %collective-permute-done.21.refs_2_ = bf16[256,128]{1,0:T(8,128)(2,1)S(1)} collective-permute-done((bf16[256,128]{1,0:T(8,128)(2,1)S(1)}, bf16[256,128]{1,0:T(8,128)(2,1)S(1)}, u32[]{:S(2)}, u32[]{:S(2)}) %collective-permute-start.21) | collective-permute-done | bytes 65568 | tf_op jit(solution)/shard_map/ppermute | solution.py:21
  (66 shorter events, 13.9 us)
Async XLA Ops:
  0.6 8.4 %collective-permute-start.1 = (bf16[512,2,512]{2,1,0:T(2,128)(2,1)}, bf16[512,2,512]{2,1,0:T(2,128)(2,1)S(1)}, u32[]{:S(2)}, u32[]{:S(2)}) collective-permute-start(bf16[512,2,512]{2,1,0:T(2,128)(2,1)} %param.11), channel_id=1, source_target_pairs={{0,1},{1,0},{2,3},{3,2},{4,5},{5,4},{6,7},{7,6},{8,9},{9,8},{10,11... | collective-permute-start | bytes 3145736 | tf_op jit(solution)/shard_map/ppermute | solution.py:165
  1.2 6.6 %collective-permute-start = (bf16[512,512]{1,0:T(8,128)(2,1)}, bf16[512,512]{1,0:T(8,128)(2,1)S(1)}, u32[]{:S(2)}, u32[]{:S(2)}) collective-permute-start(bf16[512,512]{1,0:T(8,128)(2,1)} %wq_o.2), channel_id=1, source_target_pairs={{0,1},{1,0},{2,3},{3,2},{4,5},{5,4},{6,7},{7,6},{8,9},{9,8},{10,11... | collective-permute-start | bytes 1572872 | tf_op jit(solution)/shard_map/ppermute | solution.py:165
  1.2 26.3 %collective-permute-start.5 = (bf16[512,2,512]{2,1,0:T(2,128)(2,1)}, bf16[512,2,512]{2,1,0:T(2,128)(2,1)S(1)}, u32[]{:S(2)}, u32[]{:S(2)}) collective-permute-start(bf16[512,2,512]{2,1,0:T(2,128)(2,1)} %param.14), channel_id=1, source_target_pairs={{0,1},{1,0},{2,3},{3,2},{4,5},{5,4},{6,7},{7,6},{8,9},{9,8},{10,11... | collective-permute-start | bytes 3145736 | tf_op jit(solution)/shard_map/ppermute | solution.py:165
  1.7 13.3 %collective-permute-start.3 = (bf16[512,512]{1,0:T(8,128)(2,1)}, bf16[512,512]{1,0:T(8,128)(2,1)S(1)}, u32[]{:S(2)}, u32[]{:S(2)}) collective-permute-start(bf16[512,512]{1,0:T(8,128)(2,1)} %wp_o.3), channel_id=1, source_target_pairs={{0,1},{1,0},{2,3},{3,2},{4,5},{5,4},{6,7},{7,6},{8,9},{9,8},{10,11... | collective-permute-start | bytes 1572872 | tf_op jit(solution)/shard_map/ppermute | solution.py:165
  2.8 12.1 %collective-permute-start.2 = (bf16[144,1024]{1,0:T(8,128)(2,1)S(1)}, bf16[144,1024]{1,0:T(8,128)(2,1)S(1)}, u32[]{:S(2)}, u32[]{:S(2)}) collective-permute-start(bf16[144,1024]{1,0:T(8,128)(2,1)S(1)} %bitcast.35), channel_id=1, source_target_pairs={{0,4},{4,8},{8,12},{1,5},{5,9},{9,13},{2,6},{6,10},{10,14},{3,7},{... | collective-permute-start | bytes 884744 | tf_op jit(solution)/shard_map/ppermute | solution.py:467
  7.8 10.8 %collective-permute-start.6 = (bf16[144,1024]{1,0:T(8,128)(2,1)S(1)}, bf16[144,1024]{1,0:T(8,128)(2,1)S(1)}, u32[]{:S(2)}, u32[]{:S(2)}) collective-permute-start(bf16[144,1024]{1,0:T(8,128)(2,1)S(1)} %bitcast.34), channel_id=1, source_target_pairs={{4,0},{8,4},{12,8},{5,1},{9,5},{13,9},{6,2},{10,6},{14,10},{7,3},{... | collective-permute-start | bytes 884744 | tf_op jit(solution)/shard_map/ppermute | solution.py:468
  9.1 12.9 %collective-permute-start.11 = (bf16[512,512]{1,0:T(8,128)(2,1)S(1)}, bf16[512,512]{1,0:T(8,128)(2,1)S(1)}, u32[]{:S(2)}, u32[]{:S(2)}) collective-permute-start(bf16[512,512]{1,0:T(8,128)(2,1)S(1)} %copy-done.4), channel_id=1, source_target_pairs={{0,1},{1,0},{2,3},{3,2},{4,5},{5,4},{6,7},{7,6},{8,9},{9,8},{10,11... | collective-permute-start | bytes 1572872 | tf_op jit(solution)/shard_map/ppermute | solution.py:165
  17.0 10.8 %collective-permute-start.4 = (bf16[144,1024]{1,0:T(8,128)(2,1)S(1)}, bf16[144,1024]{1,0:T(8,128)(2,1)S(1)}, u32[]{:S(2)}, u32[]{:S(2)}) collective-permute-start(bf16[144,1024]{1,0:T(8,128)(2,1)S(1)} %shard_map.96.mine), channel_id=1, source_target_pairs={{0,2},{2,0},{1,3},{3,1},{4,6},{6,4},{5,7},{7,5},{8,10},{10,8},{9,1... | collective-permute-start | bytes 884744 | tf_op jit(solution)/shard_map/ppermute | solution.py:165
  20.6 18.4 %collective-permute-start.7 = (bf16[144,1024]{1,0:T(8,128)(2,1)S(1)}, bf16[144,1024]{1,0:T(8,128)(2,1)S(1)}, u32[]{:S(2)}, u32[]{:S(2)}) collective-permute-start(bf16[144,1024]{1,0:T(8,128)(2,1)S(1)} %shard_map.98.mine), channel_id=1, source_target_pairs={{0,2},{2,0},{1,3},{3,1},{4,6},{6,4},{5,7},{7,5},{8,10},{10,8},{9,1... | collective-permute-start | bytes 884744 | tf_op jit(solution)/shard_map/ppermute | solution.py:165
  22.8 10.2 %collective-permute-start.12 = (bf16[256,128]{1,0:T(8,128)(2,1)S(1)}, bf16[256,128]{1,0:T(8,128)(2,1)S(1)}, u32[]{:S(2)}, u32[]{:S(2)}) collective-permute-start(bf16[256,128]{1,0:T(8,128)(2,1)S(1)} %get-tuple-element.52), channel_id=1, source_target_pairs={{0,4},{4,8},{8,12},{12,0},{1,5},{5,9},{9,13},{13,1},{2,6},{6,10},{... | collective-permute-start | bytes 196616 | tf_op jit(solution)/shard_map/ppermute | solution.py:21
  24.7 9.6 %collective-permute-start.13 = (bf16[256,128]{1,0:T(8,128)(2,1)S(1)}, bf16[256,128]{1,0:T(8,128)(2,1)S(1)}, u32[]{:S(2)}, u32[]{:S(2)}) collective-permute-start(bf16[256,128]{1,0:T(8,128)(2,1)S(1)} %get-tuple-element.53), channel_id=1, source_target_pairs={{0,8},{4,12},{8,0},{12,4},{1,9},{5,13},{9,1},{13,5},{2,10},{6,14},... | collective-permute-start | bytes 196616 | tf_op jit(solution)/shard_map/ppermute | solution.py:21
  28.6 11.9 %collective-permute-start.8 = (bf16[144,256]{1,0:T(8,128)(2,1)S(1)}, bf16[144,256]{1,0:T(8,128)(2,1)S(1)}, u32[]{:S(2)}, u32[]{:S(2)}) collective-permute-start(bf16[144,256]{1,0:T(8,128)(2,1)S(1)} %get-tuple-element.47), channel_id=1, source_target_pairs={{0,4},{4,8},{8,12},{12,0},{1,5},{5,9},{9,13},{13,1},{2,6},{6,10},{... | collective-permute-start | bytes 221192 | tf_op jit(solution)/shard_map/ppermute | solution.py:21
  30.4 10.1 %collective-permute-start.9 = (bf16[144,256]{1,0:T(8,128)(2,1)S(1)}, bf16[144,256]{1,0:T(8,128)(2,1)S(1)}, u32[]{:S(2)}, u32[]{:S(2)}) collective-permute-start(bf16[144,256]{1,0:T(8,128)(2,1)S(1)} %get-tuple-element.48), channel_id=1, source_target_pairs={{0,8},{4,12},{8,0},{12,4},{1,9},{5,13},{9,1},{13,5},{2,10},{6,14},... | collective-permute-start | bytes 221192 | tf_op jit(solution)/shard_map/ppermute | solution.py:21
  33.0 7.5 %collective-permute-start.10 = (bf16[144,256]{1,0:T(8,128)(2,1)S(1)}, bf16[144,256]{1,0:T(8,128)(2,1)S(1)}, u32[]{:S(2)}, u32[]{:S(2)}) collective-permute-start(bf16[144,256]{1,0:T(8,128)(2,1)S(1)} %get-tuple-element.49), channel_id=1, source_target_pairs={{0,12},{4,0},{8,4},{12,8},{1,13},{5,1},{9,5},{13,9},{2,14},{6,2},{... | collective-permute-start | bytes 221192 | tf_op jit(solution)/shard_map/ppermute | solution.py:21
  39.0 30.0 %collective-permute-start.23 = (bf16[512,512]{1,0:T(8,128)(2,1)S(1)}, bf16[512,512]{1,0:T(8,128)(2,1)S(1)}, u32[]{:S(2)}, u32[]{:S(2)}) collective-permute-start(bf16[512,512]{1,0:T(8,128)(2,1)S(1)} %copy-done.5), channel_id=1, source_target_pairs={{0,1},{1,0},{2,3},{3,2},{4,5},{5,4},{6,7},{7,6},{8,9},{9,8},{10,11... | collective-permute-start | bytes 1572872 | tf_op jit(solution)/shard_map/ppermute | solution.py:165
  39.0 22.1 %collective-permute-start.24 = (bf16[512,512]{1,0:T(8,128)(2,1)S(1)}, bf16[512,512]{1,0:T(8,128)(2,1)S(1)}, u32[]{:S(2)}, u32[]{:S(2)}) collective-permute-start(bf16[512,512]{1,0:T(8,128)(2,1)S(1)} %copy-done.5), channel_id=1, source_target_pairs={{0,2},{2,0},{1,3},{3,1},{4,6},{6,4},{5,7},{7,5},{8,10},{10,8},{9,1... | collective-permute-start | bytes 1572872 | tf_op jit(solution)/shard_map/ppermute | solution.py:165
  41.4 8.0 %collective-permute-start.15 = (bf16[144,256]{1,0:T(8,128)(2,1)S(1)}, bf16[144,256]{1,0:T(8,128)(2,1)S(1)}, u32[]{:S(2)}, u32[]{:S(2)}) collective-permute-start(bf16[144,256]{1,0:T(8,128)(2,1)S(1)} %get-tuple-element.61), channel_id=1, source_target_pairs={{0,4},{4,8},{8,12},{12,0},{1,5},{5,9},{9,13},{13,1},{2,6},{6,10},{... | collective-permute-start | bytes 221192 | tf_op jit(solution)/shard_map/ppermute | solution.py:21
  43.3 7.5 %collective-permute-start.16 = (bf16[144,256]{1,0:T(8,128)(2,1)S(1)}, bf16[144,256]{1,0:T(8,128)(2,1)S(1)}, u32[]{:S(2)}, u32[]{:S(2)}) collective-permute-start(bf16[144,256]{1,0:T(8,128)(2,1)S(1)} %get-tuple-element.62), channel_id=1, source_target_pairs={{0,8},{4,12},{8,0},{12,4},{1,9},{5,13},{9,1},{13,5},{2,10},{6,14},... | collective-permute-start | bytes 221192 | tf_op jit(solution)/shard_map/ppermute | solution.py:21
  44.3 6.5 %collective-permute-start.17 = (bf16[144,256]{1,0:T(8,128)(2,1)S(1)}, bf16[144,256]{1,0:T(8,128)(2,1)S(1)}, u32[]{:S(2)}, u32[]{:S(2)}) collective-permute-start(bf16[144,256]{1,0:T(8,128)(2,1)S(1)} %get-tuple-element.63), channel_id=1, source_target_pairs={{0,12},{4,0},{8,4},{12,8},{1,13},{5,1},{9,5},{13,9},{2,14},{6,2},{... | collective-permute-start | bytes 221192 | tf_op jit(solution)/shard_map/ppermute | solution.py:21
  54.1 4.7 %collective-permute-start.18 = (bf16[256,128]{1,0:T(8,128)(2,1)S(1)}, bf16[256,128]{1,0:T(8,128)(2,1)S(1)}, u32[]{:S(2)}, u32[]{:S(2)}) collective-permute-start(bf16[256,128]{1,0:T(8,128)(2,1)S(1)} %get-tuple-element.75), channel_id=1, source_target_pairs={{0,2},{2,0},{1,3},{3,1},{4,6},{6,4},{5,7},{7,5},{8,10},{10,8},{9,1... | collective-permute-start | bytes 196616 | tf_op jit(solution)/shard_map/ppermute | solution.py:165
  54.7 6.4 %collective-permute-start.20 = (bf16[256,128]{1,0:T(8,128)(2,1)S(1)}, bf16[256,128]{1,0:T(8,128)(2,1)S(1)}, u32[]{:S(2)}, u32[]{:S(2)}) collective-permute-start(bf16[256,128]{1,0:T(8,128)(2,1)S(1)} %get-tuple-element.76), channel_id=1, source_target_pairs={{0,2},{2,0},{1,3},{3,1},{4,6},{6,4},{5,7},{7,5},{8,10},{10,8},{9,1... | collective-permute-start | bytes 196616 | tf_op jit(solution)/shard_map/ppermute | solution.py:165
  61.1 7.9 %collective-permute-start.25 = (bf16[512,512]{1,0:T(8,128)(2,1)S(1)}, bf16[512,512]{1,0:T(8,128)(2,1)S(1)}, u32[]{:S(2)}, u32[]{:S(2)}) collective-permute-start(bf16[512,512]{1,0:T(8,128)(2,1)S(1)} %collective-permute-done.24.refs_6_), channel_id=1, source_target_pairs={{0,1},{1,0},{2,3},{3,2},{4,5},{5,4},{6,7},{7,6},{8,9},{9,8},{10,11... | collective-permute-start | bytes 1572872 | tf_op jit(solution)/shard_map/ppermute | solution.py:165
  61.1 7.8 %collective-permute-start.21 = (bf16[256,128]{1,0:T(8,128)(2,1)S(1)}, bf16[256,128]{1,0:T(8,128)(2,1)S(1)}, u32[]{:S(2)}, u32[]{:S(2)}) collective-permute-start(bf16[256,128]{1,0:T(8,128)(2,1)S(1)} %pad_maximum_fusion.3), channel_id=1, source_target_pairs={{0,8},{4,12},{8,0},{12,4},{1,9},{5,13},{9,1},{13,5},{2,10},{6,14},... | collective-permute-start | bytes 196616 | tf_op jit(solution)/shard_map/ppermute | solution.py:21
  62.6 6.3 %collective-permute-start.22 = (bf16[256,128]{1,0:T(8,128)(2,1)S(1)}, bf16[256,128]{1,0:T(8,128)(2,1)S(1)}, u32[]{:S(2)}, u32[]{:S(2)}) collective-permute-start(bf16[256,128]{1,0:T(8,128)(2,1)S(1)} %pad_maximum_fusion.4), channel_id=1, source_target_pairs={{0,4},{4,8},{8,12},{12,0},{1,5},{5,9},{9,13},{13,1},{2,6},{6,10},{... | collective-permute-start | bytes 196616 | tf_op jit(solution)/shard_map/ppermute | solution.py:21
  (9 other events, 45.7 us)

commit v8 on v7

--- a/solution.py
+++ b/solution.py
@@ -469,7 +469,6 @@
     wkv_x = swapped(enc_keyval, "batch").reshape(width // 2, 2 * hq_enc)
     wkv_enc = enc_keyval.reshape(width // 2, 2 * hq_enc)
     wq_x = swapped(enc_query, "batch")
-    dq_x = swapped(dec_query, "batch")
     dkv_x = swapped(dec_keyval, "batch").reshape(width // 2, 2 * hq_dec)
     wkv_dec = dec_keyval.reshape(width // 2, 2 * hq_dec)
 
@@ -489,6 +488,7 @@
         wkv_enc,
         wkv_x,
     )
+    dq_x = swapped(after(dec_query, q_own), "batch")
     q_out = call(
         query_kernel,
         1,
@@ -541,7 +541,7 @@
     theirs_a = swapped(part_a, "mp")
     part_b = window_half(1, after(below, part_a))
     theirs_b = swapped(part_b, "mp")
-    encoded_a, *kv_a = key_values(0, part_a, theirs_a)
+    encoded_a, *kv_a = key_values(0, part_a, after(theirs_a, *q_out))
     kv_a = [kv_a[0]] + [from_behind(kv_a[s], "tile", s) for s in range(1, tiles)]
     theirs_b, kv_a, q_in = lax.optimization_barrier((theirs_b, kv_a, q_in))
     encoded_b, *kv_b = key_values(1, part_b, theirs_b)

time: 70.4 us -> 71.9 us (1.021)
  waiting for transfers between devices: 14.6 us -> 17.2 us
  local copies, waits for them, and re-layouts: 4.28 us -> 3.05 us
    unnamed x18 -> x20, local copies, waits for them, and re-layouts: 3.17 us -> 1.94 us
    ppermute x12, waiting for transfers between devices: 2.62 us -> 3.58 us  [swapped(): return lax.ppermute(value, axis, [(0, 1), (1, 0)])]
  transfers between devices with their start and end apart: 26 -> 26, of which waited for: 5 -> 8; matrix products, arithmetic and copies ran while one was open for 6% -> 4% of each run, Pallas kernels for 22% -> 22%
where the time goes in v8:
time: 71.9 us; the launch traced here: 71.7 us
  starting transfers between devices  33.1 us (46%)
  waiting for transfers between devices  17.2 us (24%)
  Pallas kernels  16.6 us (23%)
  local copies, waits for them, and re-layouts  3.05 us (4%)
  between operations  0.89 us (1%)
  other arithmetic  0.88 us (1%)
    ppermute x12, starting transfers between devices, from_behind(): lax.ppermute(value, axis, [(i, (i + by) % devices) for i in range(devices)])  18.9 us
    pallas_call x10, Pallas kernels, call(): pl.pallas_call(kernel, out_shape=[jax.ShapeDtypeStruct(shape, dtype) for...  16.6 us
    ppermute x12, waiting for transfers between devices, from_behind(): lax.ppermute(value, axis, [(i, (i + by) % devices) for i in range(devices)])  12.6 us
    ppermute x12, starting transfers between devices, swapped(): return lax.ppermute(value, axis, [(0, 1), (1, 0)])  7.96 us
    ppermute x1, starting transfers between devices, body(): above = lax.ppermute(lower, 'tile', up)  4.93 us
    ppermute x12, waiting for transfers between devices, swapped(): return lax.ppermute(value, axis, [(0, 1), (1, 0)])  3.58 us
    unnamed x20, local copies, waits for them, and re-layouts  1.94 us
  transfers between devices with their start and end apart: 26, of which 8 were waited for; matrix products, arithmetic and copies ran while one was open for 4% of the time, Pallas kernels for 22%

profile of v8, /device:TPU:0, one launch (start us, length us, event | category | flops | bytes accessed | tf_op | source)
XLA Modules:
  0.0 71.7 jit_solution(17573149042559849671)
XLA Ops:
  2.8 4.9 %collective-permute-start.2 = (bf16[144,1024]{1,0:T(8,128)(2,1)S(1)}, bf16[144,1024]{1,0:T(8,128)(2,1)S(1)}, u32[]{:S(2)}, u32[]{:S(2)}) collective-permute-start(bf16[144,1024]{1,0:T(8,128)(2,1)S(1)} %bitcast.35), channel_id=1, source_target_pairs={{0,4},{4,8},{8,12},{1,5},{5,9},{9,13},{2,6},{6,10},{10,14},{3,7},{... | collective-permute-start | bytes 884744 | tf_op jit(solution)/shard_map/ppermute | solution.py:467
  10.6 3.1 %shard_map.95 = (bf16[288,512]{1,0:T(8,128)(2,1)S(1)}, f32[288,512]{1,0:T(8,128)S(1)}, f32[288,512]{1,0:T(8,128)S(1)}, f32[288,512]{1,0:T(8,128)S(1)}) custom-call(bf16[288,1024]{1,0:T(8,128)(2,1)S(1)} %bitcast.24, bf16[512,512]{1,0:T(8,128)(2,1)S(1)} %copy-done.3, bf16[512,512]{1,0:T(8,128)(2,1)S(1)} %collective-permute-done.wq_x, ...), custom_call_target="tpu_custom_call" | custom-call | flops 1 | bytes 4915200 | tf_op jit(solution)/shard_map/pallas_call | solution.py:427
  14.3 2.0 %shard_map.96.mine = bf16[144,1024]{1,0:T(8,128)(2,1)S(1)} custom-call(bf16[288,512]{1,0:T(8,128)(2,1)S(1)} %get-tuple-element.42.q_own, f32[288,512]{1,0:T(8,128)S(1)} %get-tuple-element.43.acc, f32[288,512]{1,0:T(8,128)S(1)} %get-tuple-element.44.total, f32[288,512]{1,0:T(8,128)S(1)} %get-tuple-element.45.top, ...), custom_call_target="tpu_custom_call" | custom-call | flops 1132462080 | bytes 4915200 | tf_op jit(solution)/shard_map/pallas_call | solution.py:427
  16.3 1.6 %collective-permute-start.4 = (bf16[144,1024]{1,0:T(8,128)(2,1)S(1)}, bf16[144,1024]{1,0:T(8,128)(2,1)S(1)}, u32[]{:S(2)}, u32[]{:S(2)}) collective-permute-start(bf16[144,1024]{1,0:T(8,128)(2,1)S(1)} %shard_map.96.mine), channel_id=1, source_target_pairs={{0,2},{2,0},{1,3},{3,1},{4,6},{6,4},{5,7},{7,5},{8,10},{10,8},{9,1... | collective-permute-start | bytes 884744 | tf_op jit(solution)/shard_map/ppermute | solution.py:165
  18.4 2.0 %shard_map.99.mine = bf16[144,1024]{1,0:T(8,128)(2,1)S(1)} custom-call(bf16[288,512]{1,0:T(8,128)(2,1)S(1)} %get-tuple-element.42.q_own, f32[288,512]{1,0:T(8,128)S(1)} %get-tuple-element.43.acc, f32[288,512]{1,0:T(8,128)S(1)} %get-tuple-element.44.total, f32[288,512]{1,0:T(8,128)S(1)} %get-tuple-element.45.top, ...), custom_call_target="tpu_custom_call" | custom-call | flops 1132462080 | bytes 4915200 | tf_op jit(solution)/shard_map/pallas_call | solution.py:427
  20.4 1.6 %collective-permute-start.8 = (bf16[144,1024]{1,0:T(8,128)(2,1)S(1)}, bf16[144,1024]{1,0:T(8,128)(2,1)S(1)}, u32[]{:S(2)}, u32[]{:S(2)}) collective-permute-start(bf16[144,1024]{1,0:T(8,128)(2,1)S(1)} %shard_map.99.mine), channel_id=1, source_target_pairs={{0,2},{2,0},{1,3},{3,1},{4,6},{6,4},{5,7},{7,5},{8,10},{10,8},{9,1... | collective-permute-start | bytes 884744 | tf_op jit(solution)/shard_map/ppermute | solution.py:165
  22.8 1.6 %collective-permute-start.12 = (bf16[256,128]{1,0:T(8,128)(2,1)S(1)}, bf16[256,128]{1,0:T(8,128)(2,1)S(1)}, u32[]{:S(2)}, u32[]{:S(2)}) collective-permute-start(bf16[256,128]{1,0:T(8,128)(2,1)S(1)} %get-tuple-element.49), channel_id=1, source_target_pairs={{0,4},{4,8},{8,12},{12,0},{1,5},{5,9},{9,13},{13,1},{2,6},{6,10},{... | collective-permute-start | bytes 196616 | tf_op jit(solution)/shard_map/ppermute | solution.py:21
  24.9 1.3 %collective-permute-done.4.theirs = bf16[144,1024]{1,0:T(8,128)(2,1)S(1)} collective-permute-done((bf16[144,1024]{1,0:T(8,128)(2,1)S(1)}, bf16[144,1024]{1,0:T(8,128)(2,1)S(1)}, u32[]{:S(2)}, u32[]{:S(2)}) %collective-permute-start.4) | collective-permute-done | bytes 294944 | tf_op jit(solution)/shard_map/ppermute | solution.py:165
  27.0 2.5 %collective-permute-start.9 = (bf16[144,256]{1,0:T(8,128)(2,1)S(1)}, bf16[144,256]{1,0:T(8,128)(2,1)S(1)}, u32[]{:S(2)}, u32[]{:S(2)}) collective-permute-start(bf16[144,256]{1,0:T(8,128)(2,1)S(1)} %get-tuple-element.56), channel_id=1, source_target_pairs={{0,4},{4,8},{8,12},{12,0},{1,5},{5,9},{9,13},{13,1},{2,6},{6,10},{... | collective-permute-start | bytes 221192 | tf_op jit(solution)/shard_map/ppermute | solution.py:21
  29.5 2.6 %collective-permute-start.10 = (bf16[144,256]{1,0:T(8,128)(2,1)S(1)}, bf16[144,256]{1,0:T(8,128)(2,1)S(1)}, u32[]{:S(2)}, u32[]{:S(2)}) collective-permute-start(bf16[144,256]{1,0:T(8,128)(2,1)S(1)} %get-tuple-element.57), channel_id=1, source_target_pairs={{0,8},{4,12},{8,0},{12,4},{1,9},{5,13},{9,1},{13,5},{2,10},{6,14},... | collective-permute-start | bytes 221192 | tf_op jit(solution)/shard_map/ppermute | solution.py:21
  32.1 1.4 %collective-permute-start.11 = (bf16[144,256]{1,0:T(8,128)(2,1)S(1)}, bf16[144,256]{1,0:T(8,128)(2,1)S(1)}, u32[]{:S(2)}, u32[]{:S(2)}) collective-permute-start(bf16[144,256]{1,0:T(8,128)(2,1)S(1)} %get-tuple-element.58), channel_id=1, source_target_pairs={{0,12},{4,0},{8,4},{12,8},{1,13},{5,1},{9,5},{13,9},{2,14},{6,2},{... | collective-permute-start | bytes 221192 | tf_op jit(solution)/shard_map/ppermute | solution.py:21
  33.5 1.7 %collective-permute-start.13 = (bf16[256,128]{1,0:T(8,128)(2,1)S(1)}, bf16[256,128]{1,0:T(8,128)(2,1)S(1)}, u32[]{:S(2)}, u32[]{:S(2)}) collective-permute-start(bf16[256,128]{1,0:T(8,128)(2,1)S(1)} %get-tuple-element.50), channel_id=1, source_target_pairs={{0,8},{4,12},{8,0},{12,4},{1,9},{5,13},{9,1},{13,5},{2,10},{6,14},... | collective-permute-start | bytes 196616 | tf_op jit(solution)/shard_map/ppermute | solution.py:21
  35.2 1.4 %collective-permute-start.14 = (bf16[256,128]{1,0:T(8,128)(2,1)S(1)}, bf16[256,128]{1,0:T(8,128)(2,1)S(1)}, u32[]{:S(2)}, u32[]{:S(2)}) collective-permute-start(bf16[256,128]{1,0:T(8,128)(2,1)S(1)} %get-tuple-element.51), channel_id=1, source_target_pairs={{0,12},{4,0},{8,4},{12,8},{1,13},{5,1},{9,5},{13,9},{2,14},{6,2},{... | collective-permute-start | bytes 196616 | tf_op jit(solution)/shard_map/ppermute | solution.py:21
  36.6 4.2 %collective-permute-done.13.refs_2_.refs_0_ = bf16[256,128]{1,0:T(8,128)(2,1)S(1)} collective-permute-done((bf16[256,128]{1,0:T(8,128)(2,1)S(1)}, bf16[256,128]{1,0:T(8,128)(2,1)S(1)}, u32[]{:S(2)}, u32[]{:S(2)}) %collective-permute-start.13) | collective-permute-done | bytes 65568 | tf_op jit(solution)/shard_map/ppermute | solution.py:21
  40.8 1.6 %collective-permute-start.24 = (bf16[512,512]{1,0:T(8,128)(2,1)S(1)}, bf16[512,512]{1,0:T(8,128)(2,1)S(1)}, u32[]{:S(2)}, u32[]{:S(2)}) collective-permute-start(bf16[512,512]{1,0:T(8,128)(2,1)S(1)} %copy-done.5), channel_id=1, source_target_pairs={{0,2},{2,0},{1,3},{3,1},{4,6},{6,4},{5,7},{7,5},{8,10},{10,8},{9,1... | collective-permute-start | bytes 1572872 | tf_op jit(solution)/shard_map/ppermute | solution.py:165
  44.5 2.4 %collective-permute-start.16 = (bf16[144,256]{1,0:T(8,128)(2,1)S(1)}, bf16[144,256]{1,0:T(8,128)(2,1)S(1)}, u32[]{:S(2)}, u32[]{:S(2)}) collective-permute-start(bf16[144,256]{1,0:T(8,128)(2,1)S(1)} %get-tuple-element.66), channel_id=1, source_target_pairs={{0,8},{4,12},{8,0},{12,4},{1,9},{5,13},{9,1},{13,5},{2,10},{6,14},... | collective-permute-start | bytes 221192 | tf_op jit(solution)/shard_map/ppermute | solution.py:21
  47.1 2.7 %shard_map.101 = (f32[1024,128]{1,0:T(8,128)S(1)}, f32[1024,128]{1,0:T(8,128)S(1)}, f32[1024,128]{1,0:T(8,128)S(1)}) custom-call(bf16[256,128]{1,0:T(8,128)(2,1)S(1)} %get-tuple-element.77.refs_0_, bf16[256,128]{1,0:T(8,128)(2,1)S(1)} %collective-permute-done.12.refs_1_, bf16[256,128]{1,0:T(8,128)(2,1)S(1)} %collective-permute-done.13.refs_2_.refs_0_, ...), custom_call_target="tpu_custom_call" | custom-call | flops 1 | bytes 1343488 | tf_op jit(solution)/shard_map/pallas_call | solution.py:427
  50.7 2.0 %collective-permute-done.16.refs_4_ = bf16[144,256]{1,0:T(8,128)(2,1)S(1)} collective-permute-done((bf16[144,256]{1,0:T(8,128)(2,1)S(1)}, bf16[144,256]{1,0:T(8,128)(2,1)S(1)}, u32[]{:S(2)}, u32[]{:S(2)}) %collective-permute-start.16) | collective-permute-done | bytes 73760 | tf_op jit(solution)/shard_map/ppermute | solution.py:21
  52.7 1.6 %shard_map.102 = (bf16[256,128]{1,0:T(8,128)(2,1)S(1)}, bf16[256,128]{1,0:T(8,128)(2,1)S(1)}) custom-call(bf16[256,128]{1,0:T(8,128)(2,1)S(1)} %collective-permute-done.13.refs_2_.refs_0_, bf16[256,128]{1,0:T(8,128)(2,1)S(1)} %collective-permute-done.14.refs_3_.refs_1_, bf16[144,256]{1,0:T(8,128)(2,1)S(1)} %get-tuple-element.64.refs_2_, ...), custom_call_target="tpu_custom_call" | custom-call | flops 1 | bytes 1343488 | tf_op jit(solution)/shard_map/pallas_call | solution.py:427
  54.3 1.6 %shard_map.103 = (bf16[256,128]{1,0:T(8,128)(2,1)S(1)}, bf16[256,128]{1,0:T(8,128)(2,1)S(1)}) custom-call(bf16[256,128]{1,0:T(8,128)(2,1)S(1)} %get-tuple-element.77.refs_0_, bf16[256,128]{1,0:T(8,128)(2,1)S(1)} %collective-permute-done.12.refs_1_, bf16[144,256]{1,0:T(8,128)(2,1)S(1)} %get-tuple-element.64.refs_2_, ...), custom_call_target="tpu_custom_call" | custom-call | flops 1 | bytes 1343488 | tf_op jit(solution)/shard_map/pallas_call | solution.py:427
  56.6 1.5 %collective-permute-start.20 = (bf16[256,128]{1,0:T(8,128)(2,1)S(1)}, bf16[256,128]{1,0:T(8,128)(2,1)S(1)}, u32[]{:S(2)}, u32[]{:S(2)}) collective-permute-start(bf16[256,128]{1,0:T(8,128)(2,1)S(1)} %get-tuple-element.80), channel_id=1, source_target_pairs={{0,2},{2,0},{1,3},{3,1},{4,6},{6,4},{5,7},{7,5},{8,10},{10,8},{9,1... | collective-permute-start | bytes 196616 | tf_op jit(solution)/shard_map/ppermute | solution.py:165
  58.1 2.2 %collective-permute-done.18 = bf16[256,128]{1,0:T(8,128)(2,1)S(1)} collective-permute-done((bf16[256,128]{1,0:T(8,128)(2,1)S(1)}, bf16[256,128]{1,0:T(8,128)(2,1)S(1)}, u32[]{:S(2)}, u32[]{:S(2)}) %collective-permute-start.18) | collective-permute-done | bytes 65568 | tf_op jit(solution)/shard_map/ppermute | solution.py:165
  60.3 2.6 %collective-permute-start.19 = (bf16[256,128]{1,0:T(8,128)(2,1)S(1)}, bf16[256,128]{1,0:T(8,128)(2,1)S(1)}, u32[]{:S(2)}, u32[]{:S(2)}) collective-permute-start(bf16[256,128]{1,0:T(8,128)(2,1)S(1)} %pad_maximum_fusion.2), channel_id=1, source_target_pairs={{0,12},{4,0},{8,4},{12,8},{1,13},{5,1},{9,5},{13,9},{2,14},{6,2},{... | collective-permute-start | bytes 196616 | tf_op jit(solution)/shard_map/ppermute | solution.py:21
  64.9 5.6 %collective-permute-done.21.refs_2_ = bf16[256,128]{1,0:T(8,128)(2,1)S(1)} collective-permute-done((bf16[256,128]{1,0:T(8,128)(2,1)S(1)}, bf16[256,128]{1,0:T(8,128)(2,1)S(1)}, u32[]{:S(2)}, u32[]{:S(2)}) %collective-permute-start.21) | collective-permute-done | bytes 65568 | tf_op jit(solution)/shard_map/ppermute | solution.py:21
  (68 shorter events, 15.1 us)
Async XLA Ops:
  0.6 7.1 %collective-permute-start.1 = (bf16[512,2,512]{2,1,0:T(2,128)(2,1)}, bf16[512,2,512]{2,1,0:T(2,128)(2,1)S(1)}, u32[]{:S(2)}, u32[]{:S(2)}) collective-permute-start(bf16[512,2,512]{2,1,0:T(2,128)(2,1)} %param.11), channel_id=1, source_target_pairs={{0,1},{1,0},{2,3},{3,2},{4,5},{5,4},{6,7},{7,6},{8,9},{9,8},{10,11... | collective-permute-start | bytes 3145736 | tf_op jit(solution)/shard_map/ppermute | solution.py:165
  1.2 8.5 %collective-permute-start = (bf16[512,512]{1,0:T(8,128)(2,1)}, bf16[512,512]{1,0:T(8,128)(2,1)S(1)}, u32[]{:S(2)}, u32[]{:S(2)}) collective-permute-start(bf16[512,512]{1,0:T(8,128)(2,1)} %wq_o.2), channel_id=1, source_target_pairs={{0,1},{1,0},{2,3},{3,2},{4,5},{5,4},{6,7},{7,6},{8,9},{9,8},{10,11... | collective-permute-start | bytes 1572872 | tf_op jit(solution)/shard_map/ppermute | solution.py:165
  1.2 23.4 %collective-permute-start.6 = (bf16[512,2,512]{2,1,0:T(2,128)(2,1)}, bf16[512,2,512]{2,1,0:T(2,128)(2,1)S(1)}, u32[]{:S(2)}, u32[]{:S(2)}) collective-permute-start(bf16[512,2,512]{2,1,0:T(2,128)(2,1)} %param.14), channel_id=1, source_target_pairs={{0,1},{1,0},{2,3},{3,2},{4,5},{5,4},{6,7},{7,6},{8,9},{9,8},{10,11... | collective-permute-start | bytes 3145736 | tf_op jit(solution)/shard_map/ppermute | solution.py:165
  1.7 12.6 %collective-permute-start.3 = (bf16[512,512]{1,0:T(8,128)(2,1)}, bf16[512,512]{1,0:T(8,128)(2,1)S(1)}, u32[]{:S(2)}, u32[]{:S(2)}) collective-permute-start(bf16[512,512]{1,0:T(8,128)(2,1)} %wp_o.3), channel_id=1, source_target_pairs={{0,1},{1,0},{2,3},{3,2},{4,5},{5,4},{6,7},{7,6},{8,9},{9,8},{10,11... | collective-permute-start | bytes 1572872 | tf_op jit(solution)/shard_map/ppermute | solution.py:165
  2.8 11.4 %collective-permute-start.2 = (bf16[144,1024]{1,0:T(8,128)(2,1)S(1)}, bf16[144,1024]{1,0:T(8,128)(2,1)S(1)}, u32[]{:S(2)}, u32[]{:S(2)}) collective-permute-start(bf16[144,1024]{1,0:T(8,128)(2,1)S(1)} %bitcast.35), channel_id=1, source_target_pairs={{0,4},{4,8},{8,12},{1,5},{5,9},{9,13},{2,6},{6,10},{10,14},{3,7},{... | collective-permute-start | bytes 884744 | tf_op jit(solution)/shard_map/ppermute | solution.py:467
  7.8 10.6 %collective-permute-start.7 = (bf16[144,1024]{1,0:T(8,128)(2,1)S(1)}, bf16[144,1024]{1,0:T(8,128)(2,1)S(1)}, u32[]{:S(2)}, u32[]{:S(2)}) collective-permute-start(bf16[144,1024]{1,0:T(8,128)(2,1)S(1)} %bitcast.34), channel_id=1, source_target_pairs={{4,0},{8,4},{12,8},{5,1},{9,5},{13,9},{6,2},{10,6},{14,10},{7,3},{... | collective-permute-start | bytes 884744 | tf_op jit(solution)/shard_map/ppermute | solution.py:468
  13.7 8.3 %collective-permute-start.5 = (bf16[512,512]{1,0:T(8,128)(2,1)S(1)}, bf16[512,512]{1,0:T(8,128)(2,1)S(1)}, u32[]{:S(2)}, u32[]{:S(2)}) collective-permute-start(bf16[512,512]{1,0:T(8,128)(2,1)S(1)} %copy-done.4), channel_id=1, source_target_pairs={{0,1},{1,0},{2,3},{3,2},{4,5},{5,4},{6,7},{7,6},{8,9},{9,8},{10,11... | collective-permute-start | bytes 1572872 | tf_op jit(solution)/shard_map/ppermute | solution.py:165
  16.3 9.9 %collective-permute-start.4 = (bf16[144,1024]{1,0:T(8,128)(2,1)S(1)}, bf16[144,1024]{1,0:T(8,128)(2,1)S(1)}, u32[]{:S(2)}, u32[]{:S(2)}) collective-permute-start(bf16[144,1024]{1,0:T(8,128)(2,1)S(1)} %shard_map.96.mine), channel_id=1, source_target_pairs={{0,2},{2,0},{1,3},{3,1},{4,6},{6,4},{5,7},{7,5},{8,10},{10,8},{9,1... | collective-permute-start | bytes 884744 | tf_op jit(solution)/shard_map/ppermute | solution.py:165
  20.4 13.1 %collective-permute-start.8 = (bf16[144,1024]{1,0:T(8,128)(2,1)S(1)}, bf16[144,1024]{1,0:T(8,128)(2,1)S(1)}, u32[]{:S(2)}, u32[]{:S(2)}) collective-permute-start(bf16[144,1024]{1,0:T(8,128)(2,1)S(1)} %shard_map.99.mine), channel_id=1, source_target_pairs={{0,2},{2,0},{1,3},{3,1},{4,6},{6,4},{5,7},{7,5},{8,10},{10,8},{9,1... | collective-permute-start | bytes 884744 | tf_op jit(solution)/shard_map/ppermute | solution.py:165
  22.8 12.5 %collective-permute-start.12 = (bf16[256,128]{1,0:T(8,128)(2,1)S(1)}, bf16[256,128]{1,0:T(8,128)(2,1)S(1)}, u32[]{:S(2)}, u32[]{:S(2)}) collective-permute-start(bf16[256,128]{1,0:T(8,128)(2,1)S(1)} %get-tuple-element.49), channel_id=1, source_target_pairs={{0,4},{4,8},{8,12},{12,0},{1,5},{5,9},{9,13},{13,1},{2,6},{6,10},{... | collective-permute-start | bytes 196616 | tf_op jit(solution)/shard_map/ppermute | solution.py:21
  27.0 15.4 %collective-permute-start.9 = (bf16[144,256]{1,0:T(8,128)(2,1)S(1)}, bf16[144,256]{1,0:T(8,128)(2,1)S(1)}, u32[]{:S(2)}, u32[]{:S(2)}) collective-permute-start(bf16[144,256]{1,0:T(8,128)(2,1)S(1)} %get-tuple-element.56), channel_id=1, source_target_pairs={{0,4},{4,8},{8,12},{12,0},{1,5},{5,9},{9,13},{13,1},{2,6},{6,10},{... | collective-permute-start | bytes 221192 | tf_op jit(solution)/shard_map/ppermute | solution.py:21
  29.5 12.9 %collective-permute-start.10 = (bf16[144,256]{1,0:T(8,128)(2,1)S(1)}, bf16[144,256]{1,0:T(8,128)(2,1)S(1)}, u32[]{:S(2)}, u32[]{:S(2)}) collective-permute-start(bf16[144,256]{1,0:T(8,128)(2,1)S(1)} %get-tuple-element.57), channel_id=1, source_target_pairs={{0,8},{4,12},{8,0},{12,4},{1,9},{5,13},{9,1},{13,5},{2,10},{6,14},... | collective-permute-start | bytes 221192 | tf_op jit(solution)/shard_map/ppermute | solution.py:21
  32.1 10.3 %collective-permute-start.11 = (bf16[144,256]{1,0:T(8,128)(2,1)S(1)}, bf16[144,256]{1,0:T(8,128)(2,1)S(1)}, u32[]{:S(2)}, u32[]{:S(2)}) collective-permute-start(bf16[144,256]{1,0:T(8,128)(2,1)S(1)} %get-tuple-element.58), channel_id=1, source_target_pairs={{0,12},{4,0},{8,4},{12,8},{1,13},{5,1},{9,5},{13,9},{2,14},{6,2},{... | collective-permute-start | bytes 221192 | tf_op jit(solution)/shard_map/ppermute | solution.py:21
  33.5 7.3 %collective-permute-start.13 = (bf16[256,128]{1,0:T(8,128)(2,1)S(1)}, bf16[256,128]{1,0:T(8,128)(2,1)S(1)}, u32[]{:S(2)}, u32[]{:S(2)}) collective-permute-start(bf16[256,128]{1,0:T(8,128)(2,1)S(1)} %get-tuple-element.50), channel_id=1, source_target_pairs={{0,8},{4,12},{8,0},{12,4},{1,9},{5,13},{9,1},{13,5},{2,10},{6,14},... | collective-permute-start | bytes 196616 | tf_op jit(solution)/shard_map/ppermute | solution.py:21
  35.2 5.6 %collective-permute-start.14 = (bf16[256,128]{1,0:T(8,128)(2,1)S(1)}, bf16[256,128]{1,0:T(8,128)(2,1)S(1)}, u32[]{:S(2)}, u32[]{:S(2)}) collective-permute-start(bf16[256,128]{1,0:T(8,128)(2,1)S(1)} %get-tuple-element.51), channel_id=1, source_target_pairs={{0,12},{4,0},{8,4},{12,8},{1,13},{5,1},{9,5},{13,9},{2,14},{6,2},{... | collective-permute-start | bytes 196616 | tf_op jit(solution)/shard_map/ppermute | solution.py:21
  40.8 29.7 %collective-permute-start.23 = (bf16[512,512]{1,0:T(8,128)(2,1)S(1)}, bf16[512,512]{1,0:T(8,128)(2,1)S(1)}, u32[]{:S(2)}, u32[]{:S(2)}) collective-permute-start(bf16[512,512]{1,0:T(8,128)(2,1)S(1)} %copy-done.5), channel_id=1, source_target_pairs={{0,1},{1,0},{2,3},{3,2},{4,5},{5,4},{6,7},{7,6},{8,9},{9,8},{10,11... | collective-permute-start | bytes 1572872 | tf_op jit(solution)/shard_map/ppermute | solution.py:165
  40.8 22.1 %collective-permute-start.24 = (bf16[512,512]{1,0:T(8,128)(2,1)S(1)}, bf16[512,512]{1,0:T(8,128)(2,1)S(1)}, u32[]{:S(2)}, u32[]{:S(2)}) collective-permute-start(bf16[512,512]{1,0:T(8,128)(2,1)S(1)} %copy-done.5), channel_id=1, source_target_pairs={{0,2},{2,0},{1,3},{3,1},{4,6},{6,4},{5,7},{7,5},{8,10},{10,8},{9,1... | collective-permute-start | bytes 1572872 | tf_op jit(solution)/shard_map/ppermute | solution.py:165
  43.2 7.4 %collective-permute-start.15 = (bf16[144,256]{1,0:T(8,128)(2,1)S(1)}, bf16[144,256]{1,0:T(8,128)(2,1)S(1)}, u32[]{:S(2)}, u32[]{:S(2)}) collective-permute-start(bf16[144,256]{1,0:T(8,128)(2,1)S(1)} %get-tuple-element.65), channel_id=1, source_target_pairs={{0,4},{4,8},{8,12},{12,0},{1,5},{5,9},{9,13},{13,1},{2,6},{6,10},{... | collective-permute-start | bytes 221192 | tf_op jit(solution)/shard_map/ppermute | solution.py:21
  44.5 8.2 %collective-permute-start.16 = (bf16[144,256]{1,0:T(8,128)(2,1)S(1)}, bf16[144,256]{1,0:T(8,128)(2,1)S(1)}, u32[]{:S(2)}, u32[]{:S(2)}) collective-permute-start(bf16[144,256]{1,0:T(8,128)(2,1)S(1)} %get-tuple-element.66), channel_id=1, source_target_pairs={{0,8},{4,12},{8,0},{12,4},{1,9},{5,13},{9,1},{13,5},{2,10},{6,14},... | collective-permute-start | bytes 221192 | tf_op jit(solution)/shard_map/ppermute | solution.py:21
  46.9 5.8 %collective-permute-start.17 = (bf16[144,256]{1,0:T(8,128)(2,1)S(1)}, bf16[144,256]{1,0:T(8,128)(2,1)S(1)}, u32[]{:S(2)}, u32[]{:S(2)}) collective-permute-start(bf16[144,256]{1,0:T(8,128)(2,1)S(1)} %get-tuple-element.67), channel_id=1, source_target_pairs={{0,12},{4,0},{8,4},{12,8},{1,13},{5,1},{9,5},{13,9},{2,14},{6,2},{... | collective-permute-start | bytes 221192 | tf_op jit(solution)/shard_map/ppermute | solution.py:21
  56.6 6.4 %collective-permute-start.20 = (bf16[256,128]{1,0:T(8,128)(2,1)S(1)}, bf16[256,128]{1,0:T(8,128)(2,1)S(1)}, u32[]{:S(2)}, u32[]{:S(2)}) collective-permute-start(bf16[256,128]{1,0:T(8,128)(2,1)S(1)} %get-tuple-element.80), channel_id=1, source_target_pairs={{0,2},{2,0},{1,3},{3,1},{4,6},{6,4},{5,7},{7,5},{8,10},{10,8},{9,1... | collective-permute-start | bytes 196616 | tf_op jit(solution)/shard_map/ppermute | solution.py:165
  62.9 7.6 %collective-permute-start.25 = (bf16[512,512]{1,0:T(8,128)(2,1)S(1)}, bf16[512,512]{1,0:T(8,128)(2,1)S(1)}, u32[]{:S(2)}, u32[]{:S(2)}) collective-permute-start(bf16[512,512]{1,0:T(8,128)(2,1)S(1)} %collective-permute-done.24.refs_6_), channel_id=1, source_target_pairs={{0,1},{1,0},{2,3},{3,2},{4,5},{5,4},{6,7},{7,6},{8,9},{9,8},{10,11... | collective-permute-start | bytes 1572872 | tf_op jit(solution)/shard_map/ppermute | solution.py:165
  63.0 7.5 %collective-permute-start.21 = (bf16[256,128]{1,0:T(8,128)(2,1)S(1)}, bf16[256,128]{1,0:T(8,128)(2,1)S(1)}, u32[]{:S(2)}, u32[]{:S(2)}) collective-permute-start(bf16[256,128]{1,0:T(8,128)(2,1)S(1)} %pad_maximum_fusion.3), channel_id=1, source_target_pairs={{0,8},{4,12},{8,0},{12,4},{1,9},{5,13},{9,1},{13,5},{2,10},{6,14},... | collective-permute-start | bytes 196616 | tf_op jit(solution)/shard_map/ppermute | solution.py:21
  64.0 6.6 %collective-permute-start.22 = (bf16[256,128]{1,0:T(8,128)(2,1)S(1)}, bf16[256,128]{1,0:T(8,128)(2,1)S(1)}, u32[]{:S(2)}, u32[]{:S(2)}) collective-permute-start(bf16[256,128]{1,0:T(8,128)(2,1)S(1)} %pad_maximum_fusion.4), channel_id=1, source_target_pairs={{0,4},{4,8},{8,12},{12,0},{1,5},{5,9},{9,13},{13,1},{2,6},{6,10},{... | collective-permute-start | bytes 196616 | tf_op jit(solution)/shard_map/ppermute | solution.py:21
  (10 other events, 50.7 us)
